TPU v7x, 32 devices: a whole 2x2x4 slice. The times are simulated.
32 devices in a mesh: shard: 4 (over x, core), context: 2 (over y), tensor: 4 (over z).
Axes of the slice: x: 2, y: 2, z: 4, core: 2. Of those that a mesh axis runs over, the one named last changes fastest.
Arguments:
- tokens: bfloat16 [8, 768, 960], P('shard', ('context', 'tensor')), may hold values from -6 to 6
- attn_gain: float32 [960], P('shard'), may hold values from 0.25 to 1.75
- w_query: bfloat16 [960, 960], P('shard'), may hold values from -0.1875 to 0.1875
- key_weight: bfloat16 [960, 320], P('shard'), may hold values from -0.1875 to 0.1875
- value_weight: bfloat16 [960, 320], P('shard'), may hold values from -0.1875 to 0.1875
- w_output: bfloat16 [960, 960], P(None, 'shard'), may hold values from -1 to 1
- mlp_gain: float32 [960], P('shard'), may hold values from 0.25 to 1.75
- w_gate: bfloat16 [960, 2560], P('shard', 'tensor'), may hold values from -0.1875 to 0.1875
- w_up: bfloat16 [960, 2560], P('shard', 'tensor'), may hold values from -0.1875 to 0.1875
- w_down: bfloat16 [2560, 960], P('tensor', 'shard'), may hold values from -0.25 to 0.25
- cotangent: bfloat16 [8, 768, 960], P('shard', ('context', 'tensor')), may hold values from -6 to 6
Outputs:
- block_out: bfloat16 [8, 768, 960], P('shard', ('context', 'tensor'))
- tokens_grad: bfloat16 [8, 768, 960], P('shard', ('context', 'tensor'))
- attn_gain_grad: float32 [960], P('shard')
- w_query_grad: float32 [960, 960], P('shard')
- w_key_grad: float32 [960, 320], P('shard')
- w_value_grad: float32 [960, 320], P('shard')
- w_output_grad: float32 [960, 960], P(None, 'shard')
- mlp_gain_grad: float32 [960], P('shard')
- w_gate_grad: float32 [960, 2560], P('shard', 'tensor')
- w_up_grad: float32 [960, 2560], P('shard', 'tensor')
- w_down_grad: float32 [2560, 960], P('tensor', 'shard')
All inputs are finite; a program needn't handle non-finite values.
Results may differ from a plain program's by a relative error of at most 0.022.
Values may be sent and summed in bfloat16 or wider, within the bound.
No kernel may reach another device: no remote copies, remote signals or barrier semaphores. Data moves between devices by JAX's collectives and lax.ppermute only.
A program may use at most 128 MiB of HBM per device.

v0:
```python
import functools

import jax
import jax.numpy as jnp
import numpy as np
from jax import lax
from jax.experimental import pallas as pl
from jax.experimental.pallas import tpu as pltpu
from jax.sharding import PartitionSpec as P

QUERY_HEADS = 15
KEY_VALUE_HEADS = 5
HEAD_SIZE = 64
GROUP = QUERY_HEADS // KEY_VALUE_HEADS
SCALE = HEAD_SIZE ** (-0.5)
EPS = 1e-05
KERNEL_VMEM = 40 * 1024 * 1024


def dot(left, right):
    return jnp.dot(left, right, preferred_element_type=jnp.float32)


def dot_rows(left, right):
    return lax.dot_general(
        left, right, (((1,), (1,)), ((), ())), preferred_element_type=jnp.float32
    )


def dot_cols(left, right):
    return lax.dot_general(
        left, right, (((0,), (0,)), ((), ())), preferred_element_type=jnp.float32
    )


def rms_scale(rows):
    return lax.rsqrt(jnp.mean(rows * rows, axis=-1, keepdims=True) + EPS)


def norm_back(scaled, rows, scale_rows):
    normed = rows * scale_rows
    return scale_rows * (scaled - normed * jnp.mean(scaled * normed, axis=-1, keepdims=True))


def after(value, *others):
    return lax.optimization_barrier((value, *others))[0]


def bits_of(count):
    return count.bit_length() - 1


def flip_blocks(rows, shards, index):
    width = rows.shape[-1] // shards
    bits = bits_of(shards)
    for place in range(bits):
        step = width << place
        pieces = [rows[..., i * step : (i + 1) * step] for i in range(rows.shape[-1] // step)]
        swapped = jnp.concatenate([pieces[i ^ 1] for i in range(len(pieces))], -1)
        rows = jnp.where((index >> (bits - 1 - place)) & 1 == 1, swapped, rows)
    return rows


def reverse_blocks(rows, shards):
    width = rows.shape[-1] // shards
    bits = bits_of(shards)
    order = [int(format(i, f"0{bits}b")[::-1], 2) for i in range(shards)]
    return jnp.concatenate([rows[..., i * width : (i + 1) * width] for i in order], -1)


def to_relative(rows, shards, index):
    return flip_blocks(reverse_blocks(rows, shards), shards, index)


def from_relative(rows, shards, index):
    return reverse_blocks(flip_blocks(rows, shards, index), shards)


def swap(value, axis, bit):
    size = lax.axis_size(axis)
    return lax.ppermute(value, axis, [(i, i ^ bit) for i in range(size)])


def gather_pieces(rows, gate, later=None):
    pieces = [rows]
    for place in reversed(range(bits_of(lax.axis_size("shard")))):
        if len(pieces) > 2:
            pieces = [jnp.concatenate(pieces, 0)]
        sent = pieces
        if gate is not None:
            sent = [after(rows, gate)]
            gate = None
        elif later is not None:
            sent = pieces[:1] + [after(piece, later) for piece in pieces[1:]]
        pieces = pieces + [swap(piece, "shard", 1 << place) for piece in sent]
    return pieces


def scatter_rows(rows, first, last):
    for place in range(first, last):
        half = rows.shape[0] // 2
        rows = rows[:half] + swap(rows[half:], "shard", 1 << place)
    return rows


def shift(value, count):
    size = lax.axis_size("tensor")
    return lax.ppermute(value, "tensor", [(i, (i + count) % size) for i in range(size)])


def both_sequences(mine, other, upper):
    return jnp.stack([jnp.where(upper, other, mine), jnp.where(upper, mine, other)])


def chunk_rows(count, group):
    chunk = -(-count // group)
    return chunk if chunk <= 16 else -(-chunk // 16) * 16


def group_halves(rows, context):
    chunk = chunk_rows(rows.shape[0], 2 * lax.axis_size("tensor"))
    half = chunk * lax.axis_size("tensor")
    padded = jnp.pad(rows, ((0, 2 * half - rows.shape[0]), (0, 0)))
    kept = lax.dynamic_slice_in_dim(padded, context * half, half, 0)
    sent = lax.dynamic_slice_in_dim(padded, (1 - context) * half, half, 0)
    return kept + swap(sent, "context", 1)


def group_part(half):
    places = lax.axis_size("tensor")
    parts = lax.all_to_all(half, "tensor", split_axis=0, concat_axis=0, tiled=True)
    parts = parts.reshape(places, half.shape[0] // places, half.shape[1]).astype(jnp.float32)
    return jnp.sum(parts, axis=0).astype(jnp.bfloat16)


def group_collect(part):
    places = lax.axis_size("tensor")
    spread = jnp.broadcast_to(part[None], (places,) + part.shape)
    spread = spread.reshape(places * part.shape[0], part.shape[1])
    return lax.all_to_all(spread, "tensor", split_axis=0, concat_axis=0, tiled=True)


def unpack_kernel(kv_cols, attn_cols, parts_ref, gain_ref, query_ref, key_ref, value_ref, out_ref):
    rows = query_ref.shape[0]
    gain = gain_ref[...]
    query_ref[...] = parts_ref[:rows, 2 * kv_cols : attn_cols].astype(jnp.float32) * gain
    key_ref[...] = (parts_ref[:rows, :kv_cols].astype(jnp.float32) * gain).T
    value_ref[...] = (parts_ref[:rows, kv_cols : 2 * kv_cols].astype(jnp.float32) * gain).T
    first = attn_cols + -attn_cols % 128
    out_ref[...] = parts_ref[:rows, first : first + out_ref.shape[0]].astype(jnp.float32).T


def unpack(parts, gain, kv_cols, attn_cols, out_cols):
    rows = gain.shape[0]
    shapes = ((rows, attn_cols - 2 * kv_cols), (kv_cols, rows), (kv_cols, rows), (out_cols, rows))
    return pl.pallas_call(
        functools.partial(unpack_kernel, kv_cols, attn_cols),
        out_shape=tuple(jax.ShapeDtypeStruct(shape, jnp.float32) for shape in shapes),
        compiler_params=pltpu.CompilerParams(vmem_limit_bytes=KERNEL_VMEM),
        cost_estimate=pl.CostEstimate(flops=0, transcendentals=0, bytes_accessed=4_000_000),
        name="unpack",
    )(parts, gain)


def rope_tables(length):
    half = HEAD_SIZE // 2
    freq = np.float32(10000.0) ** (-np.arange(half).astype(np.float32) * 2.0 / HEAD_SIZE)
    angle = np.arange(length).astype(np.float32)[:, None] * freq.astype(np.float32)[None, :]
    cosine, sine = np.cos(angle), np.sin(angle)
    return np.concatenate([cosine, cosine, -sine, sine], 1).astype(np.float32)


def turn(head, table):
    half = HEAD_SIZE // 2
    swapped = jnp.concatenate([head[:, half:], head[:, :half]], 1)
    return head * table[:, :HEAD_SIZE] + swapped * table[:, HEAD_SIZE:]


def turn_back(head, table):
    half = HEAD_SIZE // 2
    swapped = jnp.concatenate([head[:, half:], head[:, :half]], 1)
    return head * table[:, :HEAD_SIZE] - swapped * table[:, HEAD_SIZE:]


def head_cols(index):
    return slice(index * HEAD_SIZE, (index + 1) * HEAD_SIZE)


def attend_kernel(q_ref, k_ref, v_ref, qt_ref, kt_ref, qp_ref, kp_ref, mix_ref, log_ref, qr_ref, kr_ref):
    hidden = jnp.where(kp_ref[...] <= qp_ref[...], 0.0, -1e30)
    hidden = jnp.concatenate([hidden] * GROUP, 0)
    rows = q_ref.shape[0]
    for g in range(KEY_VALUE_HEADS):
        key = turn(k_ref[:, head_cols(g)], kt_ref[...]).astype(jnp.bfloat16)
        kr_ref[:, head_cols(g)] = key
        value = v_ref[:, head_cols(g)]
        heads = []
        for i in range(GROUP):
            cols = head_cols(g * GROUP + i)
            head = turn(q_ref[:, cols], qt_ref[...]).astype(jnp.bfloat16) * SCALE
            qr_ref[:, cols] = head
            heads.append(head)
        query = jnp.concatenate(heads, 0)
        scores = dot_rows(query, key) + hidden
        peak = jnp.max(scores, axis=-1, keepdims=True)
        expd = jnp.exp(scores - peak)
        total = jnp.sum(expd, axis=-1, keepdims=True)
        mixed = (dot(expd.astype(jnp.bfloat16), value) / total).astype(jnp.bfloat16)
        for i in range(GROUP):
            mix_ref[:, head_cols(g * GROUP + i)] = mixed[i * rows : (i + 1) * rows]
        log_ref[:, g : g + 1] = peak + jnp.log(total)


def attend(query, key, value, query_table, key_table, query_pos, key_pos):
    rows, keys = query.shape[0], key.shape[0]
    return pl.pallas_call(
        attend_kernel,
        out_shape=(
            jax.ShapeDtypeStruct(query.shape, jnp.bfloat16),
            jax.ShapeDtypeStruct((GROUP * rows, 8), jnp.float32),
            jax.ShapeDtypeStruct(query.shape, jnp.bfloat16),
            jax.ShapeDtypeStruct(key.shape, jnp.bfloat16),
        ),
        compiler_params=pltpu.CompilerParams(vmem_limit_bytes=KERNEL_VMEM),
        cost_estimate=pl.CostEstimate(
            flops=4 * rows * keys * QUERY_HEADS * HEAD_SIZE,
            transcendentals=rows * keys * QUERY_HEADS,
            bytes_accessed=4_000_000,
        ),
        name="attend",
    )(query, key, value, query_table, key_table, query_pos, key_pos)


def attend_back_kernel(
    q_ref, k_ref, v_ref, mix_ref, gm_ref, log_ref, qt_ref, kt_ref, qp_ref, kp_ref, grad_ref
):
    hidden = jnp.where(kp_ref[...] <= qp_ref[...], 0.0, -1e30)
    hidden = jnp.concatenate([hidden] * GROUP, 0)
    rows, keys = q_ref.shape[0], k_ref.shape[0]
    kv_cols = 2 * k_ref.shape[1]
    grad_ref[rows:, kv_cols:] = jnp.zeros((keys - rows, grad_ref.shape[1] - kv_cols), jnp.bfloat16)
    used = kv_cols + q_ref.shape[1]
    if used < grad_ref.shape[1]:
        grad_ref[:rows, used:] = jnp.zeros((rows, grad_ref.shape[1] - used), jnp.bfloat16)
    for g in range(KEY_VALUE_HEADS):
        key, value = k_ref[:, head_cols(g)], v_ref[:, head_cols(g)]
        each = [head_cols(g * GROUP + i) for i in range(GROUP)]
        query = jnp.concatenate([q_ref[:, cols] for cols in each], 0)
        mixed = jnp.concatenate([mix_ref[:, cols] for cols in each], 0)
        grad_mix = jnp.concatenate([gm_ref[:, cols] for cols in each], 0)
        scores = dot_rows(query, key) + hidden
        probs = jnp.exp(scores - log_ref[:, g : g + 1])
        grad_probs = dot_rows(grad_mix, value)
        delta = jnp.sum(
            grad_mix.astype(jnp.float32) * mixed.astype(jnp.float32), axis=-1, keepdims=True
        )
        grad_scores = (probs * (grad_probs - delta)).astype(jnp.bfloat16)
        grad_query = dot(grad_scores, key) * SCALE
        grad_key = dot_cols(grad_scores, query)
        grad_value = dot_cols(probs.astype(jnp.bfloat16), grad_mix)
        for i in range(GROUP):
            head = turn_back(grad_query[i * rows : (i + 1) * rows], qt_ref[...])
            grad_ref[:rows, head_cols(2 * KEY_VALUE_HEADS + g * GROUP + i)] = head.astype(jnp.bfloat16)
        grad_ref[:, head_cols(g)] = turn_back(grad_key, kt_ref[...]).astype(jnp.bfloat16)
        grad_ref[:, head_cols(KEY_VALUE_HEADS + g)] = grad_value.astype(jnp.bfloat16)


def attend_back(query, key, value, mix, grad_mix, log_total, query_table, key_table, query_pos, key_pos):
    rows, keys = query.shape[0], key.shape[0]
    used = 2 * key.shape[1] + query.shape[1]
    return pl.pallas_call(
        attend_back_kernel,
        out_shape=jax.ShapeDtypeStruct((keys, used + -used % 128), jnp.bfloat16),
        compiler_params=pltpu.CompilerParams(vmem_limit_bytes=KERNEL_VMEM),
        cost_estimate=pl.CostEstimate(
            flops=10 * rows * keys * QUERY_HEADS * HEAD_SIZE,
            transcendentals=rows * keys * QUERY_HEADS,
            bytes_accessed=6_000_000,
        ),
        name="attend_back",
    )(query, key, value, mix, grad_mix, log_total, query_table, key_table, query_pos, key_pos)


def body(
    tokens,
    attn_gain,
    w_query,
    key_weight,
    value_weight,
    w_output,
    mlp_gain,
    w_gate,
    w_up,
    w_down,
    cotangent,
):
    _, length, width = tokens.shape
    shards, shard = lax.axis_size("shard"), lax.axis_index("shard")
    context, place = lax.axis_index("context"), lax.axis_index("tensor")
    places = lax.axis_size("tensor")
    rows = 2 * length
    upper = place // 2 == 1
    kv_cols, hidden_cols = key_weight.shape[1], w_gate.shape[1]

    starts = [
        (which * places + (place ^ step)) * length
        for which in (context, 1 - context)
        for step in (0, 2, 1, 3)
    ]
    table = jnp.asarray(rope_tables(length * places * lax.axis_size("context")))
    key_table = jnp.concatenate([lax.dynamic_slice_in_dim(table, at, length, 0) for at in starts], 0)
    key_pos = jnp.concatenate([at + jnp.arange(length, dtype=jnp.int32) for at in starts])
    query_table, query_pos = key_table[:rows], key_pos[:rows, None]
    key_pos = key_pos[None, :]

    mine, other = jnp.where(upper, tokens[1], tokens[0]), jnp.where(upper, tokens[0], tokens[1])
    moved = swap(other, "tensor", 2)
    own = jnp.concatenate([to_relative(mine, shards, shard), to_relative(moved, shards, shard)], 0)
    beside = swap(own, "tensor", 1)
    across = swap(own, "context", 1)
    across_beside = swap(after(beside, across), "context", 1)
    all_tokens = jnp.concatenate([own, beside, across, across_beside], 0)

    def gained(weights, gain):
        joined = jnp.concatenate(weights, 1)
        return (joined.astype(jnp.float32) * gain[:, None]).astype(jnp.bfloat16)

    attn_local = jnp.concatenate([key_weight, value_weight, w_query], 1)
    attn_cols = attn_local.shape[1]
    gap = -attn_cols % 128
    gaps = jnp.zeros((attn_local.shape[0], gap), jnp.bfloat16)
    first_local = jnp.concatenate([gained([attn_local], attn_gain), gaps, w_output.T], 1)
    first_pieces = gather_pieces(first_local, None)
    ends = (2 * kv_cols, attn_cols, attn_cols + gap)
    w_kv = jnp.concatenate([piece[:, : ends[0]] for piece in first_pieces], 0)
    w_q = jnp.concatenate([piece[:, ends[0] : ends[1]] for piece in first_pieces], 0)
    out_weight = jnp.concatenate([piece[:, ends[2] :] for piece in first_pieces], 0)
    mlp_local = jnp.concatenate([gained([w_gate, w_up], mlp_gain), w_down.T], 1)

    cots = [after(to_relative(cotangent, shards, shard), beside)]
    cots.append(shift(cots[0], 1))
    cots = [after(cots[0], cots[1]), cots[1], shift(cots[1], 1)]
    cots.append(shift(cots[0], -1))
    all_tokens = after(all_tokens, cots[1])

    all_float = all_tokens.astype(jnp.float32)
    all_scale = rms_scale(all_float)
    all_normed = (all_float * all_scale).astype(jnp.bfloat16)
    tokens_f, scale_a, normed_a = all_float[:rows], all_scale[:rows], all_normed[:rows]
    query = dot(normed_a, w_q)
    key_value = dot(all_normed, w_kv)
    key, value = key_value[:, :kv_cols], key_value[:, kv_cols:].astype(jnp.bfloat16)
    mix, log_total, query_rot, key_rot = attend(
        query, key, value, query_table, key_table, query_pos, key_pos
    )
    mlp_pieces = gather_pieces(mlp_local, w_kv, mix)
    w_in = jnp.concatenate([piece[:, : 2 * hidden_cols] for piece in mlp_pieces], 0)
    w_dn = jnp.concatenate([piece[:, 2 * hidden_cols :] for piece in mlp_pieces], 0)
    hidden = tokens_f + dot_rows(mix, out_weight)
    scale_m = rms_scale(hidden)
    normed_m = (hidden * scale_m).astype(jnp.bfloat16)

    normed_m, cots[2], cots[3] = lax.optimization_barrier((normed_m, cots[2], cots[3]))

    def cot_of(k):
        above = ((place - k) % places) // 2 == 1
        pair = (cots[k], cots[(k + 2) % places])
        return jnp.concatenate([jnp.where(above, one[1], one[0]) for one in pair], 0)

    cots = [cot_of(k) for k in range(places)]
    own_cot = cots[0]
    barrier = lax.optimization_barrier

    group, acts, grads_in, backs = [normed_m], [], [], []
    arriving = shift(normed_m, 1)
    for k, cot in enumerate(cots):
        if k > 0:
            group.append(arriving if k < 3 else after(arriving, grad_nm))
            if k + 1 < places:
                arriving = shift(arriving if k == 1 else after(arriving, backs[-1]), 1)
        rows_in = group[k]
        grad_act = dot(cot, w_dn)
        inner = dot(rows_in, w_in)
        gate, up_vals = inner[:, :hidden_cols], inner[:, hidden_cols:]
        sigma = jax.nn.sigmoid(gate)
        acts.append((gate * sigma * up_vals).astype(jnp.bfloat16))
        grad_up = (grad_act * gate * sigma).astype(jnp.bfloat16)
        grad_gate = (grad_act * up_vals * sigma * (1.0 + gate * (1.0 - sigma))).astype(jnp.bfloat16)
        grads_in.append(jnp.concatenate([grad_gate, grad_up], 1))
        backs.append(dot_rows(grads_in[-1], w_in).astype(jnp.bfloat16))
        if k > 0:
            grad_nm = backs[k] if k == 1 else backs[k] + shift(grad_nm, 1)
    bits = bits_of(shards)
    *held, _ = barrier((*grads_in, *acts, grad_nm))
    group, cot_group = jnp.concatenate(group, 0), jnp.concatenate(cots, 0)
    grad_in, act = jnp.concatenate(held[:places], 0), jnp.concatenate(held[places:], 0)
    mlp_term = jnp.concatenate(
        [dot_cols(group, grad_in).astype(jnp.bfloat16), dot_cols(cot_group, act).astype(jnp.bfloat16)], 1
    )
    mlp_term = scatter_rows(mlp_term, 0, 1)
    half_cols = mlp_term.shape[1] // 2
    first, second = mlp_term[:, :half_cols], mlp_term[:, half_cols:]
    later = context == 1
    mlp_kept, mlp_sent = jnp.where(later, second, first), jnp.where(later, first, second)

    grad_nm = (backs[0] + shift(grad_nm, 1)).astype(jnp.float32)
    grad_hidden = own_cot.astype(jnp.float32) + norm_back(grad_nm, hidden, scale_m)
    gain_m_term = jnp.sum(grad_nm * (hidden * scale_m), axis=0)
    grad_hidden_low = grad_hidden.astype(jnp.bfloat16)
    grad_mix = dot(grad_hidden_low, out_weight).astype(jnp.bfloat16)
    out_term = scatter_rows(dot_cols(grad_hidden_low, mix).astype(jnp.bfloat16), 0, bits)
    forward = [dot_rows(act, w_dn).astype(jnp.bfloat16) for act in acts]
    total = shift(after(forward[1], grad_mix), 1)
    grad_mix, mlp_kept, mlp_sent = barrier((grad_mix, mlp_kept, mlp_sent))
    owned = mlp_sent.shape[0] // 2 if bits > 1 else 0
    mlp_early = swap(mlp_sent[owned:], "context", 1)

    grads = attend_back(
        query_rot, key_rot, value, mix, grad_mix, log_total, query_table, key_table, query_pos, key_pos
    )
    grads, out_term, total, mlp_early = barrier((grads, out_term, total, mlp_early))

    spot = (jnp.arange(grads.shape[1]) == attn_cols).astype(jnp.float32)
    attn_term = dot_cols(all_normed, grads) + gain_m_term[:, None] * spot[None, :]
    attn_term = scatter_rows(attn_term.astype(jnp.bfloat16), 0, 1)
    mlp_late = swap(after(mlp_sent[:owned], attn_term), "context", 1)
    attn_term = scatter_rows(attn_term, 1, bits)
    grad_query, grad_kv = grads[:rows, 2 * kv_cols : attn_cols], grads[:, : 2 * kv_cols]
    pair = grad_kv[: 2 * rows] + swap(grad_kv[2 * rows :], "context", 1)
    own_kv = pair[:rows] + swap(pair[rows:], "tensor", 1)
    out_part = group_part(group_halves(out_term, context))
    total = shift(forward[2] + total, 1)
    total = shift(forward[3] + total, 1)
    attn_term, own_kv, out_part, total = barrier((attn_term, own_kv, out_part, total))

    attn_half = group_halves(attn_term, context)
    mlp_half = scatter_rows(mlp_kept + jnp.concatenate([mlp_late, mlp_early], 0), 1, bits)
    attn_part = group_part(attn_half)
    own_kv, grad_query, mlp_half = barrier((own_kv, grad_query, mlp_half))
    block = hidden + forward[0].astype(jnp.float32) + total.astype(jnp.float32)
    block = from_relative(block.astype(jnp.bfloat16), shards, shard)
    grad_na = dot_rows(grad_query, w_q) + dot_rows(own_kv, w_kv)
    grad_tokens = grad_hidden + norm_back(grad_na, tokens_f, scale_a)
    grad_tokens = from_relative(grad_tokens.astype(jnp.bfloat16), shards, shard)
    block_back = swap(block[length:], "tensor", 2)
    attn_part, mlp_half, grad_tokens, block_back = barrier((attn_part, mlp_half, grad_tokens, block_back))

    fill = jnp.zeros((out_part.shape[0], -out_part.shape[1] % 128), jnp.bfloat16)
    parts = group_collect(jnp.concatenate([attn_part, out_part, fill], 1))
    parts_across = swap(parts, "context", 1)
    parts = jnp.concatenate(
        [jnp.where(later, parts_across, parts), jnp.where(later, parts, parts_across)], 0
    )
    mlp_other = swap(mlp_half, "context", 1)
    mlp_total = jnp.concatenate(
        [jnp.where(later, mlp_other, mlp_half), jnp.where(later, mlp_half, mlp_other)], 1
    ).astype(jnp.float32)
    gate_total = mlp_total[:, :hidden_cols] * mlp_gain[:, None]
    up_total = mlp_total[:, hidden_cols : 2 * hidden_cols] * mlp_gain[:, None]
    down_total = mlp_total[:, 2 * hidden_cols :].T
    tokens_back = swap(grad_tokens[length:], "tensor", 2)
    gate_total, block, grad_tokens = barrier((gate_total, block[:length], grad_tokens[:length]))
    block_out = both_sequences(block, block_back, upper)
    tokens_grad = both_sequences(grad_tokens, tokens_back, upper)
    query_total, key_total, value_total, out_total = unpack(
        parts, attn_gain[:, None], kv_cols, attn_cols, out_part.shape[1]
    )
    heads = parts[: attn_local.shape[0], : attn_cols + 1].astype(jnp.float32)
    gain_m_total = heads[:, attn_cols] / mlp_gain
    gain_a_total = jnp.sum(attn_local.astype(jnp.float32) * heads[:, :attn_cols], axis=1)
    return (
        block_out,
        tokens_grad,
        gain_a_total,
        query_total,
        key_total.T,
        value_total.T,
        out_total,
        gain_m_total,
        gate_total,
        up_total,
        down_total,
    )


def solution(mesh):
    specs = (
        P("shard", ("context", "tensor"), None),
        P("shard"),
        P("shard", None),
        P("shard", None),
        P("shard", None),
        P(None, "shard"),
        P("shard"),
        P("shard", "tensor"),
        P("shard", "tensor"),
        P("tensor", "shard"),
    )
    return jax.shard_map(
        body,
        mesh=mesh,
        in_specs=specs + specs[:1],
        out_specs=specs[:1] + specs,
        check_vma=False,
    )
```

profile of v0, /device:TPU:0, one launch (start us, length us, event | category | flops | bytes accessed | tf_op | source)
XLA Modules:
  0.0 304.0 jit_solution(2997273711144789106)
XLA Ops:
  27.6 8.6 %collective-permute-done.1 = bf16[192,960]{1,0:T(8,128)(2,1)} collective-permute-done((bf16[192,960]{1,0:T(8,128)(2,1)S(1)}, bf16[192,960]{1,0:T(8,128)(2,1)}, u32[]{:S(2)}, u32[]{:S(2)}) %collective-permute-start.1) | collective-permute-done | bytes 368672 | tf_op jit(solution)/shard_map/ppermute | solution.py:81
  41.4 7.7 %collective-permute-done.4 = bf16[2,96,960]{2,1,0:T(8,128)(2,1)} collective-permute-done((bf16[2,96,960]{2,1,0:T(8,128)(2,1)}, bf16[2,96,960]{2,1,0:T(8,128)(2,1)}, u32[]{:S(2)}, u32[]{:S(2)}) %collective-permute-start.4) | collective-permute-done | bytes 368672 | tf_op jit(solution)/shard_map/ppermute | solution.py:108
  65.0 9.7 %attend.1 = (bf16[192,960]{1,0:T(8,128)(2,1)S(1)}, f32[576,8]{1,0:T(8,128)S(1)}, bf16[192,960]{1,0:T(8,128)(2,1)S(1)}, bf16[768,320]{1,0:T(8,128)(2,1)S(1)}) custom-call(f32[192,960]{1,0:T(8,128)S(1)} %fusion.38.q_ref, f32[768,320]{1,0:T(8,128)S(1)} %slice.478.k_ref, bf16[768,320]{1,0:T(8,128)(2,1)S(1)} %slice.626.v_ref, ...), custom_call_target="tpu_custom_call" | custom-call | flops 566231040 | bytes 4000000 | tf_op jit(solution)/shard_map/attend/pallas_call | solution.py:216
  77.5 9.0 %collective-permute-done.10 = bf16[240,1920]{1,0:T(8,128)(2,1)S(1)} collective-permute-done((bf16[240,1920]{1,0:T(8,128)(2,1)}, bf16[240,1920]{1,0:T(8,128)(2,1)S(1)}, u32[]{:S(2)}, u32[]{:S(2)}) %collective-permute-start.10) | collective-permute-done | bytes 921632 | tf_op jit(solution)/shard_map/ppermute | solution.py:81
  94.1 9.3 %collective-permute-done.14 = bf16[192,960]{1,0:T(8,128)(2,1)S(1)} collective-permute-done((bf16[192,960]{1,0:T(8,128)(2,1)S(1)}, bf16[192,960]{1,0:T(8,128)(2,1)S(1)}, u32[]{:S(2)}, u32[]{:S(2)}) %collective-permute-start.14) | collective-permute-done | bytes 368672 | tf_op jit(solution)/shard_map/ppermute | solution.py:108
  105.4 6.4 %collective-permute-done.16 = bf16[192,960]{1,0:T(8,128)(2,1)S(1)} collective-permute-done((bf16[192,960]{1,0:T(8,128)(2,1)S(1)}, bf16[192,960]{1,0:T(8,128)(2,1)S(1)}, u32[]{:S(2)}, u32[]{:S(2)}) %collective-permute-start.16) | collective-permute-done | bytes 368672 | tf_op jit(solution)/shard_map/ppermute | solution.py:108
  112.8 7.4 %collective-permute-done.15 = bf16[192,960]{1,0:T(8,128)(2,1)S(1)} collective-permute-done((bf16[192,960]{1,0:T(8,128)(2,1)S(1)}, bf16[192,960]{1,0:T(8,128)(2,1)S(1)}, u32[]{:S(2)}, u32[]{:S(2)}) %collective-permute-start.15) | collective-permute-done | bytes 368672 | tf_op jit(solution)/shard_map/ppermute | solution.py:108
  121.6 5.9 %collective-permute-done.17 = bf16[192,960]{1,0:T(8,128)(2,1)S(1)} collective-permute-done((bf16[192,960]{1,0:T(8,128)(2,1)S(1)}, bf16[192,960]{1,0:T(8,128)(2,1)S(1)}, u32[]{:S(2)}, u32[]{:S(2)}) %collective-permute-start.17) | collective-permute-done | bytes 368672 | tf_op jit(solution)/shard_map/ppermute | solution.py:108
  133.7 6.5 %collective-permute-done.18 = bf16[192,960]{1,0:T(8,128)(2,1)S(1)} collective-permute-done((bf16[192,960]{1,0:T(8,128)(2,1)S(1)}, bf16[192,960]{1,0:T(8,128)(2,1)S(1)}, u32[]{:S(2)}, u32[]{:S(2)}) %collective-permute-start.18) | collective-permute-done | bytes 368672 | tf_op jit(solution)/shard_map/ppermute | solution.py:108
  156.2 6.6 %collective-permute-done.21 = bf16[240,960]{1,0:T(8,128)(2,1)S(1)} collective-permute-done((bf16[240,960]{1,0:T(8,128)(2,1)S(1)}, bf16[240,960]{1,0:T(8,128)(2,1)S(1)}, u32[]{:S(2)}, u32[]{:S(2)}) %collective-permute-start.21) | collective-permute-done | bytes 460832 | tf_op jit(solution)/shard_map/ppermute | solution.py:81
  163.6 10.1 %attend_back.1 = bf16[768,1664]{1,0:T(8,128)(2,1)S(1)} custom-call(bf16[192,960]{1,0:T(8,128)(2,1)S(1)} %copy-done.5, bf16[768,320]{1,0:T(8,128)(2,1)S(1)} %copy-done.1, bf16[768,320]{1,0:T(8,128)(2,1)S(1)} %slice.626.v_ref, bf16[192,960]{1,0:T(8,128)(2,1)S(1)} %get-tuple-element.66.mix_ref, bf16[192,960]{1,0:T(8,128)(2,1)S(1)} %convolution_convert_fusion.7.gm_ref, ...), custom_call_target="tpu_custom_call" | custom-call | flops 1415577600 | bytes 6000000 | tf_op jit(solution)/shard_map/attend_back/pallas_call | solution.py:271
  173.7 3.2 %add_convert_fusion = bf16[960,1664]{1,0:T(8,128)(2,1)S(1)} fusion(bf16[768,960]{1,0:T(8,128)(2,1)S(1)} %copy-done.37, bf16[768,1664]{1,0:T(8,128)(2,1)S(1)} %attend_back.1, f32[1664]{0:T(1024)S(1)} %fusion.58, f32[960]{0:T(1024)S(1)} %copy-done.87), kind=kOutput, calls=%fused_computation | convolution fusion | flops 2458460160 | bytes 7235840 | tf_op jit(solution)/shard_map/dot_general | solution.py:31
  185.1 5.7 %collective-permute-done.28 = bf16[128,960]{1,0:T(8,128)(2,1)S(1)} collective-permute-done((bf16[128,960]{1,0:T(8,128)(2,1)S(1)}, bf16[128,960]{1,0:T(8,128)(2,1)S(1)}, u32[]{:S(2)}, u32[]{:S(2)}) %collective-permute-start.28) | collective-permute-done | bytes 245792 | tf_op jit(solution)/shard_map/ppermute | solution.py:81
  191.6 3.4 %all-to-all-start = ((bf16[4,32,960]{2,1,0:T(8,128)(2,1)}), bf16[4,32,960]{2,1,0:T(8,128)(2,1)S(1)}, u32[]{:S(2)}, u32[]{:S(2)}) async-start(bf16[4,32,960]{2,1,0:T(8,128)(2,1)} %bitcast.13), calls=%async_computation | async-start | bytes 524288 | tf_op jit(solution)/shard_map/all_to_all | solution.py:131
  209.9 5.5 %collective-permute-done.32 = bf16[240,960]{1,0:T(8,128)(2,1)S(1)} collective-permute-done((bf16[240,960]{1,0:T(8,128)(2,1)}, bf16[240,960]{1,0:T(8,128)(2,1)S(1)}, u32[]{:S(2)}, u32[]{:S(2)}) %collective-permute-start.32) | collective-permute-done | bytes 460832 | tf_op jit(solution)/shard_map/ppermute | solution.py:81
  218.8 3.8 %collective-permute-start.31 = (bf16[128,1664]{1,0:T(8,128)(2,1)S(1)}, bf16[128,1664]{1,0:T(8,128)(2,1)S(1)}, u32[]{:S(2)}, u32[]{:S(2)}) collective-permute-start(bf16[128,1664]{1,0:T(8,128)(2,1)S(1)} %pad_dynamic-slice_fusion), channel_id=1, source_target_pairs={{0,4},{4,0},{1,5},{5,1},{2,6},{6,2},{3,7},{7,3},{8,12},{12,8},{9,1... | collective-permute-start | bytes 1277960 | tf_op jit(solution)/shard_map/ppermute | solution.py:81
  224.5 3.5 %collective-permute-done.33 = bf16[240,960]{1,0:T(8,128)(2,1)S(1)} collective-permute-done((bf16[240,960]{1,0:T(8,128)(2,1)S(1)}, bf16[240,960]{1,0:T(8,128)(2,1)S(1)}, u32[]{:S(2)}, u32[]{:S(2)}) %collective-permute-start.33) | collective-permute-done | bytes 460832 | tf_op jit(solution)/shard_map/ppermute | solution.py:81
  232.4 4.6 %all-to-all-start.1 = ((bf16[4,32,1664]{2,1,0:T(8,128)(2,1)}), bf16[4,32,1664]{2,1,0:T(8,128)(2,1)S(1)}, u32[]{:S(2)}, u32[]{:S(2)}) async-start(bf16[4,32,1664]{2,1,0:T(8,128)(2,1)} %bitcast.14), calls=%async_computation.1 | async-start | bytes 851968 | tf_op jit(solution)/shard_map/all_to_all | solution.py:131
  237.0 3.0 collective-permute-start.34
  240.6 13.4 %all-to-all-done.1 = bf16[4,32,1664]{2,1,0:T(8,128)(2,1)S(1)} async-done(((bf16[4,32,1664]{2,1,0:T(8,128)(2,1)}), bf16[4,32,1664]{2,1,0:T(8,128)(2,1)S(1)}, u32[]{:S(2)}, u32[]{:S(2)}) %all-to-all-start.1) | async-done | bytes 426016 | tf_op jit(solution)/shard_map/all_to_all | solution.py:131
  258.9 3.5 %all-to-all-start.2 = ((bf16[4,32,2688]{2,1,0:T(8,128)(2,1)}), bf16[4,32,2688]{2,1,0:T(8,128)(2,1)S(1)}, u32[]{:S(2)}, u32[]{:S(2)}) async-start(bf16[4,32,2688]{2,1,0:T(8,128)(2,1)} %broadcast_in_dim.16), calls=%async_computation.2 | async-start | bytes 1376256 | tf_op jit(solution)/shard_map/all_to_all | solution.py:140
  262.4 2.9 collective-permute-start.36
  269.0 15.2 %all-to-all-done.2 = bf16[4,32,2688]{2,1,0:T(8,128)(2,1)S(1)} async-done(((bf16[4,32,2688]{2,1,0:T(8,128)(2,1)}), bf16[4,32,2688]{2,1,0:T(8,128)(2,1)S(1)}, u32[]{:S(2)}, u32[]{:S(2)}) %all-to-all-start.2) | async-done | bytes 688160 | tf_op jit(solution)/shard_map/all_to_all | solution.py:140
  288.7 10.3 %collective-permute-done.37 = bf16[128,2688]{1,0:T(8,128)(2,1)S(1)} collective-permute-done((bf16[128,2688]{1,0:T(8,128)(2,1)S(1)}, bf16[128,2688]{1,0:T(8,128)(2,1)S(1)}, u32[]{:S(2)}, u32[]{:S(2)}) %collective-permute-start.37) | collective-permute-done | bytes 688160 | tf_op jit(solution)/shard_map/ppermute | solution.py:81
  (443 shorter events, 135.9 us)
Async XLA Ops:
  6.6 50.8 %collective-permute-start.6 = (bf16[240,2624]{1,0:T(8,128)(2,1)}, bf16[240,2624]{1,0:T(8,128)(2,1)}, u32[]{:S(2)}, u32[]{:S(2)}) collective-permute-start(bf16[240,2624]{1,0:T(8,128)(2,1)} %concatenate.155), channel_id=1, source_target_pairs={{0,8},{8,0},{16,24},{24,16},{1,9},{9,1},{17,25},{25,17},{2,10},{10... | collective-permute-start | bytes 3778568 | tf_op jit(solution)/shard_map/ppermute | solution.py:81
  7.1 47.7 %collective-permute-start.5 = (bf16[240,2624]{1,0:T(8,128)(2,1)}, bf16[240,2624]{1,0:T(8,128)(2,1)}, u32[]{:S(2)}, u32[]{:S(2)}) collective-permute-start(bf16[240,2624]{1,0:T(8,128)(2,1)} %concatenate.155), channel_id=1, source_target_pairs={{0,16},{8,24},{16,0},{24,8},{1,17},{9,25},{17,1},{25,9},{2,18},{10... | collective-permute-start | bytes 3778568 | tf_op jit(solution)/shard_map/ppermute | solution.py:81
  14.9 36.4 %collective-permute-start.11 = (bf16[240,1920]{1,0:T(8,128)(2,1)}, bf16[240,1920]{1,0:T(8,128)(2,1)}, u32[]{:S(2)}, u32[]{:S(2)}) collective-permute-start(bf16[240,1920]{1,0:T(8,128)(2,1)} %pad_maximum_fusion.7), channel_id=1, source_target_pairs={{0,8},{8,0},{16,24},{24,16},{1,9},{9,1},{17,25},{25,17},{2,10},{10... | collective-permute-start | bytes 2764808 | tf_op jit(solution)/shard_map/ppermute | solution.py:81
  49.1 27.1 %collective-permute-start.9 = (bf16[2,96,960]{2,1,0:T(8,128)(2,1)}, bf16[2,96,960]{2,1,0:T(8,128)(2,1)S(1)}, u32[]{:S(2)}, u32[]{:S(2)}) collective-permute-start(bf16[2,96,960]{2,1,0:T(8,128)(2,1)} %maximum_select_fusion.1), channel_id=1, source_target_pairs={{0,3},{1,0},{2,1},{3,2},{4,7},{5,4},{6,5},{7,6},{8,11},{9,8},{10,9... | collective-permute-start | bytes 1105928 | tf_op jit(solution)/shard_map/ppermute | solution.py:108
  53.8 22.4 %collective-permute-start.8 = (bf16[2,96,960]{2,1,0:T(8,128)(2,1)}, bf16[2,96,960]{2,1,0:T(8,128)(2,1)S(1)}, u32[]{:S(2)}, u32[]{:S(2)}) collective-permute-start(bf16[2,96,960]{2,1,0:T(8,128)(2,1)} %collective-permute-done.4), channel_id=1, source_target_pairs={{0,1},{1,2},{2,3},{3,0},{4,5},{5,6},{6,7},{7,4},{8,9},{9,10},{10,1... | collective-permute-start | bytes 1105928 | tf_op jit(solution)/shard_map/ppermute | solution.py:108
  63.4 23.1 %collective-permute-start.10 = (bf16[240,1920]{1,0:T(8,128)(2,1)}, bf16[240,1920]{1,0:T(8,128)(2,1)S(1)}, u32[]{:S(2)}, u32[]{:S(2)}) collective-permute-start(bf16[240,1920]{1,0:T(8,128)(2,1)} %pad_maximum_fusion.7), channel_id=1, source_target_pairs={{0,16},{8,24},{16,0},{24,8},{1,17},{9,25},{17,1},{25,9},{2,18},{10... | collective-permute-start | bytes 2764808 | tf_op jit(solution)/shard_map/ppermute | solution.py:81
  89.6 13.8 %collective-permute-start.14 = (bf16[192,960]{1,0:T(8,128)(2,1)S(1)}, bf16[192,960]{1,0:T(8,128)(2,1)S(1)}, u32[]{:S(2)}, u32[]{:S(2)}) collective-permute-start(bf16[192,960]{1,0:T(8,128)(2,1)S(1)} %collective-permute-done.13), channel_id=1, source_target_pairs={{0,1},{1,2},{2,3},{3,0},{4,5},{5,6},{6,7},{7,4},{8,9},{9,10},{10,1... | collective-permute-start | bytes 1105928 | tf_op jit(solution)/shard_map/ppermute | solution.py:108
  92.7 19.1 %collective-permute-start.16 = (bf16[192,960]{1,0:T(8,128)(2,1)S(1)}, bf16[192,960]{1,0:T(8,128)(2,1)S(1)}, u32[]{:S(2)}, u32[]{:S(2)}) collective-permute-start(bf16[192,960]{1,0:T(8,128)(2,1)S(1)} %convolution_convert_fusion.10), channel_id=1, source_target_pairs={{0,1},{1,2},{2,3},{3,0},{4,5},{5,6},{6,7},{7,4},{8,9},{9,10},{10,1... | collective-permute-start | bytes 1105928 | tf_op jit(solution)/shard_map/ppermute | solution.py:108
  103.4 16.9 %collective-permute-start.15 = (bf16[192,960]{1,0:T(8,128)(2,1)S(1)}, bf16[192,960]{1,0:T(8,128)(2,1)S(1)}, u32[]{:S(2)}, u32[]{:S(2)}) collective-permute-start(bf16[192,960]{1,0:T(8,128)(2,1)S(1)} %collective-permute-done.14), channel_id=1, source_target_pairs={{0,1},{1,2},{2,3},{3,0},{4,5},{5,6},{6,7},{7,4},{8,9},{9,10},{10,1... | collective-permute-start | bytes 1105928 | tf_op jit(solution)/shard_map/ppermute | solution.py:108
  112.7 14.7 %collective-permute-start.17 = (bf16[192,960]{1,0:T(8,128)(2,1)S(1)}, bf16[192,960]{1,0:T(8,128)(2,1)S(1)}, u32[]{:S(2)}, u32[]{:S(2)}) collective-permute-start(bf16[192,960]{1,0:T(8,128)(2,1)S(1)} %fusion.26), channel_id=1, source_target_pairs={{0,1},{1,2},{2,3},{3,0},{4,5},{5,6},{6,7},{7,4},{8,9},{9,10},{10,1... | collective-permute-start | bytes 1105928 | tf_op jit(solution)/shard_map/ppermute | solution.py:108
  133.7 16.0 %collective-permute-start.19 = (bf16[480,1920]{1,0:T(8,128)(2,1)}, bf16[480,1920]{1,0:T(8,128)(2,1)}, u32[]{:S(2)}, u32[]{:S(2)}) collective-permute-start(bf16[480,1920]{1,0:T(8,128)(2,1)} %pad_maximum_fusion.3), channel_id=1, source_target_pairs={{0,8},{8,0},{16,24},{24,16},{1,9},{9,1},{17,25},{25,17},{2,10},{10... | collective-permute-start | bytes 5529608 | tf_op jit(solution)/shard_map/ppermute | solution.py:81
  149.3 13.4 %collective-permute-start.21 = (bf16[240,960]{1,0:T(8,128)(2,1)S(1)}, bf16[240,960]{1,0:T(8,128)(2,1)S(1)}, u32[]{:S(2)}, u32[]{:S(2)}) collective-permute-start(bf16[240,960]{1,0:T(8,128)(2,1)S(1)} %slice.507), channel_id=1, source_target_pairs={{0,16},{8,24},{16,0},{24,8},{1,17},{9,25},{17,1},{25,9},{2,18},{10... | collective-permute-start | bytes 1382408 | tf_op jit(solution)/shard_map/ppermute | solution.py:81
  153.8 19.9 %collective-permute-start.23 = (bf16[240,960]{1,0:T(8,128)(2,1)S(1)}, bf16[240,960]{1,0:T(8,128)(2,1)S(1)}, u32[]{:S(2)}, u32[]{:S(2)}) collective-permute-start(bf16[240,960]{1,0:T(8,128)(2,1)S(1)} %get-tuple-element.157), channel_id=1, source_target_pairs={{0,4},{4,0},{1,5},{5,1},{2,6},{6,2},{3,7},{7,3},{8,12},{12,8},{9,1... | collective-permute-start | bytes 1382408 | tf_op jit(solution)/shard_map/ppermute | solution.py:81
  155.9 17.7 %collective-permute-start.22 = (bf16[192,960]{1,0:T(8,128)(2,1)S(1)}, bf16[192,960]{1,0:T(8,128)(2,1)S(1)}, u32[]{:S(2)}, u32[]{:S(2)}) collective-permute-start(bf16[192,960]{1,0:T(8,128)(2,1)S(1)} %convolution_convert_fusion.6), channel_id=1, source_target_pairs={{0,1},{1,2},{2,3},{3,0},{4,5},{5,6},{6,7},{7,4},{8,9},{9,10},{10,1... | collective-permute-start | bytes 1105928 | tf_op jit(solution)/shard_map/ppermute | solution.py:108
  180.0 15.1 %collective-permute-start.24 = (bf16[480,1664]{1,0:T(8,128)(2,1)}, bf16[480,1664]{1,0:T(8,128)(2,1)}, u32[]{:S(2)}, u32[]{:S(2)}) collective-permute-start(bf16[480,1664]{1,0:T(8,128)(2,1)} %slice.509), channel_id=1, source_target_pairs={{0,8},{8,0},{16,24},{24,16},{1,9},{9,1},{17,25},{25,17},{2,10},{10... | collective-permute-start | bytes 4792328 | tf_op jit(solution)/shard_map/ppermute | solution.py:81
  184.5 19.2 %collective-permute-start.29 = (bf16[192,960]{1,0:T(8,128)(2,1)}, bf16[192,960]{1,0:T(8,128)(2,1)}, u32[]{:S(2)}, u32[]{:S(2)}) collective-permute-start(bf16[192,960]{1,0:T(8,128)(2,1)} %fusion.23), channel_id=1, source_target_pairs={{0,1},{1,2},{2,3},{3,0},{4,5},{5,6},{6,7},{7,4},{8,9},{9,10},{10,1... | collective-permute-start | bytes 1105928 | tf_op jit(solution)/shard_map/ppermute | solution.py:108
  184.5 16.5 %collective-permute-start.26 = (bf16[384,640]{1,0:T(8,128)(2,1)}, bf16[384,640]{1,0:T(8,128)(2,1)}, u32[]{:S(2)}, u32[]{:S(2)}) collective-permute-start(bf16[384,640]{1,0:T(8,128)(2,1)} %slice.417), channel_id=1, source_target_pairs={{0,4},{4,0},{1,5},{5,1},{2,6},{6,2},{3,7},{7,3},{8,12},{12,8},{9,1... | collective-permute-start | bytes 1474568 | tf_op jit(solution)/shard_map/ppermute | solution.py:81
  191.6 16.5 %all-to-all-start = ((bf16[4,32,960]{2,1,0:T(8,128)(2,1)}), bf16[4,32,960]{2,1,0:T(8,128)(2,1)S(1)}, u32[]{:S(2)}, u32[]{:S(2)}) async-start(bf16[4,32,960]{2,1,0:T(8,128)(2,1)} %bitcast.13), calls=%async_computation | async-start | bytes 524288 | tf_op jit(solution)/shard_map/all_to_all | solution.py:131
  198.1 19.3 %collective-permute-start.25 = (bf16[240,1664]{1,0:T(8,128)(2,1)}, bf16[240,1664]{1,0:T(8,128)(2,1)}, u32[]{:S(2)}, u32[]{:S(2)}) collective-permute-start(bf16[240,1664]{1,0:T(8,128)(2,1)} %slice.511), channel_id=1, source_target_pairs={{0,16},{8,24},{16,0},{24,8},{1,17},{9,25},{17,1},{25,9},{2,18},{10... | collective-permute-start | bytes 2396168 | tf_op jit(solution)/shard_map/ppermute | solution.py:81
  232.4 21.6 %all-to-all-start.1 = ((bf16[4,32,1664]{2,1,0:T(8,128)(2,1)}), bf16[4,32,1664]{2,1,0:T(8,128)(2,1)S(1)}, u32[]{:S(2)}, u32[]{:S(2)}) async-start(bf16[4,32,1664]{2,1,0:T(8,128)(2,1)} %bitcast.14), calls=%async_computation.1 | async-start | bytes 851968 | tf_op jit(solution)/shard_map/all_to_all | solution.py:131
  237.0 19.0 %collective-permute-start.34 = (bf16[96,960]{1,0:T(8,128)(2,1)S(1)}, bf16[96,960]{1,0:T(8,128)(2,1)S(1)}, u32[]{:S(2)}, u32[]{:S(2)}) collective-permute-start(bf16[96,960]{1,0:T(8,128)(2,1)S(1)} %get-tuple-element.169), channel_id=1, source_target_pairs={{0,2},{1,3},{2,0},{3,1},{4,6},{5,7},{6,4},{7,5},{8,10},{9,11},{10,... | collective-permute-start | bytes 552968 | tf_op jit(solution)/shard_map/ppermute | solution.py:81
  258.9 25.3 %all-to-all-start.2 = ((bf16[4,32,2688]{2,1,0:T(8,128)(2,1)}), bf16[4,32,2688]{2,1,0:T(8,128)(2,1)S(1)}, u32[]{:S(2)}, u32[]{:S(2)}) async-start(bf16[4,32,2688]{2,1,0:T(8,128)(2,1)} %broadcast_in_dim.16), calls=%async_computation.2 | async-start | bytes 1376256 | tf_op jit(solution)/shard_map/all_to_all | solution.py:140
  262.4 24.7 %collective-permute-start.36 = (bf16[96,960]{1,0:T(8,128)(2,1)S(1)}, bf16[96,960]{1,0:T(8,128)(2,1)S(1)}, u32[]{:S(2)}, u32[]{:S(2)}) collective-permute-start(bf16[96,960]{1,0:T(8,128)(2,1)S(1)} %get-tuple-element.164), channel_id=1, source_target_pairs={{0,2},{1,3},{2,0},{3,1},{4,6},{5,7},{6,4},{7,5},{8,10},{9,11},{10,... | collective-permute-start | bytes 552968 | tf_op jit(solution)/shard_map/ppermute | solution.py:81
  284.2 14.8 %collective-permute-start.37 = (bf16[128,2688]{1,0:T(8,128)(2,1)S(1)}, bf16[128,2688]{1,0:T(8,128)(2,1)S(1)}, u32[]{:S(2)}, u32[]{:S(2)}) collective-permute-start(bf16[128,2688]{1,0:T(8,128)(2,1)S(1)} %bitcast.75), channel_id=1, source_target_pairs={{0,4},{4,0},{1,5},{5,1},{2,6},{6,2},{3,7},{7,3},{8,12},{12,8},{9,1... | collective-permute-start | bytes 2064392 | tf_op jit(solution)/shard_map/ppermute | solution.py:81
  (123 other events, 1216.3 us)
where the time goes:
time: 309 us; the launch traced here: 304 us
  waiting for transfers between devices  135 us (44%)
  starting transfers between devices  45.2 us (15%)
  local copies, waits for them, and re-layouts  34.8 us (11%)
  other arithmetic  33.8 us (11%)
  matrix products  30.1 us (10%)
  Pallas kernels  21.4 us (7%)
    ppermute x26, waiting for transfers between devices, swap(): return lax.ppermute(value, axis, [(i, i ^ bit) for i in range(size)])  62.8 us
    ppermute x12, waiting for transfers between devices, shift(): lax.ppermute(value, 'tensor', [(i, (i + count) % size) for i in range(siz...  44 us
    ppermute x26, starting transfers between devices, swap(): return lax.ppermute(value, axis, [(i, i ^ bit) for i in range(size)])  26.9 us
    all_to_all x1, waiting for transfers between devices, group_collect(): lax.all_to_all(spread, 'tensor', split_axis=0, concat_axis=0, tiled=True)  15.2 us
    all_to_all x2, waiting for transfers between devices, group_part(): lax.all_to_all(half, 'tensor', split_axis=0, concat_axis=0, tiled=True)  13.4 us
    dot_general x11, matrix products, dot_rows(): lax.dot_general(left, right, (((1,), (1,)), ((), ())), preferred_element_...  13.1 us
    unnamed x222, local copies, waits for them, and re-layouts  11.7 us
    pallas_call x1, Pallas kernels, attend_back(): pl.pallas_call(attend_back_kernel, out_shape=jax.ShapeDtypeStruct((keys,...  10.1 us
  transfers between devices with their start and end apart: 41, of which 24 were waited for; matrix products, arithmetic and copies ran while one was open for 26% of the time, Pallas kernels for 6%

commit v1 on v0

--- a/solution.py
+++ b/solution.py
@@ -96,10 +96,11 @@
     return pieces
 
 
-def scatter_rows(rows, first, last):
+def scatter_rows(rows, first, last, gate=None):
     for place in range(first, last):
         half = rows.shape[0] // 2
-        rows = rows[:half] + swap(rows[half:], "shard", 1 << place)
+        kept = rows[:half] if gate is None else after(rows[:half], gate)
+        rows = kept + swap(rows[half:], "shard", 1 << place)
     return rows
 
 
@@ -325,11 +326,14 @@
         joined = jnp.concatenate(weights, 1)
         return (joined.astype(jnp.float32) * gain[:, None]).astype(jnp.bfloat16)
 
-    attn_local = jnp.concatenate([key_weight, value_weight, w_query], 1)
+    k_early, v_early, q_early, o_early, _ = lax.optimization_barrier(
+        (key_weight, value_weight, w_query, w_output, other)
+    )
+    attn_local = jnp.concatenate([k_early, v_early, q_early], 1)
     attn_cols = attn_local.shape[1]
     gap = -attn_cols % 128
     gaps = jnp.zeros((attn_local.shape[0], gap), jnp.bfloat16)
-    first_local = jnp.concatenate([gained([attn_local], attn_gain), gaps, w_output.T], 1)
+    first_local = jnp.concatenate([gained([attn_local], attn_gain), gaps, o_early.T], 1)
     first_pieces = gather_pieces(first_local, None)
     ends = (2 * kv_cols, attn_cols, attn_cols + gap)
     w_kv = jnp.concatenate([piece[:, : ends[0]] for piece in first_pieces], 0)
@@ -397,44 +401,46 @@
     mlp_term = jnp.concatenate(
         [dot_cols(group, grad_in).astype(jnp.bfloat16), dot_cols(cot_group, act).astype(jnp.bfloat16)], 1
     )
-    mlp_term = scatter_rows(mlp_term, 0, 1)
+    mlp_beside = swap(mlp_term[mlp_term.shape[0] // 2 :], "shard", 1)
     half_cols = mlp_term.shape[1] // 2
-    first, second = mlp_term[:, :half_cols], mlp_term[:, half_cols:]
     later = context == 1
-    mlp_kept, mlp_sent = jnp.where(later, second, first), jnp.where(later, first, second)
 
     grad_nm = (backs[0] + shift(grad_nm, 1)).astype(jnp.float32)
     grad_hidden = own_cot.astype(jnp.float32) + norm_back(grad_nm, hidden, scale_m)
     gain_m_term = jnp.sum(grad_nm * (hidden * scale_m), axis=0)
     grad_hidden_low = grad_hidden.astype(jnp.bfloat16)
     grad_mix = dot(grad_hidden_low, out_weight).astype(jnp.bfloat16)
-    out_term = scatter_rows(dot_cols(grad_hidden_low, mix).astype(jnp.bfloat16), 0, bits)
+    out_term = scatter_rows(dot_cols(grad_hidden_low, mix).astype(jnp.bfloat16), 0, 1)
     forward = [dot_rows(act, w_dn).astype(jnp.bfloat16) for act in acts]
     total = shift(after(forward[1], grad_mix), 1)
-    grad_mix, mlp_kept, mlp_sent = barrier((grad_mix, mlp_kept, mlp_sent))
-    owned = mlp_sent.shape[0] // 2 if bits > 1 else 0
-    mlp_early = swap(mlp_sent[owned:], "context", 1)
-
     grads = attend_back(
         query_rot, key_rot, value, mix, grad_mix, log_total, query_table, key_table, query_pos, key_pos
     )
-    grads, out_term, total, mlp_early = barrier((grads, out_term, total, mlp_early))
+    grads, out_term, total, mlp_beside = barrier((grads, out_term, total, mlp_beside))
 
     spot = (jnp.arange(grads.shape[1]) == attn_cols).astype(jnp.float32)
     attn_term = dot_cols(all_normed, grads) + gain_m_term[:, None] * spot[None, :]
     attn_term = scatter_rows(attn_term.astype(jnp.bfloat16), 0, 1)
-    mlp_late = swap(after(mlp_sent[:owned], attn_term), "context", 1)
+    attn_core = attn_term
+    out_term = scatter_rows(out_term, 1, bits, attn_core)
     attn_term = scatter_rows(attn_term, 1, bits)
     grad_query, grad_kv = grads[:rows, 2 * kv_cols : attn_cols], grads[:, : 2 * kv_cols]
-    pair = grad_kv[: 2 * rows] + swap(grad_kv[2 * rows :], "context", 1)
+    pair = after(grad_kv[: 2 * rows], attn_core) + swap(grad_kv[2 * rows :], "context", 1)
     own_kv = pair[:rows] + swap(pair[rows:], "tensor", 1)
     out_part = group_part(group_halves(out_term, context))
+
+    mlp_term = after(mlp_term[: mlp_beside.shape[0]], attn_core) + mlp_beside
+    first, second = mlp_term[:, :half_cols], mlp_term[:, half_cols:]
+    mlp_kept, mlp_sent = jnp.where(later, second, first), jnp.where(later, first, second)
+    owned = mlp_sent.shape[0] // 2
+    mlp_moved = swap(mlp_sent[owned:], "context", 1)
+    mlp_owned = swap(mlp_sent[:owned], "context", 1)
     total = shift(forward[2] + total, 1)
     total = shift(forward[3] + total, 1)
-    attn_term, own_kv, out_part, total = barrier((attn_term, own_kv, out_part, total))
+    attn_term, own_kv, out_part, total, mlp_kept = barrier((attn_term, own_kv, out_part, total, mlp_kept))
 
     attn_half = group_halves(attn_term, context)
-    mlp_half = scatter_rows(mlp_kept + jnp.concatenate([mlp_late, mlp_early], 0), 1, bits)
+    mlp_half = scatter_rows(mlp_kept + jnp.concatenate([mlp_owned, mlp_moved], 0), 1, bits)
     attn_part = group_part(attn_half)
     own_kv, grad_query, mlp_half = barrier((own_kv, grad_query, mlp_half))
     block = hidden + forward[0].astype(jnp.float32) + total.astype(jnp.float32)

time: 309 us -> 311 us (level)
    all_to_all x2, waiting for transfers between devices: 13.4 us -> 1.82 us  [group_part(): lax.all_to_all(half, 'tensor', split_axis=0, concat_axis=0, tiled=True)]
    ppermute x12, waiting for transfers between devices: 44 us -> 55.4 us  [shift(): lax.ppermute(value, 'tensor', [(i, (i + count) % size) for i in range(siz...]
    unnamed x222 -> x139, local copies, waits for them, and re-layouts: 11.7 us -> 7.86 us
    optimization_barrier x0 -> x3, local copies, waits for them, and re-layouts: none -> 3.38 us  [body(): lax.optimization_barrier((key_weight, value_weight, w_query, w_output, ot...]
  transfers between devices with their start and end apart: 41 -> 41, of which waited for: 24 -> 22; matrix products, arithmetic and copies ran while one was open for 26% -> 29% of each run, Pallas kernels for 6% -> 7%
where the time goes in v1:
time: 311 us; the launch traced here: 306 us
  waiting for transfers between devices  134 us (43%)
  starting transfers between devices  44 us (14%)
  other arithmetic  36.9 us (12%)
  local copies, waits for them, and re-layouts  36.7 us (12%)
  matrix products  30 us (10%)
  Pallas kernels  21.6 us (7%)
    ppermute x26, waiting for transfers between devices, swap(): return lax.ppermute(value, axis, [(i, i ^ bit) for i in range(size)])  62 us
    ppermute x12, waiting for transfers between devices, shift(): lax.ppermute(value, 'tensor', [(i, (i + count) % size) for i in range(siz...  55.4 us
    ppermute x26, starting transfers between devices, swap(): return lax.ppermute(value, axis, [(i, i ^ bit) for i in range(size)])  26.1 us
    all_to_all x1, waiting for transfers between devices, group_collect(): lax.all_to_all(spread, 'tensor', split_axis=0, concat_axis=0, tiled=True)  14.7 us
    dot_general x11, matrix products, dot_rows(): lax.dot_general(left, right, (((1,), (1,)), ((), ())), preferred_element_...  14.7 us
    pallas_call x1, Pallas kernels, attend_back(): pl.pallas_call(attend_back_kernel, out_shape=jax.ShapeDtypeStruct((keys,...  10.2 us
    all_to_all x2, starting transfers between devices, group_part(): lax.all_to_all(half, 'tensor', split_axis=0, concat_axis=0, tiled=True)  9.9 us
    pallas_call x1, Pallas kernels, attend(): pl.pallas_call(attend_kernel, out_shape=(jax.ShapeDtypeStruct(query.shape...  9.72 us
  transfers between devices with their start and end apart: 41, of which 22 were waited for; matrix products, arithmetic and copies ran while one was open for 29% of the time, Pallas kernels for 7%

profile of v1, /device:TPU:0, one launch (start us, length us, event | category | flops | bytes accessed | tf_op | source)
XLA Modules:
  0.0 305.8 jit_solution(1727168154910120239)
XLA Ops:
  2.5 4.0 %collective-permute-start = (bf16[96,960]{1,0:T(8,128)(2,1)}, bf16[96,960]{1,0:T(8,128)(2,1)}, u32[]{:S(2)}, u32[]{:S(2)}) collective-permute-start(bf16[96,960]{1,0:T(8,128)(2,1)} %get-tuple-element.213), channel_id=1, source_target_pairs={{0,2},{1,3},{2,0},{3,1},{4,6},{5,7},{6,4},{7,5},{8,10},{9,11},{10,... | collective-permute-start | bytes 552968 | tf_op jit(solution)/shard_map/ppermute | solution.py:81
  28.8 8.7 %collective-permute-done.1 = bf16[192,960]{1,0:T(8,128)(2,1)} collective-permute-done((bf16[192,960]{1,0:T(8,128)(2,1)S(1)}, bf16[192,960]{1,0:T(8,128)(2,1)}, u32[]{:S(2)}, u32[]{:S(2)}) %collective-permute-start.1) | collective-permute-done | bytes 368672 | tf_op jit(solution)/shard_map/ppermute | solution.py:81
  43.5 7.3 %collective-permute-done.4 = bf16[2,96,960]{2,1,0:T(8,128)(2,1)S(1)} collective-permute-done((bf16[2,96,960]{2,1,0:T(8,128)(2,1)}, bf16[2,96,960]{2,1,0:T(8,128)(2,1)S(1)}, u32[]{:S(2)}, u32[]{:S(2)}) %collective-permute-start.4) | collective-permute-done | bytes 368672 | tf_op jit(solution)/shard_map/ppermute | solution.py:109
  67.2 9.7 %attend.1 = (bf16[192,960]{1,0:T(8,128)(2,1)S(1)}, f32[576,8]{1,0:T(8,128)S(1)}, bf16[192,960]{1,0:T(8,128)(2,1)S(1)}, bf16[768,320]{1,0:T(8,128)(2,1)S(1)}) custom-call(f32[192,960]{1,0:T(8,128)S(1)} %fusion.37.q_ref, f32[768,320]{1,0:T(8,128)S(1)} %slice.478.k_ref, bf16[768,320]{1,0:T(8,128)(2,1)S(1)} %slice.622.v_ref, ...), custom_call_target="tpu_custom_call" | custom-call | flops 566231040 | bytes 4000000 | tf_op jit(solution)/shard_map/attend/pallas_call | solution.py:217
  78.6 10.1 %collective-permute-done.10 = bf16[240,1920]{1,0:T(8,128)(2,1)S(1)} collective-permute-done((bf16[240,1920]{1,0:T(8,128)(2,1)}, bf16[240,1920]{1,0:T(8,128)(2,1)S(1)}, u32[]{:S(2)}, u32[]{:S(2)}) %collective-permute-start.10) | collective-permute-done | bytes 921632 | tf_op jit(solution)/shard_map/ppermute | solution.py:81
  95.7 9.9 %collective-permute-done.14 = bf16[192,960]{1,0:T(8,128)(2,1)S(1)} collective-permute-done((bf16[192,960]{1,0:T(8,128)(2,1)S(1)}, bf16[192,960]{1,0:T(8,128)(2,1)S(1)}, u32[]{:S(2)}, u32[]{:S(2)}) %collective-permute-start.14) | collective-permute-done | bytes 368672 | tf_op jit(solution)/shard_map/ppermute | solution.py:109
  107.6 6.4 %collective-permute-done.16 = bf16[192,960]{1,0:T(8,128)(2,1)S(1)} collective-permute-done((bf16[192,960]{1,0:T(8,128)(2,1)S(1)}, bf16[192,960]{1,0:T(8,128)(2,1)S(1)}, u32[]{:S(2)}, u32[]{:S(2)}) %collective-permute-start.16) | collective-permute-done | bytes 368672 | tf_op jit(solution)/shard_map/ppermute | solution.py:109
  115.0 7.4 %collective-permute-done.15 = bf16[192,960]{1,0:T(8,128)(2,1)S(1)} collective-permute-done((bf16[192,960]{1,0:T(8,128)(2,1)S(1)}, bf16[192,960]{1,0:T(8,128)(2,1)S(1)}, u32[]{:S(2)}, u32[]{:S(2)}) %collective-permute-start.15) | collective-permute-done | bytes 368672 | tf_op jit(solution)/shard_map/ppermute | solution.py:109
  123.8 5.8 %collective-permute-done.17 = bf16[192,960]{1,0:T(8,128)(2,1)S(1)} collective-permute-done((bf16[192,960]{1,0:T(8,128)(2,1)S(1)}, bf16[192,960]{1,0:T(8,128)(2,1)S(1)}, u32[]{:S(2)}, u32[]{:S(2)}) %collective-permute-start.17) | collective-permute-done | bytes 368672 | tf_op jit(solution)/shard_map/ppermute | solution.py:109
  134.2 4.6 %pad_maximum_fusion.3 = (bf16[480,1920]{1,0:T(8,128)(2,1)}, bf16[480,1920]{1,0:T(8,128)(2,1)S(1)}) fusion(bf16[960,640]{1,0:T(8,128)(2,1)S(1)} %convolution_convert_fusion.2, bf16[960,1280]{1,0:T(8,128)(2,1)S(1)} %convolution_convert_fusion), kind=kLoop, calls=%fused_computation.19 | loop fusion | flops 7372800 | bytes 7372800 | tf_op jit(solution)/shard_map/concatenate | solution.py:401
  138.7 3.4 %collective-permute-done.18 = bf16[192,960]{1,0:T(8,128)(2,1)S(1)} collective-permute-done((bf16[192,960]{1,0:T(8,128)(2,1)S(1)}, bf16[192,960]{1,0:T(8,128)(2,1)S(1)}, u32[]{:S(2)}, u32[]{:S(2)}) %collective-permute-start.18) | collective-permute-done | bytes 368672 | tf_op jit(solution)/shard_map/ppermute | solution.py:109
  145.9 10.2 %attend_back.1 = bf16[768,1664]{1,0:T(8,128)(2,1)S(1)} custom-call(bf16[192,960]{1,0:T(8,128)(2,1)S(1)} %get-tuple-element.72.q_ref, bf16[768,320]{1,0:T(8,128)(2,1)S(1)} %get-tuple-element.73.k_ref, bf16[768,320]{1,0:T(8,128)(2,1)S(1)} %slice.622.v_ref, bf16[192,960]{1,0:T(8,128)(2,1)S(1)} %get-tuple-element.74.mix_ref, ...), custom_call_target="tpu_custom_call" | custom-call | flops 1415577600 | bytes 6000000 | tf_op jit(solution)/shard_map/attend_back/pallas_call | solution.py:272
  156.2 3.0 collective-permute-done.20
  159.2 3.2 %add_convert_fusion = bf16[960,1664]{1,0:T(8,128)(2,1)S(1)} fusion(bf16[768,960]{1,0:T(8,128)(2,1)S(1)} %multiply_convert_fusion, bf16[768,1664]{1,0:T(8,128)(2,1)S(1)} %attend_back.1, f32[1664]{0:T(1024)S(1)} %fusion.57, f32[960]{0:T(1024)S(1)} %get-tuple-element.119), kind=kOutput, calls=%fused_computation | convolution fusion | flops 2458460160 | bytes 7235840 | tf_op jit(solution)/shard_map/dot_general | solution.py:31
  170.5 10.4 %collective-permute-done.28 = bf16[192,960]{1,0:T(8,128)(2,1)S(1)} collective-permute-done((bf16[192,960]{1,0:T(8,128)(2,1)S(1)}, bf16[192,960]{1,0:T(8,128)(2,1)S(1)}, u32[]{:S(2)}, u32[]{:S(2)}) %collective-permute-start.28) | collective-permute-done | bytes 368672 | tf_op jit(solution)/shard_map/ppermute | solution.py:109
  189.6 4.3 %collective-permute-done.27 = bf16[128,960]{1,0:T(8,128)(2,1)S(1)} collective-permute-done((bf16[128,960]{1,0:T(8,128)(2,1)S(1)}, bf16[128,960]{1,0:T(8,128)(2,1)S(1)}, u32[]{:S(2)}, u32[]{:S(2)}) %collective-permute-start.27) | collective-permute-done | bytes 245792 | tf_op jit(solution)/shard_map/ppermute | solution.py:81
  194.6 5.1 %all-to-all-start = ((bf16[4,32,960]{2,1,0:T(8,128)(2,1)}), bf16[4,32,960]{2,1,0:T(8,128)(2,1)S(1)}, u32[]{:S(2)}, u32[]{:S(2)}) async-start(bf16[4,32,960]{2,1,0:T(8,128)(2,1)} %bitcast.13), calls=%async_computation | async-start | bytes 524288 | tf_op jit(solution)/shard_map/all_to_all | solution.py:132
  210.2 6.2 %collective-permute-done.31 = bf16[240,960]{1,0:T(8,128)(2,1)} collective-permute-done((bf16[240,960]{1,0:T(8,128)(2,1)}, bf16[240,960]{1,0:T(8,128)(2,1)}, u32[]{:S(2)}, u32[]{:S(2)}) %collective-permute-start.31) | collective-permute-done | bytes 460832 | tf_op jit(solution)/shard_map/ppermute | solution.py:81
  216.4 10.5 %collective-permute-done.32 = bf16[240,960]{1,0:T(8,128)(2,1)} collective-permute-done((bf16[240,960]{1,0:T(8,128)(2,1)}, bf16[240,960]{1,0:T(8,128)(2,1)}, u32[]{:S(2)}, u32[]{:S(2)}) %collective-permute-start.32) | collective-permute-done | bytes 460832 | tf_op jit(solution)/shard_map/ppermute | solution.py:81
  233.9 4.8 %all-to-all-start.1 = ((bf16[4,32,1664]{2,1,0:T(8,128)(2,1)}), bf16[4,32,1664]{2,1,0:T(8,128)(2,1)S(1)}, u32[]{:S(2)}, u32[]{:S(2)}) async-start(bf16[4,32,1664]{2,1,0:T(8,128)(2,1)} %bitcast.14), calls=%async_computation.1 | async-start | bytes 851968 | tf_op jit(solution)/shard_map/all_to_all | solution.py:132
  250.7 5.8 %collective-permute-done.34 = bf16[96,960]{1,0:T(8,128)(2,1)S(1)} collective-permute-done((bf16[96,960]{1,0:T(8,128)(2,1)S(1)}, bf16[96,960]{1,0:T(8,128)(2,1)S(1)}, u32[]{:S(2)}, u32[]{:S(2)}) %collective-permute-start.34) | collective-permute-done | bytes 184352 | tf_op jit(solution)/shard_map/ppermute | solution.py:81
  259.1 3.6 %all-to-all-start.2 = ((bf16[4,32,2688]{2,1,0:T(8,128)(2,1)}), bf16[4,32,2688]{2,1,0:T(8,128)(2,1)S(1)}, u32[]{:S(2)}, u32[]{:S(2)}) async-start(bf16[4,32,2688]{2,1,0:T(8,128)(2,1)} %broadcast_in_dim.16), calls=%async_computation.2 | async-start | bytes 1376256 | tf_op jit(solution)/shard_map/all_to_all | solution.py:141
  270.8 14.7 %all-to-all-done.2 = bf16[4,32,2688]{2,1,0:T(8,128)(2,1)S(1)} async-done(((bf16[4,32,2688]{2,1,0:T(8,128)(2,1)}), bf16[4,32,2688]{2,1,0:T(8,128)(2,1)S(1)}, u32[]{:S(2)}, u32[]{:S(2)}) %all-to-all-start.2) | async-done | bytes 688160 | tf_op jit(solution)/shard_map/all_to_all | solution.py:141
  291.3 9.5 %collective-permute-done.37 = bf16[128,2688]{1,0:T(8,128)(2,1)S(1)} collective-permute-done((bf16[128,2688]{1,0:T(8,128)(2,1)S(1)}, bf16[128,2688]{1,0:T(8,128)(2,1)S(1)}, u32[]{:S(2)}, u32[]{:S(2)}) %collective-permute-start.37) | collective-permute-done | bytes 688160 | tf_op jit(solution)/shard_map/ppermute | solution.py:81
  (363 shorter events, 134.6 us)
Async XLA Ops:
  2.5 20.6 %collective-permute-start = (bf16[96,960]{1,0:T(8,128)(2,1)}, bf16[96,960]{1,0:T(8,128)(2,1)}, u32[]{:S(2)}, u32[]{:S(2)}) collective-permute-start(bf16[96,960]{1,0:T(8,128)(2,1)} %get-tuple-element.213), channel_id=1, source_target_pairs={{0,2},{1,3},{2,0},{3,1},{4,6},{5,7},{6,4},{7,5},{8,10},{9,11},{10,... | collective-permute-start | bytes 552968 | tf_op jit(solution)/shard_map/ppermute | solution.py:81
  12.5 47.4 %collective-permute-start.6 = (bf16[240,2624]{1,0:T(8,128)(2,1)}, bf16[240,2624]{1,0:T(8,128)(2,1)}, u32[]{:S(2)}, u32[]{:S(2)}) collective-permute-start(bf16[240,2624]{1,0:T(8,128)(2,1)} %concatenate.155), channel_id=1, source_target_pairs={{0,8},{8,0},{16,24},{24,16},{1,9},{9,1},{17,25},{25,17},{2,10},{10... | collective-permute-start | bytes 3778568 | tf_op jit(solution)/shard_map/ppermute | solution.py:81
  12.5 44.9 %collective-permute-start.5 = (bf16[240,2624]{1,0:T(8,128)(2,1)}, bf16[240,2624]{1,0:T(8,128)(2,1)}, u32[]{:S(2)}, u32[]{:S(2)}) collective-permute-start(bf16[240,2624]{1,0:T(8,128)(2,1)} %concatenate.155), channel_id=1, source_target_pairs={{0,16},{8,24},{16,0},{24,8},{1,17},{9,25},{17,1},{25,9},{2,18},{10... | collective-permute-start | bytes 3778568 | tf_op jit(solution)/shard_map/ppermute | solution.py:81
  17.0 35.2 %collective-permute-start.11 = (bf16[240,1920]{1,0:T(8,128)(2,1)}, bf16[240,1920]{1,0:T(8,128)(2,1)}, u32[]{:S(2)}, u32[]{:S(2)}) collective-permute-start(bf16[240,1920]{1,0:T(8,128)(2,1)} %pad_maximum_fusion.7), channel_id=1, source_target_pairs={{0,8},{8,0},{16,24},{24,16},{1,9},{9,1},{17,25},{25,17},{2,10},{10... | collective-permute-start | bytes 2764808 | tf_op jit(solution)/shard_map/ppermute | solution.py:81
  51.8 26.6 %collective-permute-start.9 = (bf16[2,96,960]{2,1,0:T(8,128)(2,1)}, bf16[2,96,960]{2,1,0:T(8,128)(2,1)S(1)}, u32[]{:S(2)}, u32[]{:S(2)}) collective-permute-start(bf16[2,96,960]{2,1,0:T(8,128)(2,1)} %maximum_select_fusion.1), channel_id=1, source_target_pairs={{0,3},{1,0},{2,1},{3,2},{4,7},{5,4},{6,5},{7,6},{8,11},{9,8},{10,9... | collective-permute-start | bytes 1105928 | tf_op jit(solution)/shard_map/ppermute | solution.py:109
  54.8 23.6 %collective-permute-start.8 = (bf16[2,96,960]{2,1,0:T(8,128)(2,1)S(1)}, bf16[2,96,960]{2,1,0:T(8,128)(2,1)S(1)}, u32[]{:S(2)}, u32[]{:S(2)}) collective-permute-start(bf16[2,96,960]{2,1,0:T(8,128)(2,1)S(1)} %collective-permute-done.4), channel_id=1, source_target_pairs={{0,1},{1,2},{2,3},{3,0},{4,5},{5,6},{6,7},{7,4},{8,9},{9,10},{10,1... | collective-permute-start | bytes 1105928 | tf_op jit(solution)/shard_map/ppermute | solution.py:109
  65.6 23.1 %collective-permute-start.10 = (bf16[240,1920]{1,0:T(8,128)(2,1)}, bf16[240,1920]{1,0:T(8,128)(2,1)S(1)}, u32[]{:S(2)}, u32[]{:S(2)}) collective-permute-start(bf16[240,1920]{1,0:T(8,128)(2,1)} %pad_maximum_fusion.7), channel_id=1, source_target_pairs={{0,16},{8,24},{16,0},{24,8},{1,17},{9,25},{17,1},{25,9},{2,18},{10... | collective-permute-start | bytes 2764808 | tf_op jit(solution)/shard_map/ppermute | solution.py:81
  94.9 19.1 %collective-permute-start.16 = (bf16[192,960]{1,0:T(8,128)(2,1)S(1)}, bf16[192,960]{1,0:T(8,128)(2,1)S(1)}, u32[]{:S(2)}, u32[]{:S(2)}) collective-permute-start(bf16[192,960]{1,0:T(8,128)(2,1)S(1)} %convolution_convert_fusion.10), channel_id=1, source_target_pairs={{0,1},{1,2},{2,3},{3,0},{4,5},{5,6},{6,7},{7,4},{8,9},{9,10},{10,1... | collective-permute-start | bytes 1105928 | tf_op jit(solution)/shard_map/ppermute | solution.py:109
  105.6 16.9 %collective-permute-start.15 = (bf16[192,960]{1,0:T(8,128)(2,1)S(1)}, bf16[192,960]{1,0:T(8,128)(2,1)S(1)}, u32[]{:S(2)}, u32[]{:S(2)}) collective-permute-start(bf16[192,960]{1,0:T(8,128)(2,1)S(1)} %collective-permute-done.14), channel_id=1, source_target_pairs={{0,1},{1,2},{2,3},{3,0},{4,5},{5,6},{6,7},{7,4},{8,9},{9,10},{10,1... | collective-permute-start | bytes 1105928 | tf_op jit(solution)/shard_map/ppermute | solution.py:109
  114.9 14.6 %collective-permute-start.17 = (bf16[192,960]{1,0:T(8,128)(2,1)S(1)}, bf16[192,960]{1,0:T(8,128)(2,1)S(1)}, u32[]{:S(2)}, u32[]{:S(2)}) collective-permute-start(bf16[192,960]{1,0:T(8,128)(2,1)S(1)} %fusion.25), channel_id=1, source_target_pairs={{0,1},{1,2},{2,3},{3,0},{4,5},{5,6},{6,7},{7,4},{8,9},{9,10},{10,1... | collective-permute-start | bytes 1105928 | tf_op jit(solution)/shard_map/ppermute | solution.py:109
  138.7 20.4 %collective-permute-start.21 = (bf16[480,1920]{1,0:T(8,128)(2,1)S(1)}, bf16[480,1920]{1,0:T(8,128)(2,1)S(1)}, u32[]{:S(2)}, u32[]{:S(2)}) collective-permute-start(bf16[480,1920]{1,0:T(8,128)(2,1)S(1)} %get-tuple-element.142), channel_id=1, source_target_pairs={{0,8},{8,0},{16,24},{24,16},{1,9},{9,1},{17,25},{25,17},{2,10},{10... | collective-permute-start | bytes 5529608 | tf_op jit(solution)/shard_map/ppermute | solution.py:81
  165.3 16.9 %collective-permute-start.22 = (bf16[480,1664]{1,0:T(8,128)(2,1)}, bf16[480,1664]{1,0:T(8,128)(2,1)}, u32[]{:S(2)}, u32[]{:S(2)}) collective-permute-start(bf16[480,1664]{1,0:T(8,128)(2,1)} %slice.505), channel_id=1, source_target_pairs={{0,8},{8,0},{16,24},{24,16},{1,9},{9,1},{17,25},{25,17},{2,10},{10... | collective-permute-start | bytes 4792328 | tf_op jit(solution)/shard_map/ppermute | solution.py:81
  168.4 17.2 %collective-permute-start.26 = (bf16[240,960]{1,0:T(8,128)(2,1)S(1)}, bf16[240,960]{1,0:T(8,128)(2,1)S(1)}, u32[]{:S(2)}, u32[]{:S(2)}) collective-permute-start(bf16[240,960]{1,0:T(8,128)(2,1)S(1)} %get-tuple-element.170), channel_id=1, source_target_pairs={{0,16},{8,24},{16,0},{24,8},{1,17},{9,25},{17,1},{25,9},{2,18},{10... | collective-permute-start | bytes 1382408 | tf_op jit(solution)/shard_map/ppermute | solution.py:81
  168.9 15.8 %collective-permute-start.24 = (bf16[384,640]{1,0:T(8,128)(2,1)S(1)}, bf16[384,640]{1,0:T(8,128)(2,1)S(1)}, u32[]{:S(2)}, u32[]{:S(2)}) collective-permute-start(bf16[384,640]{1,0:T(8,128)(2,1)S(1)} %get-tuple-element.143), channel_id=1, source_target_pairs={{0,4},{4,0},{1,5},{5,1},{2,6},{6,2},{3,7},{7,3},{8,12},{12,8},{9,1... | collective-permute-start | bytes 1474568 | tf_op jit(solution)/shard_map/ppermute | solution.py:81
  182.2 26.3 %collective-permute-start.29 = (bf16[192,960]{1,0:T(8,128)(2,1)}, bf16[192,960]{1,0:T(8,128)(2,1)}, u32[]{:S(2)}, u32[]{:S(2)}) collective-permute-start(bf16[192,960]{1,0:T(8,128)(2,1)} %fusion.21), channel_id=1, source_target_pairs={{0,1},{1,2},{2,3},{3,0},{4,5},{5,6},{6,7},{7,4},{8,9},{9,10},{10,1... | collective-permute-start | bytes 1105928 | tf_op jit(solution)/shard_map/ppermute | solution.py:109
  185.6 18.3 %collective-permute-start.25 = (bf16[192,640]{1,0:T(8,128)(2,1)}, bf16[192,640]{1,0:T(8,128)(2,1)}, u32[]{:S(2)}, u32[]{:S(2)}) collective-permute-start(bf16[192,640]{1,0:T(8,128)(2,1)} %slice.509), channel_id=1, source_target_pairs={{0,1},{1,0},{2,3},{3,2},{4,5},{5,4},{6,7},{7,6},{8,9},{9,8},{10,11... | collective-permute-start | bytes 737288 | tf_op jit(solution)/shard_map/ppermute | solution.py:81
  187.4 19.9 %collective-permute-start.23 = (bf16[240,1664]{1,0:T(8,128)(2,1)}, bf16[240,1664]{1,0:T(8,128)(2,1)}, u32[]{:S(2)}, u32[]{:S(2)}) collective-permute-start(bf16[240,1664]{1,0:T(8,128)(2,1)} %slice.507), channel_id=1, source_target_pairs={{0,16},{8,24},{16,0},{24,8},{1,17},{9,25},{17,1},{25,9},{2,18},{10... | collective-permute-start | bytes 2396168 | tf_op jit(solution)/shard_map/ppermute | solution.py:81
  201.9 14.5 %collective-permute-start.31 = (bf16[240,960]{1,0:T(8,128)(2,1)}, bf16[240,960]{1,0:T(8,128)(2,1)}, u32[]{:S(2)}, u32[]{:S(2)}) collective-permute-start(bf16[240,960]{1,0:T(8,128)(2,1)} %get-tuple-element.168), channel_id=1, source_target_pairs={{0,4},{4,0},{1,5},{5,1},{2,6},{6,2},{3,7},{7,3},{8,12},{12,8},{9,1... | collective-permute-start | bytes 1382408 | tf_op jit(solution)/shard_map/ppermute | solution.py:81
  203.4 23.5 %collective-permute-start.32 = (bf16[240,960]{1,0:T(8,128)(2,1)}, bf16[240,960]{1,0:T(8,128)(2,1)}, u32[]{:S(2)}, u32[]{:S(2)}) collective-permute-start(bf16[240,960]{1,0:T(8,128)(2,1)} %get-tuple-element.169), channel_id=1, source_target_pairs={{0,4},{4,0},{1,5},{5,1},{2,6},{6,2},{3,7},{7,3},{8,12},{12,8},{9,1... | collective-permute-start | bytes 1382408 | tf_op jit(solution)/shard_map/ppermute | solution.py:81
  208.6 24.3 %collective-permute-start.30 = (bf16[128,1664]{1,0:T(8,128)(2,1)S(1)}, bf16[128,1664]{1,0:T(8,128)(2,1)S(1)}, u32[]{:S(2)}, u32[]{:S(2)}) collective-permute-start(bf16[128,1664]{1,0:T(8,128)(2,1)S(1)} %pad_dynamic-slice_fusion), channel_id=1, source_target_pairs={{0,4},{4,0},{1,5},{5,1},{2,6},{6,2},{3,7},{7,3},{8,12},{12,8},{9,1... | collective-permute-start | bytes 1277960 | tf_op jit(solution)/shard_map/ppermute | solution.py:81
  233.9 16.8 %all-to-all-start.1 = ((bf16[4,32,1664]{2,1,0:T(8,128)(2,1)}), bf16[4,32,1664]{2,1,0:T(8,128)(2,1)S(1)}, u32[]{:S(2)}, u32[]{:S(2)}) async-start(bf16[4,32,1664]{2,1,0:T(8,128)(2,1)} %bitcast.14), calls=%async_computation.1 | async-start | bytes 851968 | tf_op jit(solution)/shard_map/all_to_all | solution.py:132
  259.1 26.3 %all-to-all-start.2 = ((bf16[4,32,2688]{2,1,0:T(8,128)(2,1)}), bf16[4,32,2688]{2,1,0:T(8,128)(2,1)S(1)}, u32[]{:S(2)}, u32[]{:S(2)}) async-start(bf16[4,32,2688]{2,1,0:T(8,128)(2,1)} %broadcast_in_dim.16), calls=%async_computation.2 | async-start | bytes 1376256 | tf_op jit(solution)/shard_map/all_to_all | solution.py:141
  263.4 25.3 %collective-permute-start.36 = (bf16[96,960]{1,0:T(8,128)(2,1)}, bf16[96,960]{1,0:T(8,128)(2,1)}, u32[]{:S(2)}, u32[]{:S(2)}) collective-permute-start(bf16[96,960]{1,0:T(8,128)(2,1)} %get-tuple-element.178), channel_id=1, source_target_pairs={{0,2},{1,3},{2,0},{3,1},{4,6},{5,7},{6,4},{7,5},{8,10},{9,11},{10,... | collective-permute-start | bytes 552968 | tf_op jit(solution)/shard_map/ppermute | solution.py:81
  285.5 15.3 %collective-permute-start.37 = (bf16[128,2688]{1,0:T(8,128)(2,1)S(1)}, bf16[128,2688]{1,0:T(8,128)(2,1)S(1)}, u32[]{:S(2)}, u32[]{:S(2)}) collective-permute-start(bf16[128,2688]{1,0:T(8,128)(2,1)S(1)} %bitcast.75), channel_id=1, source_target_pairs={{0,4},{4,0},{1,5},{5,1},{2,6},{6,2},{3,7},{7,3},{8,12},{12,8},{9,1... | collective-permute-start | bytes 2064392 | tf_op jit(solution)/shard_map/ppermute | solution.py:81
  (83 other events, 1007.0 us)

commit v2 on v1

--- a/solution.py
+++ b/solution.py
@@ -187,22 +187,30 @@
     return slice(index * HEAD_SIZE, (index + 1) * HEAD_SIZE)
 
 
-def attend_kernel(q_ref, k_ref, v_ref, qt_ref, kt_ref, qp_ref, kp_ref, mix_ref, log_ref, qr_ref, kr_ref):
-    hidden = jnp.where(kp_ref[...] <= qp_ref[...], 0.0, -1e30)
-    hidden = jnp.concatenate([hidden] * GROUP, 0)
-    rows = q_ref.shape[0]
+def attend_kernel(
+    x_ref, n_ref, w_ref, kt_ref, qp_ref, kp_ref, mix_ref, log_ref, qr_ref, kr_ref, v_ref, hidden_ref, normed_ref
+):
+    rows, width = x_ref.shape
+    kv_cols, q_cols = kr_ref.shape[1], qr_ref.shape[1]
+    used = 2 * kv_cols + q_cols
+    first = used + -used % 128
+    masked = jnp.where(kp_ref[...] <= qp_ref[...], 0.0, -1e30)
+    masked = jnp.concatenate([masked] * GROUP, 0)
+    keys_values = dot(n_ref[...], w_ref[:, : 2 * kv_cols])
+    queries = dot(n_ref[:rows, :], w_ref[:, 2 * kv_cols : used])
+    v_ref[...] = keys_values[:, kv_cols:].astype(jnp.bfloat16)
     for g in range(KEY_VALUE_HEADS):
-        key = turn(k_ref[:, head_cols(g)], kt_ref[...]).astype(jnp.bfloat16)
+        key = turn(keys_values[:, head_cols(g)], kt_ref[...]).astype(jnp.bfloat16)
         kr_ref[:, head_cols(g)] = key
         value = v_ref[:, head_cols(g)]
         heads = []
         for i in range(GROUP):
             cols = head_cols(g * GROUP + i)
-            head = turn(q_ref[:, cols], qt_ref[...]).astype(jnp.bfloat16) * SCALE
+            head = turn(queries[:, cols], kt_ref[:rows, :]).astype(jnp.bfloat16) * SCALE
             qr_ref[:, cols] = head
             heads.append(head)
         query = jnp.concatenate(heads, 0)
-        scores = dot_rows(query, key) + hidden
+        scores = dot_rows(query, key) + masked
         peak = jnp.max(scores, axis=-1, keepdims=True)
         expd = jnp.exp(scores - peak)
         total = jnp.sum(expd, axis=-1, keepdims=True)
@@ -210,26 +218,33 @@
         for i in range(GROUP):
             mix_ref[:, head_cols(g * GROUP + i)] = mixed[i * rows : (i + 1) * rows]
         log_ref[:, g : g + 1] = peak + jnp.log(total)
-
-
-def attend(query, key, value, query_table, key_table, query_pos, key_pos):
-    rows, keys = query.shape[0], key.shape[0]
+    hidden = x_ref[...].astype(jnp.float32) + dot_rows(mix_ref[...], w_ref[:, first : first + q_cols])
+    hidden_ref[...] = hidden
+    normed_ref[...] = (hidden * rms_scale(hidden)).astype(jnp.bfloat16)
+
+
+def attend(tokens, normed, weights, key_table, query_pos, key_pos, kv_cols, q_cols):
+    (rows, width), keys = tokens.shape, normed.shape[0]
+    bf16, f32 = jnp.bfloat16, jnp.float32
     return pl.pallas_call(
         attend_kernel,
         out_shape=(
-            jax.ShapeDtypeStruct(query.shape, jnp.bfloat16),
-            jax.ShapeDtypeStruct((GROUP * rows, 8), jnp.float32),
-            jax.ShapeDtypeStruct(query.shape, jnp.bfloat16),
-            jax.ShapeDtypeStruct(key.shape, jnp.bfloat16),
+            jax.ShapeDtypeStruct((rows, q_cols), bf16),
+            jax.ShapeDtypeStruct((GROUP * rows, 8), f32),
+            jax.ShapeDtypeStruct((rows, q_cols), bf16),
+            jax.ShapeDtypeStruct((keys, kv_cols), bf16),
+            jax.ShapeDtypeStruct((keys, kv_cols), bf16),
+            jax.ShapeDtypeStruct((rows, width), f32),
+            jax.ShapeDtypeStruct((rows, width), bf16),
         ),
         compiler_params=pltpu.CompilerParams(vmem_limit_bytes=KERNEL_VMEM),
         cost_estimate=pl.CostEstimate(
-            flops=4 * rows * keys * QUERY_HEADS * HEAD_SIZE,
+            flops=4 * rows * keys * QUERY_HEADS * HEAD_SIZE + 4 * keys * width * kv_cols,
             transcendentals=rows * keys * QUERY_HEADS,
-            bytes_accessed=4_000_000,
+            bytes_accessed=10_000_000,
         ),
         name="attend",
-    )(query, key, value, query_table, key_table, query_pos, key_pos)
+    )(tokens, normed, weights, key_table, query_pos, key_pos)
 
 
 def attend_back_kernel(
@@ -336,9 +351,7 @@
     first_local = jnp.concatenate([gained([attn_local], attn_gain), gaps, o_early.T], 1)
     first_pieces = gather_pieces(first_local, None)
     ends = (2 * kv_cols, attn_cols, attn_cols + gap)
-    w_kv = jnp.concatenate([piece[:, : ends[0]] for piece in first_pieces], 0)
-    w_q = jnp.concatenate([piece[:, ends[0] : ends[1]] for piece in first_pieces], 0)
-    out_weight = jnp.concatenate([piece[:, ends[2] :] for piece in first_pieces], 0)
+    first_weight = lax.optimization_barrier(jnp.concatenate(first_pieces, 0))
     mlp_local = jnp.concatenate([gained([w_gate, w_up], mlp_gain), w_down.T], 1)
 
     cots = [after(to_relative(cotangent, shards, shard), beside)]
@@ -350,20 +363,15 @@
     all_float = all_tokens.astype(jnp.float32)
     all_scale = rms_scale(all_float)
     all_normed = (all_float * all_scale).astype(jnp.bfloat16)
-    tokens_f, scale_a, normed_a = all_float[:rows], all_scale[:rows], all_normed[:rows]
-    query = dot(normed_a, w_q)
-    key_value = dot(all_normed, w_kv)
-    key, value = key_value[:, :kv_cols], key_value[:, kv_cols:].astype(jnp.bfloat16)
-    mix, log_total, query_rot, key_rot = attend(
-        query, key, value, query_table, key_table, query_pos, key_pos
-    )
-    mlp_pieces = gather_pieces(mlp_local, w_kv, mix)
+    tokens_f, scale_a = all_float[:rows], all_scale[:rows]
+    mix, log_total, query_rot, key_rot, value, hidden, normed_m = attend(
+        own, all_normed, first_weight, key_table, query_pos, key_pos, kv_cols, w_query.shape[1]
+    )
+    w_kv, w_q, out_weight = first_weight[:, : ends[0]], first_weight[:, ends[0] : ends[1]], first_weight[:, ends[2] :]
+    mlp_pieces = gather_pieces(mlp_local, first_weight, mix)
     w_in = jnp.concatenate([piece[:, : 2 * hidden_cols] for piece in mlp_pieces], 0)
     w_dn = jnp.concatenate([piece[:, 2 * hidden_cols :] for piece in mlp_pieces], 0)
-    hidden = tokens_f + dot_rows(mix, out_weight)
     scale_m = rms_scale(hidden)
-    normed_m = (hidden * scale_m).astype(jnp.bfloat16)
-
     normed_m, cots[2], cots[3] = lax.optimization_barrier((normed_m, cots[2], cots[3]))
 
     def cot_of(k):
@@ -434,13 +442,14 @@
     mlp_kept, mlp_sent = jnp.where(later, second, first), jnp.where(later, first, second)
     owned = mlp_sent.shape[0] // 2
     mlp_moved = swap(mlp_sent[owned:], "context", 1)
-    mlp_owned = swap(mlp_sent[:owned], "context", 1)
     total = shift(forward[2] + total, 1)
-    total = shift(forward[3] + total, 1)
+    total = shift(after(forward[3], attn_core) + total, 1)
     attn_term, own_kv, out_part, total, mlp_kept = barrier((attn_term, own_kv, out_part, total, mlp_kept))
 
     attn_half = group_halves(attn_term, context)
-    mlp_half = scatter_rows(mlp_kept + jnp.concatenate([mlp_owned, mlp_moved], 0), 1, bits)
+    mlp_owned = swap(after(mlp_sent[:owned], attn_half), "context", 1)
+    mlp_half = swap(mlp_kept[owned:] + mlp_moved, "shard", 2) + mlp_kept[:owned] + mlp_owned
+    mlp_half = scatter_rows(mlp_half, 2, bits)
     attn_part = group_part(attn_half)
     own_kv, grad_query, mlp_half = barrier((own_kv, grad_query, mlp_half))
     block = hidden + forward[0].astype(jnp.float32) + total.astype(jnp.float32)
@@ -448,8 +457,7 @@
     grad_na = dot_rows(grad_query, w_q) + dot_rows(own_kv, w_kv)
     grad_tokens = grad_hidden + norm_back(grad_na, tokens_f, scale_a)
     grad_tokens = from_relative(grad_tokens.astype(jnp.bfloat16), shards, shard)
-    block_back = swap(block[length:], "tensor", 2)
-    attn_part, mlp_half, grad_tokens, block_back = barrier((attn_part, mlp_half, grad_tokens, block_back))
+    attn_part, mlp_half, grad_tokens = barrier((attn_part, mlp_half, grad_tokens))
 
     fill = jnp.zeros((out_part.shape[0], -out_part.shape[1] % 128), jnp.bfloat16)
     parts = group_collect(jnp.concatenate([attn_part, out_part, fill], 1))
@@ -465,6 +473,7 @@
     up_total = mlp_total[:, hidden_cols : 2 * hidden_cols] * mlp_gain[:, None]
     down_total = mlp_total[:, 2 * hidden_cols :].T
     tokens_back = swap(grad_tokens[length:], "tensor", 2)
+    block_back = swap(block[length:], "tensor", 2)
     gate_total, block, grad_tokens = barrier((gate_total, block[:length], grad_tokens[:length]))
     block_out = both_sequences(block, block_back, upper)
     tokens_grad = both_sequences(grad_tokens, tokens_back, upper)

time: 311 us -> 288 us (0.926)
  waiting for transfers between devices: 134 us -> 120 us
  other arithmetic: 36.9 us -> 47.4 us
  local copies, waits for them, and re-layouts: 36.7 us -> 29.7 us
  starting transfers between devices: 44 us -> 37 us
  matrix products: 30 us -> 24.5 us
    ppermute x12, waiting for transfers between devices: 55.4 us -> 42 us  [shift(): lax.ppermute(value, 'tensor', [(i, (i + count) % size) for i in range(siz...]
    ppermute x26, starting transfers between devices: 26.1 us -> 19.7 us  [swap(): return lax.ppermute(value, axis, [(i, i ^ bit) for i in range(size)])]
    slice x14 -> x3, local copies, waits for them, and re-layouts: 8.19 us -> 2.89 us  [the longest x1 2.18 us: body(): mlp_moved = swap(mlp_sent[owned:], 'context', 1)]
    dot_general x11 -> x10, matrix products: 14.7 us -> 11.5 us  [dot_rows(): lax.dot_general(left, right, (((1,), (1,)), ((), ())), preferred_element_...]
    convert_element_type x1, other arithmetic: 0.38 us -> 3.52 us  [body(): all_float = all_tokens.astype(jnp.float32)]
    dot_general x11 -> x9, matrix products: 7.79 us -> 5.62 us  [dot(): return jnp.dot(left, right, preferred_element_type=jnp.float32)]
    unnamed x139 -> x124, local copies, waits for them, and re-layouts: 7.86 us -> 6.63 us
  transfers between devices with their start and end apart: 41 -> 41, of which waited for: 22 -> 25; matrix products, arithmetic and copies ran while one was open for 29% -> 30% of each run, Pallas kernels for 7% -> 7%
where the time goes in v2:
time: 288 us; the launch traced here: 283 us
  waiting for transfers between devices  120 us (42%)
  other arithmetic  47.4 us (16%)
  starting transfers between devices  37 us (13%)
  local copies, waits for them, and re-layouts  29.7 us (10%)
  matrix products  24.5 us (9%)
  Pallas kernels  21.7 us (8%)
    ppermute x26, waiting for transfers between devices, swap(): return lax.ppermute(value, axis, [(i, i ^ bit) for i in range(size)])  60.1 us
    ppermute x12, waiting for transfers between devices, shift(): lax.ppermute(value, 'tensor', [(i, (i + count) % size) for i in range(siz...  42 us
    ppermute x26, starting transfers between devices, swap(): return lax.ppermute(value, axis, [(i, i ^ bit) for i in range(size)])  19.7 us
    all_to_all x1, waiting for transfers between devices, group_collect(): lax.all_to_all(spread, 'tensor', split_axis=0, concat_axis=0, tiled=True)  14.8 us
    dot_general x10, matrix products, dot_rows(): lax.dot_general(left, right, (((1,), (1,)), ((), ())), preferred_element_...  11.5 us
    pallas_call x1, Pallas kernels, attend_back(): pl.pallas_call(attend_back_kernel, out_shape=jax.ShapeDtypeStruct((keys,...  10.1 us
    pallas_call x1, Pallas kernels, attend(): pl.pallas_call(attend_kernel, out_shape=(jax.ShapeDtypeStruct((rows, q_co...  9.8 us
    all_to_all x2, starting transfers between devices, group_part(): lax.all_to_all(half, 'tensor', split_axis=0, concat_axis=0, tiled=True)  8.31 us
  transfers between devices with their start and end apart: 41, of which 25 were waited for; matrix products, arithmetic and copies ran while one was open for 30% of the time, Pallas kernels for 7%

profile of v2, /device:TPU:0, one launch (start us, length us, event | category | flops | bytes accessed | tf_op | source)
XLA Modules:
  0.0 282.7 jit_solution(832412435089836214)
XLA Ops:
  2.5 4.0 %collective-permute-start = (bf16[96,960]{1,0:T(8,128)(2,1)}, bf16[96,960]{1,0:T(8,128)(2,1)}, u32[]{:S(2)}, u32[]{:S(2)}) collective-permute-start(bf16[96,960]{1,0:T(8,128)(2,1)} %get-tuple-element.215), channel_id=1, source_target_pairs={{0,2},{1,3},{2,0},{3,1},{4,6},{5,7},{6,4},{7,5},{8,10},{9,11},{10,... | collective-permute-start | bytes 552968 | tf_op jit(solution)/shard_map/ppermute | solution.py:81
  28.2 6.0 %collective-permute-done.1 = bf16[192,960]{1,0:T(8,128)(2,1)S(1)} collective-permute-done((bf16[192,960]{1,0:T(8,128)(2,1)S(1)}, bf16[192,960]{1,0:T(8,128)(2,1)S(1)}, u32[]{:S(2)}, u32[]{:S(2)}) %collective-permute-start.1) | collective-permute-done | bytes 368672 | tf_op jit(solution)/shard_map/ppermute | solution.py:81
  45.5 5.5 %collective-permute-done.4 = bf16[2,96,960]{2,1,0:T(8,128)(2,1)} collective-permute-done((bf16[2,96,960]{2,1,0:T(8,128)(2,1)}, bf16[2,96,960]{2,1,0:T(8,128)(2,1)}, u32[]{:S(2)}, u32[]{:S(2)}) %collective-permute-start.4) | collective-permute-done | bytes 368672 | tf_op jit(solution)/shard_map/ppermute | solution.py:109
  57.1 3.2 %pad_maximum_fusion.w_ref = bf16[960,2624]{1,0:T(8,128)(2,1)S(1)} fusion(bf16[240,2624]{1,0:T(8,128)(2,1)S(1)} %collective-permute-done.7, bf16[240,2624]{1,0:T(8,128)(2,1)} %collective-permute-done.6, bf16[240,2624]{1,0:T(8,128)(2,1)} %collective-permute-done.5, bf16[240,2624]{1,0:T(8,128)(2,1)} %concatenate.146), kind=kLoop, calls=%fused_computation.1 | loop fusion | flops 20152320 | bytes 10076160 | tf_op jit(solution)/shard_map/concatenate | solution.py:354
  61.0 9.8 %attend.1 = (bf16[192,960]{1,0:T(8,128)(2,1)S(1)}, f32[576,8]{1,0:T(8,128)S(1)}, bf16[192,960]{1,0:T(8,128)(2,1)S(1)}, bf16[768,320]{1,0:T(8,128)(2,1)S(1)}, bf1...) custom-call(bf16[192,960]{1,0:T(8,128)(2,1)S(1)} %pad_maximum_fusion.10.x_ref, ...), custom_call_target="tpu_custom_call" | custom-call | flops 1509949440 | bytes 10000000 | tf_op jit(solution)/shard_map/attend/pallas_call | solution.py:229
  72.3 6.4 %collective-permute-done.10 = bf16[240,1920]{1,0:T(8,128)(2,1)S(1)} collective-permute-done((bf16[240,1920]{1,0:T(8,128)(2,1)}, bf16[240,1920]{1,0:T(8,128)(2,1)S(1)}, u32[]{:S(2)}, u32[]{:S(2)}) %collective-permute-start.10) | collective-permute-done | bytes 921632 | tf_op jit(solution)/shard_map/ppermute | solution.py:81
  85.5 9.5 %collective-permute-done.14 = bf16[192,960]{1,0:T(8,128)(2,1)S(1)} collective-permute-done((bf16[192,960]{1,0:T(8,128)(2,1)S(1)}, bf16[192,960]{1,0:T(8,128)(2,1)S(1)}, u32[]{:S(2)}, u32[]{:S(2)}) %collective-permute-start.14) | collective-permute-done | bytes 368672 | tf_op jit(solution)/shard_map/ppermute | solution.py:109
  97.0 6.4 %collective-permute-done.16 = bf16[192,960]{1,0:T(8,128)(2,1)S(1)} collective-permute-done((bf16[192,960]{1,0:T(8,128)(2,1)S(1)}, bf16[192,960]{1,0:T(8,128)(2,1)S(1)}, u32[]{:S(2)}, u32[]{:S(2)}) %collective-permute-start.16) | collective-permute-done | bytes 368672 | tf_op jit(solution)/shard_map/ppermute | solution.py:109
  104.4 7.5 %collective-permute-done.15 = bf16[192,960]{1,0:T(8,128)(2,1)S(1)} collective-permute-done((bf16[192,960]{1,0:T(8,128)(2,1)S(1)}, bf16[192,960]{1,0:T(8,128)(2,1)S(1)}, u32[]{:S(2)}, u32[]{:S(2)}) %collective-permute-start.15) | collective-permute-done | bytes 368672 | tf_op jit(solution)/shard_map/ppermute | solution.py:109
  113.2 6.7 %collective-permute-done.17 = bf16[192,960]{1,0:T(8,128)(2,1)S(1)} collective-permute-done((bf16[192,960]{1,0:T(8,128)(2,1)S(1)}, bf16[192,960]{1,0:T(8,128)(2,1)S(1)}, u32[]{:S(2)}, u32[]{:S(2)}) %collective-permute-start.17) | collective-permute-done | bytes 368672 | tf_op jit(solution)/shard_map/ppermute | solution.py:109
  124.8 4.5 %pad_maximum_fusion.2 = (bf16[480,1920]{1,0:T(8,128)(2,1)}, bf16[480,1920]{1,0:T(8,128)(2,1)S(1)}) fusion(bf16[960,640]{1,0:T(8,128)(2,1)S(1)} %convolution_convert_fusion.2, bf16[960,1280]{1,0:T(8,128)(2,1)S(1)} %convolution_convert_fusion), kind=kLoop, calls=%fused_computation.22 | loop fusion | flops 7372800 | bytes 7372800 | tf_op jit(solution)/shard_map/concatenate | solution.py:409
  129.4 4.5 %collective-permute-done.18 = bf16[192,960]{1,0:T(8,128)(2,1)S(1)} collective-permute-done((bf16[192,960]{1,0:T(8,128)(2,1)S(1)}, bf16[192,960]{1,0:T(8,128)(2,1)S(1)}, u32[]{:S(2)}, u32[]{:S(2)}) %collective-permute-start.18) | collective-permute-done | bytes 368672 | tf_op jit(solution)/shard_map/ppermute | solution.py:109
  137.7 10.1 %attend_back.1 = bf16[768,1664]{1,0:T(8,128)(2,1)S(1)} custom-call(bf16[192,960]{1,0:T(8,128)(2,1)S(1)} %get-tuple-element.83.q_ref, bf16[768,320]{1,0:T(8,128)(2,1)S(1)} %get-tuple-element.84.k_ref, bf16[768,320]{1,0:T(8,128)(2,1)S(1)} %get-tuple-element.85.v_ref, bf16[192,960]{1,0:T(8,128)(2,1)S(1)} %get-tuple-element.81.mix_ref, ...), custom_call_target="tpu_custom_call" | custom-call | flops 1415577600 | bytes 6000000 | tf_op jit(solution)/shard_map/attend_back/pallas_call | solution.py:287
  150.8 3.2 %add_convert_fusion = bf16[960,1664]{1,0:T(8,128)(2,1)S(1)} fusion(bf16[768,960]{1,0:T(8,128)(2,1)S(1)} %multiply_convert_fusion.n_ref, bf16[768,1664]{1,0:T(8,128)(2,1)S(1)} %attend_back.1, f32[1664]{0:T(1024)S(1)} %fusion.66, f32[960]{0:T(1024)S(1)} %get-tuple-element.127), kind=kOutput, calls=%fused_computation | convolution fusion | flops 2458460160 | bytes 7235840 | tf_op jit(solution)/shard_map/dot_general | solution.py:31
  157.2 3.5 %convert_element_type.136 = f32[768,960]{1,0:T(8,128)} convert(bf16[768,960]{1,0:T(8,128)(2,1)} %copy-done.3) | non-fusion elementwise | flops 737280 | bytes 4423680 | tf_op jit(solution)/shard_map/convert_element_type | solution.py:363
  168.3 7.6 %collective-permute-done.24 = bf16[384,640]{1,0:T(8,128)(2,1)S(1)} collective-permute-done((bf16[384,640]{1,0:T(8,128)(2,1)S(1)}, bf16[384,640]{1,0:T(8,128)(2,1)S(1)}, u32[]{:S(2)}, u32[]{:S(2)}) %collective-permute-start.24) | collective-permute-done | bytes 491552 | tf_op jit(solution)/shard_map/ppermute | solution.py:81
  185.9 3.5 %all-to-all-start = ((bf16[4,32,960]{2,1,0:T(8,128)(2,1)}), bf16[4,32,960]{2,1,0:T(8,128)(2,1)S(1)}, u32[]{:S(2)}, u32[]{:S(2)}) async-start(bf16[4,32,960]{2,1,0:T(8,128)(2,1)} %bitcast.13), calls=%async_computation | async-start | bytes 524288 | tf_op jit(solution)/shard_map/all_to_all | solution.py:132
  200.6 4.9 %collective-permute-done.32 = bf16[240,960]{1,0:T(8,128)(2,1)} collective-permute-done((bf16[240,960]{1,0:T(8,128)(2,1)}, bf16[240,960]{1,0:T(8,128)(2,1)}, u32[]{:S(2)}, u32[]{:S(2)}) %collective-permute-start.32) | collective-permute-done | bytes 460832 | tf_op jit(solution)/shard_map/ppermute | solution.py:81
  215.1 4.8 %all-to-all-start.1 = ((bf16[4,32,1664]{2,1,0:T(8,128)(2,1)}), bf16[4,32,1664]{2,1,0:T(8,128)(2,1)S(1)}, u32[]{:S(2)}, u32[]{:S(2)}) async-start(bf16[4,32,1664]{2,1,0:T(8,128)(2,1)} %bitcast.14), calls=%async_computation.1 | async-start | bytes 851968 | tf_op jit(solution)/shard_map/all_to_all | solution.py:132
  219.9 5.7 %collective-permute-done.34 = bf16[240,960]{1,0:T(8,128)(2,1)S(1)} collective-permute-done((bf16[240,960]{1,0:T(8,128)(2,1)S(1)}, bf16[240,960]{1,0:T(8,128)(2,1)S(1)}, u32[]{:S(2)}, u32[]{:S(2)}) %collective-permute-start.34) | collective-permute-done | bytes 460832 | tf_op jit(solution)/shard_map/ppermute | solution.py:81
  233.6 4.0 %all-to-all-start.2 = ((bf16[4,32,2688]{2,1,0:T(8,128)(2,1)}), bf16[4,32,2688]{2,1,0:T(8,128)(2,1)S(1)}, u32[]{:S(2)}, u32[]{:S(2)}) async-start(bf16[4,32,2688]{2,1,0:T(8,128)(2,1)} %broadcast_in_dim.16), calls=%async_computation.2 | async-start | bytes 1376256 | tf_op jit(solution)/shard_map/all_to_all | solution.py:141
  242.6 5.9 %collective-permute-done.35 = bf16[240,960]{1,0:T(8,128)(2,1)S(1)} collective-permute-done((bf16[240,960]{1,0:T(8,128)(2,1)S(1)}, bf16[240,960]{1,0:T(8,128)(2,1)S(1)}, u32[]{:S(2)}, u32[]{:S(2)}) %collective-permute-start.35) | collective-permute-done | bytes 460832 | tf_op jit(solution)/shard_map/ppermute | solution.py:81
  248.8 14.8 %all-to-all-done.2 = bf16[4,32,2688]{2,1,0:T(8,128)(2,1)S(1)} async-done(((bf16[4,32,2688]{2,1,0:T(8,128)(2,1)}), bf16[4,32,2688]{2,1,0:T(8,128)(2,1)S(1)}, u32[]{:S(2)}, u32[]{:S(2)}) %all-to-all-start.2) | async-done | bytes 688160 | tf_op jit(solution)/shard_map/all_to_all | solution.py:141
  273.1 4.5 %collective-permute-done.37 = bf16[128,2688]{1,0:T(8,128)(2,1)S(1)} collective-permute-done((bf16[128,2688]{1,0:T(8,128)(2,1)S(1)}, bf16[128,2688]{1,0:T(8,128)(2,1)S(1)}, u32[]{:S(2)}, u32[]{:S(2)}) %collective-permute-start.37) | collective-permute-done | bytes 688160 | tf_op jit(solution)/shard_map/ppermute | solution.py:81
  (335 shorter events, 133.4 us)
Async XLA Ops:
  2.5 19.0 %collective-permute-start = (bf16[96,960]{1,0:T(8,128)(2,1)}, bf16[96,960]{1,0:T(8,128)(2,1)}, u32[]{:S(2)}, u32[]{:S(2)}) collective-permute-start(bf16[96,960]{1,0:T(8,128)(2,1)} %get-tuple-element.215), channel_id=1, source_target_pairs={{0,2},{1,3},{2,0},{3,1},{4,6},{5,7},{6,4},{7,5},{8,10},{9,11},{10,... | collective-permute-start | bytes 552968 | tf_op jit(solution)/shard_map/ppermute | solution.py:81
  12.4 30.1 %collective-permute-start.5 = (bf16[240,2624]{1,0:T(8,128)(2,1)}, bf16[240,2624]{1,0:T(8,128)(2,1)}, u32[]{:S(2)}, u32[]{:S(2)}) collective-permute-start(bf16[240,2624]{1,0:T(8,128)(2,1)} %concatenate.146), channel_id=1, source_target_pairs={{0,16},{8,24},{16,0},{24,8},{1,17},{9,25},{17,1},{25,9},{2,18},{10... | collective-permute-start | bytes 3778568 | tf_op jit(solution)/shard_map/ppermute | solution.py:81
  13.9 43.3 %collective-permute-start.6 = (bf16[240,2624]{1,0:T(8,128)(2,1)}, bf16[240,2624]{1,0:T(8,128)(2,1)}, u32[]{:S(2)}, u32[]{:S(2)}) collective-permute-start(bf16[240,2624]{1,0:T(8,128)(2,1)} %concatenate.146), channel_id=1, source_target_pairs={{0,8},{8,0},{16,24},{24,16},{1,9},{9,1},{17,25},{25,17},{2,10},{10... | collective-permute-start | bytes 3778568 | tf_op jit(solution)/shard_map/ppermute | solution.py:81
  15.9 37.3 %collective-permute-start.11 = (bf16[240,1920]{1,0:T(8,128)(2,1)}, bf16[240,1920]{1,0:T(8,128)(2,1)}, u32[]{:S(2)}, u32[]{:S(2)}) collective-permute-start(bf16[240,1920]{1,0:T(8,128)(2,1)} %pad_maximum_fusion.5), channel_id=1, source_target_pairs={{0,8},{8,0},{16,24},{24,16},{1,9},{9,1},{17,25},{25,17},{2,10},{10... | collective-permute-start | bytes 2764808 | tf_op jit(solution)/shard_map/ppermute | solution.py:81
  42.5 14.7 %collective-permute-start.7 = (bf16[240,2624]{1,0:T(8,128)(2,1)}, bf16[240,2624]{1,0:T(8,128)(2,1)S(1)}, u32[]{:S(2)}, u32[]{:S(2)}) collective-permute-start(bf16[240,2624]{1,0:T(8,128)(2,1)} %collective-permute-done.5), channel_id=1, source_target_pairs={{0,8},{8,0},{16,24},{24,16},{1,9},{9,1},{17,25},{25,17},{2,10},{10... | collective-permute-start | bytes 3778568 | tf_op jit(solution)/shard_map/ppermute | solution.py:81
  51.0 19.9 %collective-permute-start.9 = (bf16[2,96,960]{2,1,0:T(8,128)(2,1)}, bf16[2,96,960]{2,1,0:T(8,128)(2,1)S(1)}, u32[]{:S(2)}, u32[]{:S(2)}) collective-permute-start(bf16[2,96,960]{2,1,0:T(8,128)(2,1)} %maximum_select_fusion.1), channel_id=1, source_target_pairs={{0,3},{1,0},{2,1},{3,2},{4,7},{5,4},{6,5},{7,6},{8,11},{9,8},{10,9... | collective-permute-start | bytes 1105928 | tf_op jit(solution)/shard_map/ppermute | solution.py:109
  51.0 19.9 %collective-permute-start.8 = (bf16[2,96,960]{2,1,0:T(8,128)(2,1)}, bf16[2,96,960]{2,1,0:T(8,128)(2,1)S(1)}, u32[]{:S(2)}, u32[]{:S(2)}) collective-permute-start(bf16[2,96,960]{2,1,0:T(8,128)(2,1)} %collective-permute-done.4), channel_id=1, source_target_pairs={{0,1},{1,2},{2,3},{3,0},{4,5},{5,6},{6,7},{7,4},{8,9},{9,10},{10,1... | collective-permute-start | bytes 1105928 | tf_op jit(solution)/shard_map/ppermute | solution.py:109
  60.4 18.3 %collective-permute-start.10 = (bf16[240,1920]{1,0:T(8,128)(2,1)}, bf16[240,1920]{1,0:T(8,128)(2,1)S(1)}, u32[]{:S(2)}, u32[]{:S(2)}) collective-permute-start(bf16[240,1920]{1,0:T(8,128)(2,1)} %pad_maximum_fusion.5), channel_id=1, source_target_pairs={{0,16},{8,24},{16,0},{24,8},{1,17},{9,25},{17,1},{25,9},{2,18},{10... | collective-permute-start | bytes 2764808 | tf_op jit(solution)/shard_map/ppermute | solution.py:81
  81.0 14.0 %collective-permute-start.14 = (bf16[192,960]{1,0:T(8,128)(2,1)S(1)}, bf16[192,960]{1,0:T(8,128)(2,1)S(1)}, u32[]{:S(2)}, u32[]{:S(2)}) collective-permute-start(bf16[192,960]{1,0:T(8,128)(2,1)S(1)} %collective-permute-done.13), channel_id=1, source_target_pairs={{0,1},{1,2},{2,3},{3,0},{4,5},{5,6},{6,7},{7,4},{8,9},{9,10},{10,1... | collective-permute-start | bytes 1105928 | tf_op jit(solution)/shard_map/ppermute | solution.py:109
  84.7 18.7 %collective-permute-start.16 = (bf16[192,960]{1,0:T(8,128)(2,1)S(1)}, bf16[192,960]{1,0:T(8,128)(2,1)S(1)}, u32[]{:S(2)}, u32[]{:S(2)}) collective-permute-start(bf16[192,960]{1,0:T(8,128)(2,1)S(1)} %convolution_convert_fusion.8), channel_id=1, source_target_pairs={{0,1},{1,2},{2,3},{3,0},{4,5},{5,6},{6,7},{7,4},{8,9},{9,10},{10,1... | collective-permute-start | bytes 1105928 | tf_op jit(solution)/shard_map/ppermute | solution.py:109
  95.0 16.9 %collective-permute-start.15 = (bf16[192,960]{1,0:T(8,128)(2,1)S(1)}, bf16[192,960]{1,0:T(8,128)(2,1)S(1)}, u32[]{:S(2)}, u32[]{:S(2)}) collective-permute-start(bf16[192,960]{1,0:T(8,128)(2,1)S(1)} %collective-permute-done.14), channel_id=1, source_target_pairs={{0,1},{1,2},{2,3},{3,0},{4,5},{5,6},{6,7},{7,4},{8,9},{9,10},{10,1... | collective-permute-start | bytes 1105928 | tf_op jit(solution)/shard_map/ppermute | solution.py:109
  104.3 15.6 %collective-permute-start.17 = (bf16[192,960]{1,0:T(8,128)(2,1)S(1)}, bf16[192,960]{1,0:T(8,128)(2,1)S(1)}, u32[]{:S(2)}, u32[]{:S(2)}) collective-permute-start(bf16[192,960]{1,0:T(8,128)(2,1)S(1)} %fusion.36), channel_id=1, source_target_pairs={{0,1},{1,2},{2,3},{3,0},{4,5},{5,6},{6,7},{7,4},{8,9},{9,10},{10,1... | collective-permute-start | bytes 1105928 | tf_op jit(solution)/shard_map/ppermute | solution.py:109
  129.4 21.4 %collective-permute-start.21 = (bf16[480,1920]{1,0:T(8,128)(2,1)S(1)}, bf16[480,1920]{1,0:T(8,128)(2,1)S(1)}, u32[]{:S(2)}, u32[]{:S(2)}) collective-permute-start(bf16[480,1920]{1,0:T(8,128)(2,1)S(1)} %get-tuple-element.150), channel_id=1, source_target_pairs={{0,8},{8,0},{16,24},{24,16},{1,9},{9,1},{17,25},{25,17},{2,10},{10... | collective-permute-start | bytes 5529608 | tf_op jit(solution)/shard_map/ppermute | solution.py:81
  162.9 14.1 %collective-permute-start.26 = (bf16[240,960]{1,0:T(8,128)(2,1)S(1)}, bf16[240,960]{1,0:T(8,128)(2,1)S(1)}, u32[]{:S(2)}, u32[]{:S(2)}) collective-permute-start(bf16[240,960]{1,0:T(8,128)(2,1)S(1)} %get-tuple-element.172), channel_id=1, source_target_pairs={{0,16},{8,24},{16,0},{24,8},{1,17},{9,25},{17,1},{25,9},{2,18},{10... | collective-permute-start | bytes 1382408 | tf_op jit(solution)/shard_map/ppermute | solution.py:81
  163.8 15.0 %collective-permute-start.28 = (bf16[192,960]{1,0:T(8,128)(2,1)S(1)}, bf16[192,960]{1,0:T(8,128)(2,1)S(1)}, u32[]{:S(2)}, u32[]{:S(2)}) collective-permute-start(bf16[192,960]{1,0:T(8,128)(2,1)S(1)} %fusion.33), channel_id=1, source_target_pairs={{0,1},{1,2},{2,3},{3,0},{4,5},{5,6},{6,7},{7,4},{8,9},{9,10},{10,1... | collective-permute-start | bytes 1105928 | tf_op jit(solution)/shard_map/ppermute | solution.py:109
  167.4 31.1 %collective-permute-start.23 = (bf16[240,1664]{1,0:T(8,128)(2,1)}, bf16[240,1664]{1,0:T(8,128)(2,1)}, u32[]{:S(2)}, u32[]{:S(2)}) collective-permute-start(bf16[240,1664]{1,0:T(8,128)(2,1)} %slice.448), channel_id=1, source_target_pairs={{0,16},{8,24},{16,0},{24,8},{1,17},{9,25},{17,1},{25,9},{2,18},{10... | collective-permute-start | bytes 2396168 | tf_op jit(solution)/shard_map/ppermute | solution.py:81
  176.8 17.1 %collective-permute-start.25 = (bf16[192,640]{1,0:T(8,128)(2,1)}, bf16[192,640]{1,0:T(8,128)(2,1)}, u32[]{:S(2)}, u32[]{:S(2)}) collective-permute-start(bf16[192,640]{1,0:T(8,128)(2,1)} %slice.450), channel_id=1, source_target_pairs={{0,1},{1,0},{2,3},{3,2},{4,5},{5,4},{6,7},{7,6},{8,9},{9,8},{10,11... | collective-permute-start | bytes 737288 | tf_op jit(solution)/shard_map/ppermute | solution.py:81
  179.7 20.3 %collective-permute-start.29 = (bf16[192,960]{1,0:T(8,128)(2,1)}, bf16[192,960]{1,0:T(8,128)(2,1)}, u32[]{:S(2)}, u32[]{:S(2)}) collective-permute-start(bf16[192,960]{1,0:T(8,128)(2,1)} %add.313), channel_id=1, source_target_pairs={{0,1},{1,2},{2,3},{3,0},{4,5},{5,6},{6,7},{7,4},{8,9},{9,10},{10,1... | collective-permute-start | bytes 1105928 | tf_op jit(solution)/shard_map/ppermute | solution.py:109
  191.7 13.8 %collective-permute-start.32 = (bf16[240,960]{1,0:T(8,128)(2,1)}, bf16[240,960]{1,0:T(8,128)(2,1)}, u32[]{:S(2)}, u32[]{:S(2)}) collective-permute-start(bf16[240,960]{1,0:T(8,128)(2,1)} %get-tuple-element.170), channel_id=1, source_target_pairs={{0,4},{4,0},{1,5},{5,1},{2,6},{6,2},{3,7},{7,3},{8,12},{12,8},{9,1... | collective-permute-start | bytes 1382408 | tf_op jit(solution)/shard_map/ppermute | solution.py:81
  215.1 17.4 %all-to-all-start.1 = ((bf16[4,32,1664]{2,1,0:T(8,128)(2,1)}), bf16[4,32,1664]{2,1,0:T(8,128)(2,1)S(1)}, u32[]{:S(2)}, u32[]{:S(2)}) async-start(bf16[4,32,1664]{2,1,0:T(8,128)(2,1)} %bitcast.14), calls=%async_computation.1 | async-start | bytes 851968 | tf_op jit(solution)/shard_map/all_to_all | solution.py:132
  233.6 30.1 %all-to-all-start.2 = ((bf16[4,32,2688]{2,1,0:T(8,128)(2,1)}), bf16[4,32,2688]{2,1,0:T(8,128)(2,1)S(1)}, u32[]{:S(2)}, u32[]{:S(2)}) async-start(bf16[4,32,2688]{2,1,0:T(8,128)(2,1)} %broadcast_in_dim.16), calls=%async_computation.2 | async-start | bytes 1376256 | tf_op jit(solution)/shard_map/all_to_all | solution.py:141
  238.9 29.1 %collective-permute-start.30 = (bf16[96,960]{1,0:T(8,128)(2,1)}, bf16[96,960]{1,0:T(8,128)(2,1)}, u32[]{:S(2)}, u32[]{:S(2)}) collective-permute-start(bf16[96,960]{1,0:T(8,128)(2,1)} %get-tuple-element.184), channel_id=1, source_target_pairs={{0,2},{1,3},{2,0},{3,1},{4,6},{5,7},{6,4},{7,5},{8,10},{9,11},{10,... | collective-permute-start | bytes 552968 | tf_op jit(solution)/shard_map/ppermute | solution.py:81
  242.6 27.9 %collective-permute-start.36 = (bf16[96,960]{1,0:T(8,128)(2,1)}, bf16[96,960]{1,0:T(8,128)(2,1)}, u32[]{:S(2)}, u32[]{:S(2)}) collective-permute-start(bf16[96,960]{1,0:T(8,128)(2,1)} %get-tuple-element.180), channel_id=1, source_target_pairs={{0,2},{1,3},{2,0},{3,1},{4,6},{5,7},{6,4},{7,5},{8,10},{9,11},{10,... | collective-permute-start | bytes 552968 | tf_op jit(solution)/shard_map/ppermute | solution.py:81
  263.7 14.0 %collective-permute-start.37 = (bf16[128,2688]{1,0:T(8,128)(2,1)S(1)}, bf16[128,2688]{1,0:T(8,128)(2,1)S(1)}, u32[]{:S(2)}, u32[]{:S(2)}) collective-permute-start(bf16[128,2688]{1,0:T(8,128)(2,1)S(1)} %bitcast.71), channel_id=1, source_target_pairs={{0,4},{4,0},{1,5},{5,1},{2,6},{6,2},{3,7},{7,3},{8,12},{12,8},{9,1... | collective-permute-start | bytes 2064392 | tf_op jit(solution)/shard_map/ppermute | solution.py:81
  (75 other events, 813.5 us)

commit v3 on v2

--- a/solution.py
+++ b/solution.py
@@ -418,7 +418,7 @@
     gain_m_term = jnp.sum(grad_nm * (hidden * scale_m), axis=0)
     grad_hidden_low = grad_hidden.astype(jnp.bfloat16)
     grad_mix = dot(grad_hidden_low, out_weight).astype(jnp.bfloat16)
-    out_term = scatter_rows(dot_cols(grad_hidden_low, mix).astype(jnp.bfloat16), 0, 1)
+    out_term = scatter_rows(dot_cols(grad_hidden_low, mix).astype(jnp.bfloat16), 0, bits)
     forward = [dot_rows(act, w_dn).astype(jnp.bfloat16) for act in acts]
     total = shift(after(forward[1], grad_mix), 1)
     grads = attend_back(
@@ -430,12 +430,11 @@
     attn_term = dot_cols(all_normed, grads) + gain_m_term[:, None] * spot[None, :]
     attn_term = scatter_rows(attn_term.astype(jnp.bfloat16), 0, 1)
     attn_core = attn_term
-    out_term = scatter_rows(out_term, 1, bits, attn_core)
     attn_term = scatter_rows(attn_term, 1, bits)
     grad_query, grad_kv = grads[:rows, 2 * kv_cols : attn_cols], grads[:, : 2 * kv_cols]
     pair = after(grad_kv[: 2 * rows], attn_core) + swap(grad_kv[2 * rows :], "context", 1)
     own_kv = pair[:rows] + swap(pair[rows:], "tensor", 1)
-    out_part = group_part(group_halves(out_term, context))
+    out_part = group_part(group_halves(after(out_term, attn_core), context))
 
     mlp_term = after(mlp_term[: mlp_beside.shape[0]], attn_core) + mlp_beside
     first, second = mlp_term[:, :half_cols], mlp_term[:, half_cols:]

time: 288 us -> 295 us (1.024)
  waiting for transfers between devices: 120 us -> 125 us
  transfers between devices with their start and end apart: 41 -> 41, of which waited for: 25 -> 24; matrix products, arithmetic and copies ran while one was open for 30% -> 29% of each run, Pallas kernels for 7% -> 7%
where the time goes in v3:
time: 295 us; the launch traced here: 290 us
  waiting for transfers between devices  125 us (42%)
  other arithmetic  47.2 us (16%)
  starting transfers between devices  39.8 us (13%)
  local copies, waits for them, and re-layouts  29.2 us (10%)
  matrix products  24.6 us (8%)
  Pallas kernels  21.7 us (7%)
    ppermute x26, waiting for transfers between devices, swap(): return lax.ppermute(value, axis, [(i, i ^ bit) for i in range(size)])  60.8 us
    ppermute x12, waiting for transfers between devices, shift(): lax.ppermute(value, 'tensor', [(i, (i + count) % size) for i in range(siz...  44.9 us
    ppermute x26, starting transfers between devices, swap(): return lax.ppermute(value, axis, [(i, i ^ bit) for i in range(size)])  21.7 us
    all_to_all x1, waiting for transfers between devices, group_collect(): lax.all_to_all(spread, 'tensor', split_axis=0, concat_axis=0, tiled=True)  14.2 us
    dot_general x10, matrix products, dot_rows(): lax.dot_general(left, right, (((1,), (1,)), ((), ())), preferred_element_...  11.5 us
    pallas_call x1, Pallas kernels, attend_back(): pl.pallas_call(attend_back_kernel, out_shape=jax.ShapeDtypeStruct((keys,...  10.1 us
    pallas_call x1, Pallas kernels, attend(): pl.pallas_call(attend_kernel, out_shape=(jax.ShapeDtypeStruct((rows, q_co...  9.8 us
    all_to_all x2, starting transfers between devices, group_part(): lax.all_to_all(half, 'tensor', split_axis=0, concat_axis=0, tiled=True)  8.42 us
  transfers between devices with their start and end apart: 41, of which 24 were waited for; matrix products, arithmetic and copies ran while one was open for 29% of the time, Pallas kernels for 7%

profile of v3, /device:TPU:0, one launch (start us, length us, event | category | flops | bytes accessed | tf_op | source)
XLA Modules:
  0.0 289.9 jit_solution(16656819056691311454)
XLA Ops:
  2.5 4.0 %collective-permute-start = (bf16[96,960]{1,0:T(8,128)(2,1)}, bf16[96,960]{1,0:T(8,128)(2,1)}, u32[]{:S(2)}, u32[]{:S(2)}) collective-permute-start(bf16[96,960]{1,0:T(8,128)(2,1)} %get-tuple-element.213), channel_id=1, source_target_pairs={{0,2},{1,3},{2,0},{3,1},{4,6},{5,7},{6,4},{7,5},{8,10},{9,11},{10,... | collective-permute-start | bytes 552968 | tf_op jit(solution)/shard_map/ppermute | solution.py:81
  28.2 6.0 %collective-permute-done.1 = bf16[192,960]{1,0:T(8,128)(2,1)S(1)} collective-permute-done((bf16[192,960]{1,0:T(8,128)(2,1)S(1)}, bf16[192,960]{1,0:T(8,128)(2,1)S(1)}, u32[]{:S(2)}, u32[]{:S(2)}) %collective-permute-start.1) | collective-permute-done | bytes 368672 | tf_op jit(solution)/shard_map/ppermute | solution.py:81
  45.5 5.5 %collective-permute-done.4 = bf16[2,96,960]{2,1,0:T(8,128)(2,1)} collective-permute-done((bf16[2,96,960]{2,1,0:T(8,128)(2,1)}, bf16[2,96,960]{2,1,0:T(8,128)(2,1)}, u32[]{:S(2)}, u32[]{:S(2)}) %collective-permute-start.4) | collective-permute-done | bytes 368672 | tf_op jit(solution)/shard_map/ppermute | solution.py:109
  57.1 3.2 %pad_maximum_fusion.w_ref = bf16[960,2624]{1,0:T(8,128)(2,1)S(1)} fusion(bf16[240,2624]{1,0:T(8,128)(2,1)S(1)} %collective-permute-done.7, bf16[240,2624]{1,0:T(8,128)(2,1)} %collective-permute-done.6, bf16[240,2624]{1,0:T(8,128)(2,1)} %collective-permute-done.5, bf16[240,2624]{1,0:T(8,128)(2,1)} %concatenate.146), kind=kLoop, calls=%fused_computation.1 | loop fusion | flops 20152320 | bytes 10076160 | tf_op jit(solution)/shard_map/concatenate | solution.py:354
  61.0 9.8 %attend.1 = (bf16[192,960]{1,0:T(8,128)(2,1)S(1)}, f32[576,8]{1,0:T(8,128)S(1)}, bf16[192,960]{1,0:T(8,128)(2,1)S(1)}, bf16[768,320]{1,0:T(8,128)(2,1)S(1)}, bf1...) custom-call(bf16[192,960]{1,0:T(8,128)(2,1)S(1)} %pad_maximum_fusion.10.x_ref, ...), custom_call_target="tpu_custom_call" | custom-call | flops 1509949440 | bytes 10000000 | tf_op jit(solution)/shard_map/attend/pallas_call | solution.py:229
  72.3 6.4 %collective-permute-done.10 = bf16[240,1920]{1,0:T(8,128)(2,1)S(1)} collective-permute-done((bf16[240,1920]{1,0:T(8,128)(2,1)}, bf16[240,1920]{1,0:T(8,128)(2,1)S(1)}, u32[]{:S(2)}, u32[]{:S(2)}) %collective-permute-start.10) | collective-permute-done | bytes 921632 | tf_op jit(solution)/shard_map/ppermute | solution.py:81
  85.5 9.5 %collective-permute-done.14 = bf16[192,960]{1,0:T(8,128)(2,1)S(1)} collective-permute-done((bf16[192,960]{1,0:T(8,128)(2,1)S(1)}, bf16[192,960]{1,0:T(8,128)(2,1)S(1)}, u32[]{:S(2)}, u32[]{:S(2)}) %collective-permute-start.14) | collective-permute-done | bytes 368672 | tf_op jit(solution)/shard_map/ppermute | solution.py:109
  97.0 6.4 %collective-permute-done.16 = bf16[192,960]{1,0:T(8,128)(2,1)S(1)} collective-permute-done((bf16[192,960]{1,0:T(8,128)(2,1)S(1)}, bf16[192,960]{1,0:T(8,128)(2,1)S(1)}, u32[]{:S(2)}, u32[]{:S(2)}) %collective-permute-start.16) | collective-permute-done | bytes 368672 | tf_op jit(solution)/shard_map/ppermute | solution.py:109
  104.4 7.4 %collective-permute-done.15 = bf16[192,960]{1,0:T(8,128)(2,1)S(1)} collective-permute-done((bf16[192,960]{1,0:T(8,128)(2,1)S(1)}, bf16[192,960]{1,0:T(8,128)(2,1)S(1)}, u32[]{:S(2)}, u32[]{:S(2)}) %collective-permute-start.15) | collective-permute-done | bytes 368672 | tf_op jit(solution)/shard_map/ppermute | solution.py:109
  113.2 6.7 %collective-permute-done.17 = bf16[192,960]{1,0:T(8,128)(2,1)S(1)} collective-permute-done((bf16[192,960]{1,0:T(8,128)(2,1)S(1)}, bf16[192,960]{1,0:T(8,128)(2,1)S(1)}, u32[]{:S(2)}, u32[]{:S(2)}) %collective-permute-start.17) | collective-permute-done | bytes 368672 | tf_op jit(solution)/shard_map/ppermute | solution.py:109
  124.9 9.0 %collective-permute-done.18 = bf16[192,960]{1,0:T(8,128)(2,1)S(1)} collective-permute-done((bf16[192,960]{1,0:T(8,128)(2,1)S(1)}, bf16[192,960]{1,0:T(8,128)(2,1)S(1)}, u32[]{:S(2)}, u32[]{:S(2)}) %collective-permute-start.18) | collective-permute-done | bytes 368672 | tf_op jit(solution)/shard_map/ppermute | solution.py:109
  136.0 4.5 %pad_maximum_fusion.2 = (bf16[480,1920]{1,0:T(8,128)(2,1)}, bf16[480,1920]{1,0:T(8,128)(2,1)S(1)}) fusion(bf16[960,640]{1,0:T(8,128)(2,1)S(1)} %convolution_convert_fusion.2, bf16[960,1280]{1,0:T(8,128)(2,1)S(1)} %convolution_convert_fusion), kind=kLoop, calls=%fused_computation.22 | loop fusion | flops 7372800 | bytes 7372800 | tf_op jit(solution)/shard_map/concatenate | solution.py:409
  142.9 10.1 %attend_back.1 = bf16[768,1664]{1,0:T(8,128)(2,1)S(1)} custom-call(bf16[192,960]{1,0:T(8,128)(2,1)S(1)} %get-tuple-element.83.q_ref, bf16[768,320]{1,0:T(8,128)(2,1)S(1)} %get-tuple-element.84.k_ref, bf16[768,320]{1,0:T(8,128)(2,1)S(1)} %get-tuple-element.85.v_ref, bf16[192,960]{1,0:T(8,128)(2,1)S(1)} %get-tuple-element.81.mix_ref, ...), custom_call_target="tpu_custom_call" | custom-call | flops 1415577600 | bytes 6000000 | tf_op jit(solution)/shard_map/attend_back/pallas_call | solution.py:287
  162.0 3.5 %convert_element_type.136 = f32[768,960]{1,0:T(8,128)} convert(bf16[768,960]{1,0:T(8,128)(2,1)} %copy-done.3) | non-fusion elementwise | flops 737280 | bytes 4423680 | tf_op jit(solution)/shard_map/convert_element_type | solution.py:363
  173.3 7.4 %collective-permute-done.25 = bf16[384,640]{1,0:T(8,128)(2,1)S(1)} collective-permute-done((bf16[384,640]{1,0:T(8,128)(2,1)S(1)}, bf16[384,640]{1,0:T(8,128)(2,1)S(1)}, u32[]{:S(2)}, u32[]{:S(2)}) %collective-permute-start.25) | collective-permute-done | bytes 491552 | tf_op jit(solution)/shard_map/ppermute | solution.py:81
  190.6 3.6 %all-to-all-start = ((bf16[4,32,960]{2,1,0:T(8,128)(2,1)}), bf16[4,32,960]{2,1,0:T(8,128)(2,1)S(1)}, u32[]{:S(2)}, u32[]{:S(2)}) async-start(bf16[4,32,960]{2,1,0:T(8,128)(2,1)} %bitcast.13), calls=%async_computation | async-start | bytes 524288 | tf_op jit(solution)/shard_map/all_to_all | solution.py:132
  198.6 5.2 %all-to-all-done = bf16[4,32,960]{2,1,0:T(8,128)(2,1)S(1)} async-done(((bf16[4,32,960]{2,1,0:T(8,128)(2,1)}), bf16[4,32,960]{2,1,0:T(8,128)(2,1)S(1)}, u32[]{:S(2)}, u32[]{:S(2)}) %all-to-all-start) | async-done | bytes 245792 | tf_op jit(solution)/shard_map/all_to_all | solution.py:132
  205.9 3.5 %collective-permute-done.32 = bf16[240,960]{1,0:T(8,128)(2,1)} collective-permute-done((bf16[240,960]{1,0:T(8,128)(2,1)}, bf16[240,960]{1,0:T(8,128)(2,1)}, u32[]{:S(2)}, u32[]{:S(2)}) %collective-permute-start.32) | collective-permute-done | bytes 460832 | tf_op jit(solution)/shard_map/ppermute | solution.py:81
  220.3 4.8 %all-to-all-start.1 = ((bf16[4,32,1664]{2,1,0:T(8,128)(2,1)}), bf16[4,32,1664]{2,1,0:T(8,128)(2,1)S(1)}, u32[]{:S(2)}, u32[]{:S(2)}) async-start(bf16[4,32,1664]{2,1,0:T(8,128)(2,1)} %bitcast.14), calls=%async_computation.1 | async-start | bytes 851968 | tf_op jit(solution)/shard_map/all_to_all | solution.py:132
  225.0 6.4 %collective-permute-done.34 = bf16[240,960]{1,0:T(8,128)(2,1)S(1)} collective-permute-done((bf16[240,960]{1,0:T(8,128)(2,1)S(1)}, bf16[240,960]{1,0:T(8,128)(2,1)S(1)}, u32[]{:S(2)}, u32[]{:S(2)}) %collective-permute-start.34) | collective-permute-done | bytes 460832 | tf_op jit(solution)/shard_map/ppermute | solution.py:81
  239.5 3.5 %all-to-all-start.2 = ((bf16[4,32,2688]{2,1,0:T(8,128)(2,1)}), bf16[4,32,2688]{2,1,0:T(8,128)(2,1)S(1)}, u32[]{:S(2)}, u32[]{:S(2)}) async-start(bf16[4,32,2688]{2,1,0:T(8,128)(2,1)} %broadcast_in_dim.16), calls=%async_computation.2 | async-start | bytes 1376256 | tf_op jit(solution)/shard_map/all_to_all | solution.py:141
  248.1 6.9 %collective-permute-done.35 = bf16[240,960]{1,0:T(8,128)(2,1)S(1)} collective-permute-done((bf16[240,960]{1,0:T(8,128)(2,1)S(1)}, bf16[240,960]{1,0:T(8,128)(2,1)S(1)}, u32[]{:S(2)}, u32[]{:S(2)}) %collective-permute-start.35) | collective-permute-done | bytes 460832 | tf_op jit(solution)/shard_map/ppermute | solution.py:81
  255.4 14.2 %all-to-all-done.2 = bf16[4,32,2688]{2,1,0:T(8,128)(2,1)S(1)} async-done(((bf16[4,32,2688]{2,1,0:T(8,128)(2,1)}), bf16[4,32,2688]{2,1,0:T(8,128)(2,1)S(1)}, u32[]{:S(2)}, u32[]{:S(2)}) %all-to-all-start.2) | async-done | bytes 688160 | tf_op jit(solution)/shard_map/all_to_all | solution.py:141
  279.7 5.2 %collective-permute-done.37 = bf16[128,2688]{1,0:T(8,128)(2,1)S(1)} collective-permute-done((bf16[128,2688]{1,0:T(8,128)(2,1)S(1)}, bf16[128,2688]{1,0:T(8,128)(2,1)S(1)}, u32[]{:S(2)}, u32[]{:S(2)}) %collective-permute-start.37) | collective-permute-done | bytes 688160 | tf_op jit(solution)/shard_map/ppermute | solution.py:81
  (335 shorter events, 134.4 us)
Async XLA Ops:
  2.5 19.0 %collective-permute-start = (bf16[96,960]{1,0:T(8,128)(2,1)}, bf16[96,960]{1,0:T(8,128)(2,1)}, u32[]{:S(2)}, u32[]{:S(2)}) collective-permute-start(bf16[96,960]{1,0:T(8,128)(2,1)} %get-tuple-element.213), channel_id=1, source_target_pairs={{0,2},{1,3},{2,0},{3,1},{4,6},{5,7},{6,4},{7,5},{8,10},{9,11},{10,... | collective-permute-start | bytes 552968 | tf_op jit(solution)/shard_map/ppermute | solution.py:81
  12.4 30.1 %collective-permute-start.5 = (bf16[240,2624]{1,0:T(8,128)(2,1)}, bf16[240,2624]{1,0:T(8,128)(2,1)}, u32[]{:S(2)}, u32[]{:S(2)}) collective-permute-start(bf16[240,2624]{1,0:T(8,128)(2,1)} %concatenate.146), channel_id=1, source_target_pairs={{0,16},{8,24},{16,0},{24,8},{1,17},{9,25},{17,1},{25,9},{2,18},{10... | collective-permute-start | bytes 3778568 | tf_op jit(solution)/shard_map/ppermute | solution.py:81
  13.8 43.3 %collective-permute-start.6 = (bf16[240,2624]{1,0:T(8,128)(2,1)}, bf16[240,2624]{1,0:T(8,128)(2,1)}, u32[]{:S(2)}, u32[]{:S(2)}) collective-permute-start(bf16[240,2624]{1,0:T(8,128)(2,1)} %concatenate.146), channel_id=1, source_target_pairs={{0,8},{8,0},{16,24},{24,16},{1,9},{9,1},{17,25},{25,17},{2,10},{10... | collective-permute-start | bytes 3778568 | tf_op jit(solution)/shard_map/ppermute | solution.py:81
  15.9 37.3 %collective-permute-start.11 = (bf16[240,1920]{1,0:T(8,128)(2,1)}, bf16[240,1920]{1,0:T(8,128)(2,1)}, u32[]{:S(2)}, u32[]{:S(2)}) collective-permute-start(bf16[240,1920]{1,0:T(8,128)(2,1)} %pad_maximum_fusion.5), channel_id=1, source_target_pairs={{0,8},{8,0},{16,24},{24,16},{1,9},{9,1},{17,25},{25,17},{2,10},{10... | collective-permute-start | bytes 2764808 | tf_op jit(solution)/shard_map/ppermute | solution.py:81
  42.5 14.6 %collective-permute-start.7 = (bf16[240,2624]{1,0:T(8,128)(2,1)}, bf16[240,2624]{1,0:T(8,128)(2,1)S(1)}, u32[]{:S(2)}, u32[]{:S(2)}) collective-permute-start(bf16[240,2624]{1,0:T(8,128)(2,1)} %collective-permute-done.5), channel_id=1, source_target_pairs={{0,8},{8,0},{16,24},{24,16},{1,9},{9,1},{17,25},{25,17},{2,10},{10... | collective-permute-start | bytes 3778568 | tf_op jit(solution)/shard_map/ppermute | solution.py:81
  51.0 19.9 %collective-permute-start.9 = (bf16[2,96,960]{2,1,0:T(8,128)(2,1)}, bf16[2,96,960]{2,1,0:T(8,128)(2,1)S(1)}, u32[]{:S(2)}, u32[]{:S(2)}) collective-permute-start(bf16[2,96,960]{2,1,0:T(8,128)(2,1)} %maximum_select_fusion.1), channel_id=1, source_target_pairs={{0,3},{1,0},{2,1},{3,2},{4,7},{5,4},{6,5},{7,6},{8,11},{9,8},{10,9... | collective-permute-start | bytes 1105928 | tf_op jit(solution)/shard_map/ppermute | solution.py:109
  51.0 19.9 %collective-permute-start.8 = (bf16[2,96,960]{2,1,0:T(8,128)(2,1)}, bf16[2,96,960]{2,1,0:T(8,128)(2,1)S(1)}, u32[]{:S(2)}, u32[]{:S(2)}) collective-permute-start(bf16[2,96,960]{2,1,0:T(8,128)(2,1)} %collective-permute-done.4), channel_id=1, source_target_pairs={{0,1},{1,2},{2,3},{3,0},{4,5},{5,6},{6,7},{7,4},{8,9},{9,10},{10,1... | collective-permute-start | bytes 1105928 | tf_op jit(solution)/shard_map/ppermute | solution.py:109
  60.4 18.3 %collective-permute-start.10 = (bf16[240,1920]{1,0:T(8,128)(2,1)}, bf16[240,1920]{1,0:T(8,128)(2,1)S(1)}, u32[]{:S(2)}, u32[]{:S(2)}) collective-permute-start(bf16[240,1920]{1,0:T(8,128)(2,1)} %pad_maximum_fusion.5), channel_id=1, source_target_pairs={{0,16},{8,24},{16,0},{24,8},{1,17},{9,25},{17,1},{25,9},{2,18},{10... | collective-permute-start | bytes 2764808 | tf_op jit(solution)/shard_map/ppermute | solution.py:81
  81.0 14.0 %collective-permute-start.14 = (bf16[192,960]{1,0:T(8,128)(2,1)S(1)}, bf16[192,960]{1,0:T(8,128)(2,1)S(1)}, u32[]{:S(2)}, u32[]{:S(2)}) collective-permute-start(bf16[192,960]{1,0:T(8,128)(2,1)S(1)} %collective-permute-done.13), channel_id=1, source_target_pairs={{0,1},{1,2},{2,3},{3,0},{4,5},{5,6},{6,7},{7,4},{8,9},{9,10},{10,1... | collective-permute-start | bytes 1105928 | tf_op jit(solution)/shard_map/ppermute | solution.py:109
  84.7 18.7 %collective-permute-start.16 = (bf16[192,960]{1,0:T(8,128)(2,1)S(1)}, bf16[192,960]{1,0:T(8,128)(2,1)S(1)}, u32[]{:S(2)}, u32[]{:S(2)}) collective-permute-start(bf16[192,960]{1,0:T(8,128)(2,1)S(1)} %convolution_convert_fusion.8), channel_id=1, source_target_pairs={{0,1},{1,2},{2,3},{3,0},{4,5},{5,6},{6,7},{7,4},{8,9},{9,10},{10,1... | collective-permute-start | bytes 1105928 | tf_op jit(solution)/shard_map/ppermute | solution.py:109
  95.0 16.9 %collective-permute-start.15 = (bf16[192,960]{1,0:T(8,128)(2,1)S(1)}, bf16[192,960]{1,0:T(8,128)(2,1)S(1)}, u32[]{:S(2)}, u32[]{:S(2)}) collective-permute-start(bf16[192,960]{1,0:T(8,128)(2,1)S(1)} %collective-permute-done.14), channel_id=1, source_target_pairs={{0,1},{1,2},{2,3},{3,0},{4,5},{5,6},{6,7},{7,4},{8,9},{9,10},{10,1... | collective-permute-start | bytes 1105928 | tf_op jit(solution)/shard_map/ppermute | solution.py:109
  104.3 15.5 %collective-permute-start.17 = (bf16[192,960]{1,0:T(8,128)(2,1)S(1)}, bf16[192,960]{1,0:T(8,128)(2,1)S(1)}, u32[]{:S(2)}, u32[]{:S(2)}) collective-permute-start(bf16[192,960]{1,0:T(8,128)(2,1)S(1)} %fusion.36), channel_id=1, source_target_pairs={{0,1},{1,2},{2,3},{3,0},{4,5},{5,6},{6,7},{7,4},{8,9},{9,10},{10,1... | collective-permute-start | bytes 1105928 | tf_op jit(solution)/shard_map/ppermute | solution.py:109
  140.5 15.1 %collective-permute-start.22 = (bf16[480,1920]{1,0:T(8,128)(2,1)S(1)}, bf16[480,1920]{1,0:T(8,128)(2,1)S(1)}, u32[]{:S(2)}, u32[]{:S(2)}) collective-permute-start(bf16[480,1920]{1,0:T(8,128)(2,1)S(1)} %get-tuple-element.150), channel_id=1, source_target_pairs={{0,8},{8,0},{16,24},{24,16},{1,9},{9,1},{17,25},{25,17},{2,10},{10... | collective-permute-start | bytes 5529608 | tf_op jit(solution)/shard_map/ppermute | solution.py:81
  167.0 13.7 %collective-permute-start.25 = (bf16[384,640]{1,0:T(8,128)(2,1)S(1)}, bf16[384,640]{1,0:T(8,128)(2,1)S(1)}, u32[]{:S(2)}, u32[]{:S(2)}) collective-permute-start(bf16[384,640]{1,0:T(8,128)(2,1)S(1)} %get-tuple-element.151), channel_id=1, source_target_pairs={{0,4},{4,0},{1,5},{5,1},{2,6},{6,2},{3,7},{7,3},{8,12},{12,8},{9,1... | collective-permute-start | bytes 1474568 | tf_op jit(solution)/shard_map/ppermute | solution.py:81
  168.2 14.1 %collective-permute-start.28 = (bf16[192,960]{1,0:T(8,128)(2,1)S(1)}, bf16[192,960]{1,0:T(8,128)(2,1)S(1)}, u32[]{:S(2)}, u32[]{:S(2)}) collective-permute-start(bf16[192,960]{1,0:T(8,128)(2,1)S(1)} %fusion.33), channel_id=1, source_target_pairs={{0,1},{1,2},{2,3},{3,0},{4,5},{5,6},{6,7},{7,4},{8,9},{9,10},{10,1... | collective-permute-start | bytes 1105928 | tf_op jit(solution)/shard_map/ppermute | solution.py:109
  171.6 32.3 %collective-permute-start.24 = (bf16[240,1664]{1,0:T(8,128)(2,1)}, bf16[240,1664]{1,0:T(8,128)(2,1)}, u32[]{:S(2)}, u32[]{:S(2)}) collective-permute-start(bf16[240,1664]{1,0:T(8,128)(2,1)} %slice.450), channel_id=1, source_target_pairs={{0,16},{8,24},{16,0},{24,8},{1,17},{9,25},{17,1},{25,9},{2,18},{10... | collective-permute-start | bytes 2396168 | tf_op jit(solution)/shard_map/ppermute | solution.py:81
  181.7 15.3 %collective-permute-start.26 = (bf16[192,640]{1,0:T(8,128)(2,1)}, bf16[192,640]{1,0:T(8,128)(2,1)}, u32[]{:S(2)}, u32[]{:S(2)}) collective-permute-start(bf16[192,640]{1,0:T(8,128)(2,1)} %slice.452), channel_id=1, source_target_pairs={{0,1},{1,0},{2,3},{3,2},{4,5},{5,4},{6,7},{7,6},{8,9},{9,8},{10,11... | collective-permute-start | bytes 737288 | tf_op jit(solution)/shard_map/ppermute | solution.py:81
  183.2 22.2 %collective-permute-start.29 = (bf16[192,960]{1,0:T(8,128)(2,1)}, bf16[192,960]{1,0:T(8,128)(2,1)}, u32[]{:S(2)}, u32[]{:S(2)}) collective-permute-start(bf16[192,960]{1,0:T(8,128)(2,1)} %add.313), channel_id=1, source_target_pairs={{0,1},{1,2},{2,3},{3,0},{4,5},{5,6},{6,7},{7,4},{8,9},{9,10},{10,1... | collective-permute-start | bytes 1105928 | tf_op jit(solution)/shard_map/ppermute | solution.py:109
  211.5 13.6 %collective-permute-start.33 = (bf16[240,960]{1,0:T(8,128)(2,1)}, bf16[240,960]{1,0:T(8,128)(2,1)}, u32[]{:S(2)}, u32[]{:S(2)}) collective-permute-start(bf16[240,960]{1,0:T(8,128)(2,1)} %slice_add_fusion.4), channel_id=1, source_target_pairs={{0,16},{8,24},{16,0},{24,8},{1,17},{9,25},{17,1},{25,9},{2,18},{10... | collective-permute-start | bytes 1382408 | tf_op jit(solution)/shard_map/ppermute | solution.py:81
  220.3 18.1 %all-to-all-start.1 = ((bf16[4,32,1664]{2,1,0:T(8,128)(2,1)}), bf16[4,32,1664]{2,1,0:T(8,128)(2,1)S(1)}, u32[]{:S(2)}, u32[]{:S(2)}) async-start(bf16[4,32,1664]{2,1,0:T(8,128)(2,1)} %bitcast.14), calls=%async_computation.1 | async-start | bytes 851968 | tf_op jit(solution)/shard_map/all_to_all | solution.py:132
  239.5 30.1 %all-to-all-start.2 = ((bf16[4,32,2688]{2,1,0:T(8,128)(2,1)}), bf16[4,32,2688]{2,1,0:T(8,128)(2,1)S(1)}, u32[]{:S(2)}, u32[]{:S(2)}) async-start(bf16[4,32,2688]{2,1,0:T(8,128)(2,1)} %broadcast_in_dim.16), calls=%async_computation.2 | async-start | bytes 1376256 | tf_op jit(solution)/shard_map/all_to_all | solution.py:141
  244.4 29.5 %collective-permute-start.30 = (bf16[96,960]{1,0:T(8,128)(2,1)}, bf16[96,960]{1,0:T(8,128)(2,1)}, u32[]{:S(2)}, u32[]{:S(2)}) collective-permute-start(bf16[96,960]{1,0:T(8,128)(2,1)} %get-tuple-element.182), channel_id=1, source_target_pairs={{0,2},{1,3},{2,0},{3,1},{4,6},{5,7},{6,4},{7,5},{8,10},{9,11},{10,... | collective-permute-start | bytes 552968 | tf_op jit(solution)/shard_map/ppermute | solution.py:81
  248.1 29.0 %collective-permute-start.36 = (bf16[96,960]{1,0:T(8,128)(2,1)}, bf16[96,960]{1,0:T(8,128)(2,1)}, u32[]{:S(2)}, u32[]{:S(2)}) collective-permute-start(bf16[96,960]{1,0:T(8,128)(2,1)} %get-tuple-element.178), channel_id=1, source_target_pairs={{0,2},{1,3},{2,0},{3,1},{4,6},{5,7},{6,4},{7,5},{8,10},{9,11},{10,... | collective-permute-start | bytes 552968 | tf_op jit(solution)/shard_map/ppermute | solution.py:81
  269.6 15.3 %collective-permute-start.37 = (bf16[128,2688]{1,0:T(8,128)(2,1)S(1)}, bf16[128,2688]{1,0:T(8,128)(2,1)S(1)}, u32[]{:S(2)}, u32[]{:S(2)}) collective-permute-start(bf16[128,2688]{1,0:T(8,128)(2,1)S(1)} %bitcast.71), channel_id=1, source_target_pairs={{0,4},{4,0},{1,5},{5,1},{2,6},{6,2},{3,7},{7,3},{8,12},{12,8},{9,1... | collective-permute-start | bytes 2064392 | tf_op jit(solution)/shard_map/ppermute | solution.py:81
  (75 other events, 876.2 us)

commit v4 on v2

--- a/solution.py
+++ b/solution.py
@@ -358,12 +358,12 @@
     cots.append(shift(cots[0], 1))
     cots = [after(cots[0], cots[1]), cots[1], shift(cots[1], 1)]
     cots.append(shift(cots[0], -1))
-    all_tokens = after(all_tokens, cots[1])
 
     all_float = all_tokens.astype(jnp.float32)
     all_scale = rms_scale(all_float)
-    all_normed = (all_float * all_scale).astype(jnp.bfloat16)
-    tokens_f, scale_a = all_float[:rows], all_scale[:rows]
+    all_normed = after((all_float * all_scale).astype(jnp.bfloat16), cots[1])
+    tokens_f = own.astype(jnp.float32)
+    scale_a = rms_scale(tokens_f)
     mix, log_total, query_rot, key_rot, value, hidden, normed_m = attend(
         own, all_normed, first_weight, key_table, query_pos, key_pos, kv_cols, w_query.shape[1]
     )

time: 288 us -> 287 us (level)
  waiting for transfers between devices: 120 us -> 114 us
  starting transfers between devices: 37 us -> 42.3 us
  other arithmetic: 47.4 us -> 43.1 us
    ppermute x26, starting transfers between devices: 19.7 us -> 25 us  [swap(): return lax.ppermute(value, axis, [(i, i ^ bit) for i in range(size)])]
    ppermute x26, waiting for transfers between devices: 60.1 us -> 56.4 us  [swap(): return lax.ppermute(value, axis, [(i, i ^ bit) for i in range(size)])]
    convert_element_type x2 -> x1, other arithmetic: 3.84 us -> 0.32 us  [body(): all_normed = after((all_float * all_scale).astype(jnp.bfloat16), cots[1])]
    unnamed x124 -> x132, local copies, waits for them, and re-layouts: 6.63 us -> 8.53 us
  transfers between devices with their start and end apart: 41 -> 41, of which waited for: 25 -> 27; matrix products, arithmetic and copies ran while one was open for 30% -> 30% of each run, Pallas kernels for 7% -> 7%
where the time goes in v4:
time: 287 us; the launch traced here: 281 us
  waiting for transfers between devices  114 us (40%)
  other arithmetic  43.1 us (15%)
  starting transfers between devices  42.3 us (15%)
  local copies, waits for them, and re-layouts  31.8 us (11%)
  matrix products  25.9 us (9%)
  Pallas kernels  21.7 us (8%)
    ppermute x26, waiting for transfers between devices, swap(): return lax.ppermute(value, axis, [(i, i ^ bit) for i in range(size)])  56.4 us
    ppermute x12, waiting for transfers between devices, shift(): lax.ppermute(value, 'tensor', [(i, (i + count) % size) for i in range(siz...  40.6 us
    ppermute x26, starting transfers between devices, swap(): return lax.ppermute(value, axis, [(i, i ^ bit) for i in range(size)])  25 us
    all_to_all x1, waiting for transfers between devices, group_collect(): lax.all_to_all(spread, 'tensor', split_axis=0, concat_axis=0, tiled=True)  14.1 us
    dot_general x10, matrix products, dot_rows(): lax.dot_general(left, right, (((1,), (1,)), ((), ())), preferred_element_...  12.8 us
    pallas_call x1, Pallas kernels, attend_back(): pl.pallas_call(attend_back_kernel, out_shape=jax.ShapeDtypeStruct((keys,...  10.1 us
    pallas_call x1, Pallas kernels, attend(): pl.pallas_call(attend_kernel, out_shape=(jax.ShapeDtypeStruct((rows, q_co...  9.8 us
    unnamed x132, local copies, waits for them, and re-layouts  8.53 us
  transfers between devices with their start and end apart: 41, of which 27 were waited for; matrix products, arithmetic and copies ran while one was open for 30% of the time, Pallas kernels for 7%

profile of v4, /device:TPU:0, one launch (start us, length us, event | category | flops | bytes accessed | tf_op | source)
XLA Modules:
  0.0 281.4 jit_solution(7843818087853628251)
XLA Ops:
  2.5 4.0 %collective-permute-start = (bf16[96,960]{1,0:T(8,128)(2,1)}, bf16[96,960]{1,0:T(8,128)(2,1)}, u32[]{:S(2)}, u32[]{:S(2)}) collective-permute-start(bf16[96,960]{1,0:T(8,128)(2,1)} %get-tuple-element.215), channel_id=1, source_target_pairs={{0,2},{1,3},{2,0},{3,1},{4,6},{5,7},{6,4},{7,5},{8,10},{9,11},{10,... | collective-permute-start | bytes 552968 | tf_op jit(solution)/shard_map/ppermute | solution.py:81
  29.1 5.8 %collective-permute-done.1 = bf16[192,960]{1,0:T(8,128)(2,1)} collective-permute-done((bf16[192,960]{1,0:T(8,128)(2,1)S(1)}, bf16[192,960]{1,0:T(8,128)(2,1)}, u32[]{:S(2)}, u32[]{:S(2)}) %collective-permute-start.1) | collective-permute-done | bytes 368672 | tf_op jit(solution)/shard_map/ppermute | solution.py:81
  47.0 5.6 %collective-permute-done.4 = bf16[2,96,960]{2,1,0:T(8,128)(2,1)S(1)} collective-permute-done((bf16[2,96,960]{2,1,0:T(8,128)(2,1)}, bf16[2,96,960]{2,1,0:T(8,128)(2,1)S(1)}, u32[]{:S(2)}, u32[]{:S(2)}) %collective-permute-start.4) | collective-permute-done | bytes 368672 | tf_op jit(solution)/shard_map/ppermute | solution.py:109
  58.2 3.2 %pad_maximum_fusion.w_ref = bf16[960,2624]{1,0:T(8,128)(2,1)S(1)} fusion(bf16[240,2624]{1,0:T(8,128)(2,1)S(1)} %collective-permute-done.7, bf16[240,2624]{1,0:T(8,128)(2,1)} %collective-permute-done.6, bf16[240,2624]{1,0:T(8,128)(2,1)} %collective-permute-done.5, bf16[240,2624]{1,0:T(8,128)(2,1)} %concatenate.146), kind=kLoop, calls=%fused_computation.1 | loop fusion | flops 20152320 | bytes 10076160 | tf_op jit(solution)/shard_map/concatenate | solution.py:354
  62.0 9.8 %attend.1 = (bf16[192,960]{1,0:T(8,128)(2,1)S(1)}, f32[576,8]{1,0:T(8,128)S(1)}, bf16[192,960]{1,0:T(8,128)(2,1)S(1)}, bf16[768,320]{1,0:T(8,128)(2,1)S(1)}, bf1...) custom-call(bf16[192,960]{1,0:T(8,128)(2,1)S(1)} %pad_maximum_fusion.10.x_ref, ...), custom_call_target="tpu_custom_call" | custom-call | flops 1509949440 | bytes 10000000 | tf_op jit(solution)/shard_map/attend/pallas_call | solution.py:229
  72.3 7.3 %collective-permute-done.10 = bf16[240,1920]{1,0:T(8,128)(2,1)S(1)} collective-permute-done((bf16[240,1920]{1,0:T(8,128)(2,1)}, bf16[240,1920]{1,0:T(8,128)(2,1)S(1)}, u32[]{:S(2)}, u32[]{:S(2)}) %collective-permute-start.10) | collective-permute-done | bytes 921632 | tf_op jit(solution)/shard_map/ppermute | solution.py:81
  86.6 8.9 %collective-permute-done.14 = bf16[192,960]{1,0:T(8,128)(2,1)S(1)} collective-permute-done((bf16[192,960]{1,0:T(8,128)(2,1)S(1)}, bf16[192,960]{1,0:T(8,128)(2,1)S(1)}, u32[]{:S(2)}, u32[]{:S(2)}) %collective-permute-start.14) | collective-permute-done | bytes 368672 | tf_op jit(solution)/shard_map/ppermute | solution.py:109
  97.4 6.4 %collective-permute-done.16 = bf16[192,960]{1,0:T(8,128)(2,1)S(1)} collective-permute-done((bf16[192,960]{1,0:T(8,128)(2,1)S(1)}, bf16[192,960]{1,0:T(8,128)(2,1)S(1)}, u32[]{:S(2)}, u32[]{:S(2)}) %collective-permute-start.16) | collective-permute-done | bytes 368672 | tf_op jit(solution)/shard_map/ppermute | solution.py:109
  104.8 7.4 %collective-permute-done.15 = bf16[192,960]{1,0:T(8,128)(2,1)S(1)} collective-permute-done((bf16[192,960]{1,0:T(8,128)(2,1)S(1)}, bf16[192,960]{1,0:T(8,128)(2,1)S(1)}, u32[]{:S(2)}, u32[]{:S(2)}) %collective-permute-start.15) | collective-permute-done | bytes 368672 | tf_op jit(solution)/shard_map/ppermute | solution.py:109
  113.6 5.9 %collective-permute-done.17 = bf16[192,960]{1,0:T(8,128)(2,1)S(1)} collective-permute-done((bf16[192,960]{1,0:T(8,128)(2,1)S(1)}, bf16[192,960]{1,0:T(8,128)(2,1)S(1)}, u32[]{:S(2)}, u32[]{:S(2)}) %collective-permute-start.17) | collective-permute-done | bytes 368672 | tf_op jit(solution)/shard_map/ppermute | solution.py:109
  124.0 4.5 %pad_maximum_fusion.2 = (bf16[480,1920]{1,0:T(8,128)(2,1)}, bf16[480,1920]{1,0:T(8,128)(2,1)S(1)}) fusion(bf16[960,640]{1,0:T(8,128)(2,1)S(1)} %convolution_convert_fusion.2, bf16[960,1280]{1,0:T(8,128)(2,1)S(1)} %convolution_convert_fusion), kind=kLoop, calls=%fused_computation.24 | loop fusion | flops 7372800 | bytes 7372800 | tf_op jit(solution)/shard_map/concatenate | solution.py:409
  128.6 3.7 %collective-permute-done.18 = bf16[192,960]{1,0:T(8,128)(2,1)S(1)} collective-permute-done((bf16[192,960]{1,0:T(8,128)(2,1)S(1)}, bf16[192,960]{1,0:T(8,128)(2,1)S(1)}, u32[]{:S(2)}, u32[]{:S(2)}) %collective-permute-start.18) | collective-permute-done | bytes 368672 | tf_op jit(solution)/shard_map/ppermute | solution.py:109
  136.1 10.1 %attend_back.1 = bf16[768,1664]{1,0:T(8,128)(2,1)S(1)} custom-call(bf16[192,960]{1,0:T(8,128)(2,1)S(1)} %get-tuple-element.83.q_ref, bf16[768,320]{1,0:T(8,128)(2,1)S(1)} %get-tuple-element.84.k_ref, bf16[768,320]{1,0:T(8,128)(2,1)S(1)} %get-tuple-element.85.v_ref, bf16[192,960]{1,0:T(8,128)(2,1)S(1)} %get-tuple-element.81.mix_ref, ...), custom_call_target="tpu_custom_call" | custom-call | flops 1415577600 | bytes 6000000 | tf_op jit(solution)/shard_map/attend_back/pallas_call | solution.py:287
  149.2 3.2 %add_convert_fusion = bf16[960,1664]{1,0:T(8,128)(2,1)S(1)} fusion(bf16[768,960]{1,0:T(8,128)(2,1)S(1)} %fusion.1.n_ref, bf16[768,1664]{1,0:T(8,128)(2,1)S(1)} %attend_back.1, f32[1664]{0:T(1024)S(1)} %fusion.76, f32[960]{0:T(1024)S(1)} %get-tuple-element.127), kind=kOutput, calls=%fused_computation | convolution fusion | flops 2458460160 | bytes 7235840 | tf_op jit(solution)/shard_map/dot_general | solution.py:31
  166.4 7.0 %collective-permute-done.24 = bf16[384,640]{1,0:T(8,128)(2,1)S(1)} collective-permute-done((bf16[384,640]{1,0:T(8,128)(2,1)S(1)}, bf16[384,640]{1,0:T(8,128)(2,1)S(1)}, u32[]{:S(2)}, u32[]{:S(2)}) %collective-permute-start.24) | collective-permute-done | bytes 491552 | tf_op jit(solution)/shard_map/ppermute | solution.py:81
  183.4 3.5 %all-to-all-start = ((bf16[4,32,960]{2,1,0:T(8,128)(2,1)}), bf16[4,32,960]{2,1,0:T(8,128)(2,1)S(1)}, u32[]{:S(2)}, u32[]{:S(2)}) async-start(bf16[4,32,960]{2,1,0:T(8,128)(2,1)} %bitcast.13), calls=%async_computation | async-start | bytes 524288 | tf_op jit(solution)/shard_map/all_to_all | solution.py:132
  198.6 3.2 %collective-permute-done.32 = bf16[240,960]{1,0:T(8,128)(2,1)} collective-permute-done((bf16[240,960]{1,0:T(8,128)(2,1)}, bf16[240,960]{1,0:T(8,128)(2,1)}, u32[]{:S(2)}, u32[]{:S(2)}) %collective-permute-start.32) | collective-permute-done | bytes 460832 | tf_op jit(solution)/shard_map/ppermute | solution.py:81
  213.0 4.8 %all-to-all-start.1 = ((bf16[4,32,1664]{2,1,0:T(8,128)(2,1)}), bf16[4,32,1664]{2,1,0:T(8,128)(2,1)S(1)}, u32[]{:S(2)}, u32[]{:S(2)}) async-start(bf16[4,32,1664]{2,1,0:T(8,128)(2,1)} %bitcast.14), calls=%async_computation.1 | async-start | bytes 851968 | tf_op jit(solution)/shard_map/all_to_all | solution.py:132
  217.8 5.2 %collective-permute-done.34 = bf16[240,960]{1,0:T(8,128)(2,1)S(1)} collective-permute-done((bf16[240,960]{1,0:T(8,128)(2,1)S(1)}, bf16[240,960]{1,0:T(8,128)(2,1)S(1)}, u32[]{:S(2)}, u32[]{:S(2)}) %collective-permute-start.34) | collective-permute-done | bytes 460832 | tf_op jit(solution)/shard_map/ppermute | solution.py:81
  231.1 3.7 %all-to-all-start.2 = ((bf16[4,32,2688]{2,1,0:T(8,128)(2,1)}), bf16[4,32,2688]{2,1,0:T(8,128)(2,1)S(1)}, u32[]{:S(2)}, u32[]{:S(2)}) async-start(bf16[4,32,2688]{2,1,0:T(8,128)(2,1)} %broadcast_in_dim.16), calls=%async_computation.2 | async-start | bytes 1376256 | tf_op jit(solution)/shard_map/all_to_all | solution.py:141
  240.6 5.9 %collective-permute-done.35 = bf16[240,960]{1,0:T(8,128)(2,1)S(1)} collective-permute-done((bf16[240,960]{1,0:T(8,128)(2,1)S(1)}, bf16[240,960]{1,0:T(8,128)(2,1)S(1)}, u32[]{:S(2)}, u32[]{:S(2)}) %collective-permute-start.35) | collective-permute-done | bytes 460832 | tf_op jit(solution)/shard_map/ppermute | solution.py:81
  246.9 14.1 %all-to-all-done.2 = bf16[4,32,2688]{2,1,0:T(8,128)(2,1)S(1)} async-done(((bf16[4,32,2688]{2,1,0:T(8,128)(2,1)}), bf16[4,32,2688]{2,1,0:T(8,128)(2,1)S(1)}, u32[]{:S(2)}, u32[]{:S(2)}) %all-to-all-start.2) | async-done | bytes 688160 | tf_op jit(solution)/shard_map/all_to_all | solution.py:141
  265.3 3.2 %collective-permute-done.36 = bf16[96,960]{1,0:T(8,128)(2,1)} collective-permute-done((bf16[96,960]{1,0:T(8,128)(2,1)}, bf16[96,960]{1,0:T(8,128)(2,1)}, u32[]{:S(2)}, u32[]{:S(2)}) %collective-permute-start.36) | collective-permute-done | bytes 184352 | tf_op jit(solution)/shard_map/ppermute | solution.py:81
  271.1 5.2 %collective-permute-done.37 = bf16[128,2688]{1,0:T(8,128)(2,1)S(1)} collective-permute-done((bf16[128,2688]{1,0:T(8,128)(2,1)S(1)}, bf16[128,2688]{1,0:T(8,128)(2,1)S(1)}, u32[]{:S(2)}, u32[]{:S(2)}) %collective-permute-start.37) | collective-permute-done | bytes 688160 | tf_op jit(solution)/shard_map/ppermute | solution.py:81
  (343 shorter events, 136.8 us)
Async XLA Ops:
  2.5 19.6 %collective-permute-start = (bf16[96,960]{1,0:T(8,128)(2,1)}, bf16[96,960]{1,0:T(8,128)(2,1)}, u32[]{:S(2)}, u32[]{:S(2)}) collective-permute-start(bf16[96,960]{1,0:T(8,128)(2,1)} %get-tuple-element.215), channel_id=1, source_target_pairs={{0,2},{1,3},{2,0},{3,1},{4,6},{5,7},{6,4},{7,5},{8,10},{9,11},{10,... | collective-permute-start | bytes 552968 | tf_op jit(solution)/shard_map/ppermute | solution.py:81
  12.4 30.1 %collective-permute-start.5 = (bf16[240,2624]{1,0:T(8,128)(2,1)}, bf16[240,2624]{1,0:T(8,128)(2,1)}, u32[]{:S(2)}, u32[]{:S(2)}) collective-permute-start(bf16[240,2624]{1,0:T(8,128)(2,1)} %concatenate.146), channel_id=1, source_target_pairs={{0,16},{8,24},{16,0},{24,8},{1,17},{9,25},{17,1},{25,9},{2,18},{10... | collective-permute-start | bytes 3778568 | tf_op jit(solution)/shard_map/ppermute | solution.py:81
  13.9 44.3 %collective-permute-start.6 = (bf16[240,2624]{1,0:T(8,128)(2,1)}, bf16[240,2624]{1,0:T(8,128)(2,1)}, u32[]{:S(2)}, u32[]{:S(2)}) collective-permute-start(bf16[240,2624]{1,0:T(8,128)(2,1)} %concatenate.146), channel_id=1, source_target_pairs={{0,8},{8,0},{16,24},{24,16},{1,9},{9,1},{17,25},{25,17},{2,10},{10... | collective-permute-start | bytes 3778568 | tf_op jit(solution)/shard_map/ppermute | solution.py:81
  15.9 38.9 %collective-permute-start.11 = (bf16[240,1920]{1,0:T(8,128)(2,1)}, bf16[240,1920]{1,0:T(8,128)(2,1)}, u32[]{:S(2)}, u32[]{:S(2)}) collective-permute-start(bf16[240,1920]{1,0:T(8,128)(2,1)} %pad_maximum_fusion.5), channel_id=1, source_target_pairs={{0,8},{8,0},{16,24},{24,16},{1,9},{9,1},{17,25},{25,17},{2,10},{10... | collective-permute-start | bytes 2764808 | tf_op jit(solution)/shard_map/ppermute | solution.py:81
  42.5 15.6 %collective-permute-start.7 = (bf16[240,2624]{1,0:T(8,128)(2,1)}, bf16[240,2624]{1,0:T(8,128)(2,1)S(1)}, u32[]{:S(2)}, u32[]{:S(2)}) collective-permute-start(bf16[240,2624]{1,0:T(8,128)(2,1)} %collective-permute-done.5), channel_id=1, source_target_pairs={{0,8},{8,0},{16,24},{24,16},{1,9},{9,1},{17,25},{25,17},{2,10},{10... | collective-permute-start | bytes 3778568 | tf_op jit(solution)/shard_map/ppermute | solution.py:81
  52.6 19.3 %collective-permute-start.9 = (bf16[2,96,960]{2,1,0:T(8,128)(2,1)}, bf16[2,96,960]{2,1,0:T(8,128)(2,1)S(1)}, u32[]{:S(2)}, u32[]{:S(2)}) collective-permute-start(bf16[2,96,960]{2,1,0:T(8,128)(2,1)} %maximum_select_fusion.1), channel_id=1, source_target_pairs={{0,3},{1,0},{2,1},{3,2},{4,7},{5,4},{6,5},{7,6},{8,11},{9,8},{10,9... | collective-permute-start | bytes 1105928 | tf_op jit(solution)/shard_map/ppermute | solution.py:109
  52.6 19.3 %collective-permute-start.8 = (bf16[2,96,960]{2,1,0:T(8,128)(2,1)S(1)}, bf16[2,96,960]{2,1,0:T(8,128)(2,1)S(1)}, u32[]{:S(2)}, u32[]{:S(2)}) collective-permute-start(bf16[2,96,960]{2,1,0:T(8,128)(2,1)S(1)} %collective-permute-done.4), channel_id=1, source_target_pairs={{0,1},{1,2},{2,3},{3,0},{4,5},{5,6},{6,7},{7,4},{8,9},{9,10},{10,1... | collective-permute-start | bytes 1105928 | tf_op jit(solution)/shard_map/ppermute | solution.py:109
  61.4 18.2 %collective-permute-start.10 = (bf16[240,1920]{1,0:T(8,128)(2,1)}, bf16[240,1920]{1,0:T(8,128)(2,1)S(1)}, u32[]{:S(2)}, u32[]{:S(2)}) collective-permute-start(bf16[240,1920]{1,0:T(8,128)(2,1)} %pad_maximum_fusion.5), channel_id=1, source_target_pairs={{0,16},{8,24},{16,0},{24,8},{1,17},{9,25},{17,1},{25,9},{2,18},{10... | collective-permute-start | bytes 2764808 | tf_op jit(solution)/shard_map/ppermute | solution.py:81
  81.6 13.8 %collective-permute-start.14 = (bf16[192,960]{1,0:T(8,128)(2,1)S(1)}, bf16[192,960]{1,0:T(8,128)(2,1)S(1)}, u32[]{:S(2)}, u32[]{:S(2)}) collective-permute-start(bf16[192,960]{1,0:T(8,128)(2,1)S(1)} %collective-permute-done.13), channel_id=1, source_target_pairs={{0,1},{1,2},{2,3},{3,0},{4,5},{5,6},{6,7},{7,4},{8,9},{9,10},{10,1... | collective-permute-start | bytes 1105928 | tf_op jit(solution)/shard_map/ppermute | solution.py:109
  85.1 18.7 %collective-permute-start.16 = (bf16[192,960]{1,0:T(8,128)(2,1)S(1)}, bf16[192,960]{1,0:T(8,128)(2,1)S(1)}, u32[]{:S(2)}, u32[]{:S(2)}) collective-permute-start(bf16[192,960]{1,0:T(8,128)(2,1)S(1)} %convolution_convert_fusion.8), channel_id=1, source_target_pairs={{0,1},{1,2},{2,3},{3,0},{4,5},{5,6},{6,7},{7,4},{8,9},{9,10},{10,1... | collective-permute-start | bytes 1105928 | tf_op jit(solution)/shard_map/ppermute | solution.py:109
  95.4 16.9 %collective-permute-start.15 = (bf16[192,960]{1,0:T(8,128)(2,1)S(1)}, bf16[192,960]{1,0:T(8,128)(2,1)S(1)}, u32[]{:S(2)}, u32[]{:S(2)}) collective-permute-start(bf16[192,960]{1,0:T(8,128)(2,1)S(1)} %collective-permute-done.14), channel_id=1, source_target_pairs={{0,1},{1,2},{2,3},{3,0},{4,5},{5,6},{6,7},{7,4},{8,9},{9,10},{10,1... | collective-permute-start | bytes 1105928 | tf_op jit(solution)/shard_map/ppermute | solution.py:109
  104.7 14.8 %collective-permute-start.17 = (bf16[192,960]{1,0:T(8,128)(2,1)S(1)}, bf16[192,960]{1,0:T(8,128)(2,1)S(1)}, u32[]{:S(2)}, u32[]{:S(2)}) collective-permute-start(bf16[192,960]{1,0:T(8,128)(2,1)S(1)} %fusion.38), channel_id=1, source_target_pairs={{0,1},{1,2},{2,3},{3,0},{4,5},{5,6},{6,7},{7,4},{8,9},{9,10},{10,1... | collective-permute-start | bytes 1105928 | tf_op jit(solution)/shard_map/ppermute | solution.py:109
  128.6 20.7 %collective-permute-start.21 = (bf16[480,1920]{1,0:T(8,128)(2,1)S(1)}, bf16[480,1920]{1,0:T(8,128)(2,1)S(1)}, u32[]{:S(2)}, u32[]{:S(2)}) collective-permute-start(bf16[480,1920]{1,0:T(8,128)(2,1)S(1)} %get-tuple-element.150), channel_id=1, source_target_pairs={{0,8},{8,0},{16,24},{24,16},{1,9},{9,1},{17,25},{25,17},{2,10},{10... | collective-permute-start | bytes 5529608 | tf_op jit(solution)/shard_map/ppermute | solution.py:81
  160.9 14.1 %collective-permute-start.26 = (bf16[240,960]{1,0:T(8,128)(2,1)S(1)}, bf16[240,960]{1,0:T(8,128)(2,1)S(1)}, u32[]{:S(2)}, u32[]{:S(2)}) collective-permute-start(bf16[240,960]{1,0:T(8,128)(2,1)S(1)} %get-tuple-element.172), channel_id=1, source_target_pairs={{0,16},{8,24},{16,0},{24,8},{1,17},{9,25},{17,1},{25,9},{2,18},{10... | collective-permute-start | bytes 1382408 | tf_op jit(solution)/shard_map/ppermute | solution.py:81
  161.7 14.6 %collective-permute-start.28 = (bf16[192,960]{1,0:T(8,128)(2,1)S(1)}, bf16[192,960]{1,0:T(8,128)(2,1)S(1)}, u32[]{:S(2)}, u32[]{:S(2)}) collective-permute-start(bf16[192,960]{1,0:T(8,128)(2,1)S(1)} %fusion.35), channel_id=1, source_target_pairs={{0,1},{1,2},{2,3},{3,0},{4,5},{5,6},{6,7},{7,4},{8,9},{9,10},{10,1... | collective-permute-start | bytes 1105928 | tf_op jit(solution)/shard_map/ppermute | solution.py:109
  165.5 30.6 %collective-permute-start.23 = (bf16[240,1664]{1,0:T(8,128)(2,1)}, bf16[240,1664]{1,0:T(8,128)(2,1)}, u32[]{:S(2)}, u32[]{:S(2)}) collective-permute-start(bf16[240,1664]{1,0:T(8,128)(2,1)} %slice.439), channel_id=1, source_target_pairs={{0,16},{8,24},{16,0},{24,8},{1,17},{9,25},{17,1},{25,9},{2,18},{10... | collective-permute-start | bytes 2396168 | tf_op jit(solution)/shard_map/ppermute | solution.py:81
  174.3 17.1 %collective-permute-start.25 = (bf16[192,640]{1,0:T(8,128)(2,1)}, bf16[192,640]{1,0:T(8,128)(2,1)}, u32[]{:S(2)}, u32[]{:S(2)}) collective-permute-start(bf16[192,640]{1,0:T(8,128)(2,1)} %slice.441), channel_id=1, source_target_pairs={{0,1},{1,0},{2,3},{3,2},{4,5},{5,4},{6,7},{7,6},{8,9},{9,8},{10,11... | collective-permute-start | bytes 737288 | tf_op jit(solution)/shard_map/ppermute | solution.py:81
  177.2 20.3 %collective-permute-start.29 = (bf16[192,960]{1,0:T(8,128)(2,1)}, bf16[192,960]{1,0:T(8,128)(2,1)}, u32[]{:S(2)}, u32[]{:S(2)}) collective-permute-start(bf16[192,960]{1,0:T(8,128)(2,1)} %add.312), channel_id=1, source_target_pairs={{0,1},{1,2},{2,3},{3,0},{4,5},{5,6},{6,7},{7,4},{8,9},{9,10},{10,1... | collective-permute-start | bytes 1105928 | tf_op jit(solution)/shard_map/ppermute | solution.py:109
  203.9 13.9 %collective-permute-start.33 = (bf16[240,960]{1,0:T(8,128)(2,1)}, bf16[240,960]{1,0:T(8,128)(2,1)}, u32[]{:S(2)}, u32[]{:S(2)}) collective-permute-start(bf16[240,960]{1,0:T(8,128)(2,1)} %slice_add_fusion.3), channel_id=1, source_target_pairs={{0,16},{8,24},{16,0},{24,8},{1,17},{9,25},{17,1},{25,9},{2,18},{10... | collective-permute-start | bytes 1382408 | tf_op jit(solution)/shard_map/ppermute | solution.py:81
  213.0 17.0 %all-to-all-start.1 = ((bf16[4,32,1664]{2,1,0:T(8,128)(2,1)}), bf16[4,32,1664]{2,1,0:T(8,128)(2,1)S(1)}, u32[]{:S(2)}, u32[]{:S(2)}) async-start(bf16[4,32,1664]{2,1,0:T(8,128)(2,1)} %bitcast.14), calls=%async_computation.1 | async-start | bytes 851968 | tf_op jit(solution)/shard_map/all_to_all | solution.py:132
  231.1 29.9 %all-to-all-start.2 = ((bf16[4,32,2688]{2,1,0:T(8,128)(2,1)}), bf16[4,32,2688]{2,1,0:T(8,128)(2,1)S(1)}, u32[]{:S(2)}, u32[]{:S(2)}) async-start(bf16[4,32,2688]{2,1,0:T(8,128)(2,1)} %broadcast_in_dim.16), calls=%async_computation.2 | async-start | bytes 1376256 | tf_op jit(solution)/shard_map/all_to_all | solution.py:141
  237.0 28.3 %collective-permute-start.30 = (bf16[96,960]{1,0:T(8,128)(2,1)}, bf16[96,960]{1,0:T(8,128)(2,1)}, u32[]{:S(2)}, u32[]{:S(2)}) collective-permute-start(bf16[96,960]{1,0:T(8,128)(2,1)} %get-tuple-element.184), channel_id=1, source_target_pairs={{0,2},{1,3},{2,0},{3,1},{4,6},{5,7},{6,4},{7,5},{8,10},{9,11},{10,... | collective-permute-start | bytes 552968 | tf_op jit(solution)/shard_map/ppermute | solution.py:81
  240.6 27.9 %collective-permute-start.36 = (bf16[96,960]{1,0:T(8,128)(2,1)}, bf16[96,960]{1,0:T(8,128)(2,1)}, u32[]{:S(2)}, u32[]{:S(2)}) collective-permute-start(bf16[96,960]{1,0:T(8,128)(2,1)} %get-tuple-element.180), channel_id=1, source_target_pairs={{0,2},{1,3},{2,0},{3,1},{4,6},{5,7},{6,4},{7,5},{8,10},{9,11},{10,... | collective-permute-start | bytes 552968 | tf_op jit(solution)/shard_map/ppermute | solution.py:81
  261.0 15.3 %collective-permute-start.37 = (bf16[128,2688]{1,0:T(8,128)(2,1)S(1)}, bf16[128,2688]{1,0:T(8,128)(2,1)S(1)}, u32[]{:S(2)}, u32[]{:S(2)}) collective-permute-start(bf16[128,2688]{1,0:T(8,128)(2,1)S(1)} %bitcast.71), channel_id=1, source_target_pairs={{0,4},{4,0},{1,5},{5,1},{2,6},{6,2},{3,7},{7,3},{8,12},{12,8},{9,1... | collective-permute-start | bytes 2064392 | tf_op jit(solution)/shard_map/ppermute | solution.py:81
  (79 other events, 852.8 us)

commit v5 on v4

--- a/solution.py
+++ b/solution.py
@@ -427,11 +427,16 @@
     grads, out_term, total, mlp_beside = barrier((grads, out_term, total, mlp_beside))
 
     spot = (jnp.arange(grads.shape[1]) == attn_cols).astype(jnp.float32)
-    attn_term = dot_cols(all_normed, grads) + gain_m_term[:, None] * spot[None, :]
-    attn_term = scatter_rows(attn_term.astype(jnp.bfloat16), 0, 1)
-    attn_core = attn_term
+    half = all_normed.shape[1] // 2
+    sent, kept = [
+        (dot_cols(all_normed[:, part], grads) + gain_m_term[part, None] * spot[None, :]).astype(jnp.bfloat16)
+        for part in (slice(half, None), slice(half))
+    ]
+    arrived = swap(sent, "shard", 1)
+    attn_core = kept[half // 2 :] + arrived[half // 2 :]
     out_term = scatter_rows(out_term, 1, bits, attn_core)
-    attn_term = scatter_rows(attn_term, 1, bits)
+    attn_term = kept[: half // 2] + arrived[: half // 2] + swap(attn_core, "shard", 2)
+    attn_term = scatter_rows(attn_term, 2, bits)
     grad_query, grad_kv = grads[:rows, 2 * kv_cols : attn_cols], grads[:, : 2 * kv_cols]
     pair = after(grad_kv[: 2 * rows], attn_core) + swap(grad_kv[2 * rows :], "context", 1)
     own_kv = pair[:rows] + swap(pair[rows:], "tensor", 1)

time: 287 us -> 279 us (0.972)
  starting transfers between devices: 42.3 us -> 51 us
  local copies, waits for them, and re-layouts: 31.8 us -> 25.7 us
  waiting for transfers between devices: 114 us -> 109 us
  other arithmetic: 43.1 us -> 38.2 us
    ppermute x12, waiting for transfers between devices: 40.6 us -> 34.3 us  [shift(): lax.ppermute(value, 'tensor', [(i, (i + count) % size) for i in range(siz...]
    ppermute x26, starting transfers between devices: 25 us -> 29.7 us  [swap(): return lax.ppermute(value, axis, [(i, i ^ bit) for i in range(size)])]
    add x4 -> x2, other arithmetic: 4.18 us -> 0.28 us  [scatter_rows(): rows = kept + swap(rows[half:], 'shard', 1 << place)]
    unnamed x132 -> x96, local copies, waits for them, and re-layouts: 8.53 us -> 4.8 us
    ppermute x12, starting transfers between devices: 5.28 us -> 8.92 us  [shift(): lax.ppermute(value, 'tensor', [(i, (i + count) % size) for i in range(siz...]
    unnamed x9, other arithmetic: 3.66 us -> 0.59 us
    add x0 -> x2, other arithmetic: none -> 3 us  [the longest x1 1.82 us: body(): kept[:half // 2] + arrived[:half // 2] + swap(attn_core, 'shard', 2)]
    dot_general x4 -> x5, matrix products: 7.42 us -> 7.62 us  [dot_cols(): lax.dot_general(left, right, (((0,), (0,)), ((), ())), preferred_element_...]
  transfers between devices with their start and end apart: 41 -> 41, of which waited for: 27 -> 27; matrix products, arithmetic and copies ran while one was open for 30% -> 28% of each run, Pallas kernels for 7% -> 7%
where the time goes in v5:
time: 279 us; the launch traced here: 273 us
  waiting for transfers between devices  109 us (39%)
  starting transfers between devices  51 us (18%)
  other arithmetic  38.2 us (14%)
  local copies, waits for them, and re-layouts  25.7 us (9%)
  matrix products  24.8 us (9%)
  Pallas kernels  21.9 us (8%)
    ppermute x26, waiting for transfers between devices, swap(): return lax.ppermute(value, axis, [(i, i ^ bit) for i in range(size)])  56.5 us
    ppermute x12, waiting for transfers between devices, shift(): lax.ppermute(value, 'tensor', [(i, (i + count) % size) for i in range(siz...  34.3 us
    ppermute x26, starting transfers between devices, swap(): return lax.ppermute(value, axis, [(i, i ^ bit) for i in range(size)])  29.7 us
    all_to_all x1, waiting for transfers between devices, group_collect(): lax.all_to_all(spread, 'tensor', split_axis=0, concat_axis=0, tiled=True)  14.3 us
    dot_general x10, matrix products, dot_rows(): lax.dot_general(left, right, (((1,), (1,)), ((), ())), preferred_element_...  11.4 us
    pallas_call x1, Pallas kernels, attend_back(): pl.pallas_call(attend_back_kernel, out_shape=jax.ShapeDtypeStruct((keys,...  10.2 us
    pallas_call x1, Pallas kernels, attend(): pl.pallas_call(attend_kernel, out_shape=(jax.ShapeDtypeStruct((rows, q_co...  9.96 us
    ppermute x12, starting transfers between devices, shift(): lax.ppermute(value, 'tensor', [(i, (i + count) % size) for i in range(siz...  8.92 us
  transfers between devices with their start and end apart: 41, of which 27 were waited for; matrix products, arithmetic and copies ran while one was open for 28% of the time, Pallas kernels for 7%

profile of v5, /device:TPU:0, one launch (start us, length us, event | category | flops | bytes accessed | tf_op | source)
XLA Modules:
  0.0 273.0 jit_solution(2893451230344414458)
XLA Ops:
  2.5 4.0 %collective-permute-start = (bf16[96,960]{1,0:T(8,128)(2,1)}, bf16[96,960]{1,0:T(8,128)(2,1)}, u32[]{:S(2)}, u32[]{:S(2)}) collective-permute-start(bf16[96,960]{1,0:T(8,128)(2,1)} %get-tuple-element.215), channel_id=1, source_target_pairs={{0,2},{1,3},{2,0},{3,1},{4,6},{5,7},{6,4},{7,5},{8,10},{9,11},{10,... | collective-permute-start | bytes 552968 | tf_op jit(solution)/shard_map/ppermute | solution.py:81
  26.3 5.2 %collective-permute-done.1 = bf16[192,960]{1,0:T(8,128)(2,1)} collective-permute-done((bf16[192,960]{1,0:T(8,128)(2,1)S(1)}, bf16[192,960]{1,0:T(8,128)(2,1)}, u32[]{:S(2)}, u32[]{:S(2)}) %collective-permute-start.1) | collective-permute-done | bytes 368672 | tf_op jit(solution)/shard_map/ppermute | solution.py:81
  35.6 6.8 %collective-permute-done.5 = bf16[240,2624]{1,0:T(8,128)(2,1)} collective-permute-done((bf16[240,2624]{1,0:T(8,128)(2,1)}, bf16[240,2624]{1,0:T(8,128)(2,1)}, u32[]{:S(2)}, u32[]{:S(2)}) %collective-permute-start.5) | collective-permute-done | bytes 1259552 | tf_op jit(solution)/shard_map/ppermute | solution.py:81
  51.3 3.3 %pad_maximum_fusion.w_ref = bf16[960,2624]{1,0:T(8,128)(2,1)S(1)} fusion(bf16[240,2624]{1,0:T(8,128)(2,1)S(1)} %collective-permute-done.7, bf16[240,2624]{1,0:T(8,128)(2,1)} %collective-permute-done.6, bf16[240,2624]{1,0:T(8,128)(2,1)} %collective-permute-done.5, bf16[240,2624]{1,0:T(8,128)(2,1)} %concatenate.146), kind=kLoop, calls=%fused_computation | loop fusion | flops 20152320 | bytes 10076160 | tf_op jit(solution)/shard_map/concatenate | solution.py:354
  56.2 10.0 %attend.1 = (bf16[192,960]{1,0:T(8,128)(2,1)S(1)}, f32[576,8]{1,0:T(8,128)S(1)}, bf16[192,960]{1,0:T(8,128)(2,1)S(1)}, bf16[768,320]{1,0:T(8,128)(2,1)S(1)}, bf1...) custom-call(bf16[192,960]{1,0:T(8,128)(2,1)S(1)} %pad_maximum_fusion.10.x_ref, ...), custom_call_target="tpu_custom_call" | custom-call | flops 1509949440 | bytes 10000000 | tf_op jit(solution)/shard_map/attend/pallas_call | solution.py:229
  68.7 8.5 %collective-permute-done.10 = bf16[240,1920]{1,0:T(8,128)(2,1)S(1)} collective-permute-done((bf16[240,1920]{1,0:T(8,128)(2,1)}, bf16[240,1920]{1,0:T(8,128)(2,1)S(1)}, u32[]{:S(2)}, u32[]{:S(2)}) %collective-permute-start.10) | collective-permute-done | bytes 921632 | tf_op jit(solution)/shard_map/ppermute | solution.py:81
  85.4 7.7 %collective-permute-done.14 = bf16[192,960]{1,0:T(8,128)(2,1)S(1)} collective-permute-done((bf16[192,960]{1,0:T(8,128)(2,1)S(1)}, bf16[192,960]{1,0:T(8,128)(2,1)S(1)}, u32[]{:S(2)}, u32[]{:S(2)}) %collective-permute-start.14) | collective-permute-done | bytes 368672 | tf_op jit(solution)/shard_map/ppermute | solution.py:109
  95.1 6.4 %collective-permute-done.16 = bf16[192,960]{1,0:T(8,128)(2,1)S(1)} collective-permute-done((bf16[192,960]{1,0:T(8,128)(2,1)S(1)}, bf16[192,960]{1,0:T(8,128)(2,1)S(1)}, u32[]{:S(2)}, u32[]{:S(2)}) %collective-permute-start.16) | collective-permute-done | bytes 368672 | tf_op jit(solution)/shard_map/ppermute | solution.py:109
  102.5 7.4 %collective-permute-done.15 = bf16[192,960]{1,0:T(8,128)(2,1)S(1)} collective-permute-done((bf16[192,960]{1,0:T(8,128)(2,1)S(1)}, bf16[192,960]{1,0:T(8,128)(2,1)S(1)}, u32[]{:S(2)}, u32[]{:S(2)}) %collective-permute-start.15) | collective-permute-done | bytes 368672 | tf_op jit(solution)/shard_map/ppermute | solution.py:109
  111.3 4.8 %collective-permute-done.17 = bf16[192,960]{1,0:T(8,128)(2,1)S(1)} collective-permute-done((bf16[192,960]{1,0:T(8,128)(2,1)S(1)}, bf16[192,960]{1,0:T(8,128)(2,1)S(1)}, u32[]{:S(2)}, u32[]{:S(2)}) %collective-permute-start.17) | collective-permute-done | bytes 368672 | tf_op jit(solution)/shard_map/ppermute | solution.py:109
  120.6 3.6 %pad_maximum_fusion.2 = (bf16[480,1920]{1,0:T(8,128)(2,1)S(1)}, bf16[480,1920]{1,0:T(8,128)(2,1)S(1)}) fusion(bf16[960,640]{1,0:T(8,128)(2,1)S(1)} %convolution_convert_fusion.2, bf16[960,1280]{1,0:T(8,128)(2,1)S(1)} %convolution_convert_fusion), kind=kLoop, calls=%fused_computation.25 | loop fusion | flops 7372800 | bytes 7372800 | tf_op jit(solution)/shard_map/concatenate | solution.py:409
  124.4 3.3 %collective-permute-done.18 = bf16[192,960]{1,0:T(8,128)(2,1)S(1)} collective-permute-done((bf16[192,960]{1,0:T(8,128)(2,1)S(1)}, bf16[192,960]{1,0:T(8,128)(2,1)S(1)}, u32[]{:S(2)}, u32[]{:S(2)}) %collective-permute-start.18) | collective-permute-done | bytes 368672 | tf_op jit(solution)/shard_map/ppermute | solution.py:109
  132.2 10.2 %attend_back.1 = bf16[768,1664]{1,0:T(8,128)(2,1)S(1)} custom-call(bf16[192,960]{1,0:T(8,128)(2,1)S(1)} %get-tuple-element.83.q_ref, bf16[768,320]{1,0:T(8,128)(2,1)S(1)} %get-tuple-element.84.k_ref, bf16[768,320]{1,0:T(8,128)(2,1)S(1)} %get-tuple-element.85.v_ref, bf16[192,960]{1,0:T(8,128)(2,1)S(1)} %get-tuple-element.81.mix_ref, ...), custom_call_target="tpu_custom_call" | custom-call | flops 1415577600 | bytes 6000000 | tf_op jit(solution)/shard_map/attend_back/pallas_call | solution.py:287
  155.5 6.5 %collective-permute-done.24 = bf16[384,640]{1,0:T(8,128)(2,1)S(1)} collective-permute-done((bf16[384,640]{1,0:T(8,128)(2,1)S(1)}, bf16[384,640]{1,0:T(8,128)(2,1)S(1)}, u32[]{:S(2)}, u32[]{:S(2)}) %collective-permute-start.24) | collective-permute-done | bytes 491552 | tf_op jit(solution)/shard_map/ppermute | solution.py:81
  172.1 3.4 %all-to-all-start = ((bf16[4,32,960]{2,1,0:T(8,128)(2,1)}), bf16[4,32,960]{2,1,0:T(8,128)(2,1)S(1)}, u32[]{:S(2)}, u32[]{:S(2)}) async-start(bf16[4,32,960]{2,1,0:T(8,128)(2,1)} %bitcast.13), calls=%async_computation | async-start | bytes 524288 | tf_op jit(solution)/shard_map/all_to_all | solution.py:132
  180.9 3.8 %all-to-all-done = bf16[4,32,960]{2,1,0:T(8,128)(2,1)S(1)} async-done(((bf16[4,32,960]{2,1,0:T(8,128)(2,1)}), bf16[4,32,960]{2,1,0:T(8,128)(2,1)S(1)}, u32[]{:S(2)}, u32[]{:S(2)}) %all-to-all-start) | async-done | bytes 245792 | tf_op jit(solution)/shard_map/all_to_all | solution.py:132
  195.5 3.1 %collective-permute-done.31 = bf16[128,1664]{1,0:T(8,128)(2,1)S(1)} collective-permute-done((bf16[128,1664]{1,0:T(8,128)(2,1)S(1)}, bf16[128,1664]{1,0:T(8,128)(2,1)S(1)}, u32[]{:S(2)}, u32[]{:S(2)}) %collective-permute-start.31) | collective-permute-done | bytes 426016 | tf_op jit(solution)/shard_map/ppermute | solution.py:81
  202.3 4.8 %all-to-all-start.1 = ((bf16[4,32,1664]{2,1,0:T(8,128)(2,1)}), bf16[4,32,1664]{2,1,0:T(8,128)(2,1)}, u32[]{:S(2)}, u32[]{:S(2)}) async-start(bf16[4,32,1664]{2,1,0:T(8,128)(2,1)} %bitcast.14), calls=%async_computation.1 | async-start | bytes 851968 | tf_op jit(solution)/shard_map/all_to_all | solution.py:132
  207.0 5.4 %collective-permute-done.34 = bf16[240,960]{1,0:T(8,128)(2,1)} collective-permute-done((bf16[240,960]{1,0:T(8,128)(2,1)}, bf16[240,960]{1,0:T(8,128)(2,1)}, u32[]{:S(2)}, u32[]{:S(2)}) %collective-permute-start.34) | collective-permute-done | bytes 460832 | tf_op jit(solution)/shard_map/ppermute | solution.py:81
  221.7 4.2 %all-to-all-start.2 = ((bf16[4,32,2688]{2,1,0:T(8,128)(2,1)}), bf16[4,32,2688]{2,1,0:T(8,128)(2,1)}, u32[]{:S(2)}, u32[]{:S(2)}) async-start(bf16[4,32,2688]{2,1,0:T(8,128)(2,1)} %broadcast_in_dim.16), calls=%async_computation.2 | async-start | bytes 1376256 | tf_op jit(solution)/shard_map/all_to_all | solution.py:141
  232.2 5.7 %collective-permute-done.35 = bf16[240,960]{1,0:T(8,128)(2,1)S(1)} collective-permute-done((bf16[240,960]{1,0:T(8,128)(2,1)S(1)}, bf16[240,960]{1,0:T(8,128)(2,1)S(1)}, u32[]{:S(2)}, u32[]{:S(2)}) %collective-permute-start.35) | collective-permute-done | bytes 460832 | tf_op jit(solution)/shard_map/ppermute | solution.py:81
  238.2 14.3 %all-to-all-done.2 = bf16[4,32,2688]{2,1,0:T(8,128)(2,1)} async-done(((bf16[4,32,2688]{2,1,0:T(8,128)(2,1)}), bf16[4,32,2688]{2,1,0:T(8,128)(2,1)}, u32[]{:S(2)}, u32[]{:S(2)}) %all-to-all-start.2) | async-done | bytes 688160 | tf_op jit(solution)/shard_map/all_to_all | solution.py:141
  256.7 3.1 %collective-permute-done.36 = bf16[96,960]{1,0:T(8,128)(2,1)} collective-permute-done((bf16[96,960]{1,0:T(8,128)(2,1)}, bf16[96,960]{1,0:T(8,128)(2,1)}, u32[]{:S(2)}, u32[]{:S(2)}) %collective-permute-start.36) | collective-permute-done | bytes 184352 | tf_op jit(solution)/shard_map/ppermute | solution.py:81
  262.5 5.5 %collective-permute-done.37 = bf16[128,2688]{1,0:T(8,128)(2,1)S(1)} collective-permute-done((bf16[128,2688]{1,0:T(8,128)(2,1)}, bf16[128,2688]{1,0:T(8,128)(2,1)S(1)}, u32[]{:S(2)}, u32[]{:S(2)}) %collective-permute-start.37) | collective-permute-done | bytes 688160 | tf_op jit(solution)/shard_map/ppermute | solution.py:81
  (307 shorter events, 129.7 us)
Async XLA Ops:
  2.5 16.2 %collective-permute-start = (bf16[96,960]{1,0:T(8,128)(2,1)}, bf16[96,960]{1,0:T(8,128)(2,1)}, u32[]{:S(2)}, u32[]{:S(2)}) collective-permute-start(bf16[96,960]{1,0:T(8,128)(2,1)} %get-tuple-element.215), channel_id=1, source_target_pairs={{0,2},{1,3},{2,0},{3,1},{4,6},{5,7},{6,4},{7,5},{8,10},{9,11},{10,... | collective-permute-start | bytes 552968 | tf_op jit(solution)/shard_map/ppermute | solution.py:81
  12.3 30.1 %collective-permute-start.5 = (bf16[240,2624]{1,0:T(8,128)(2,1)}, bf16[240,2624]{1,0:T(8,128)(2,1)}, u32[]{:S(2)}, u32[]{:S(2)}) collective-permute-start(bf16[240,2624]{1,0:T(8,128)(2,1)} %concatenate.146), channel_id=1, source_target_pairs={{0,16},{8,24},{16,0},{24,8},{1,17},{9,25},{17,1},{25,9},{2,18},{10... | collective-permute-start | bytes 3778568 | tf_op jit(solution)/shard_map/ppermute | solution.py:81
  13.8 37.5 %collective-permute-start.6 = (bf16[240,2624]{1,0:T(8,128)(2,1)}, bf16[240,2624]{1,0:T(8,128)(2,1)}, u32[]{:S(2)}, u32[]{:S(2)}) collective-permute-start(bf16[240,2624]{1,0:T(8,128)(2,1)} %concatenate.146), channel_id=1, source_target_pairs={{0,8},{8,0},{16,24},{24,16},{1,9},{9,1},{17,25},{25,17},{2,10},{10... | collective-permute-start | bytes 3778568 | tf_op jit(solution)/shard_map/ppermute | solution.py:81
  15.9 33.3 %collective-permute-start.11 = (bf16[240,1920]{1,0:T(8,128)(2,1)}, bf16[240,1920]{1,0:T(8,128)(2,1)}, u32[]{:S(2)}, u32[]{:S(2)}) collective-permute-start(bf16[240,1920]{1,0:T(8,128)(2,1)} %pad_maximum_fusion.5), channel_id=1, source_target_pairs={{0,8},{8,0},{16,24},{24,16},{1,9},{9,1},{17,25},{25,17},{2,10},{10... | collective-permute-start | bytes 2764808 | tf_op jit(solution)/shard_map/ppermute | solution.py:81
  46.9 20.0 %collective-permute-start.9 = (bf16[2,96,960]{2,1,0:T(8,128)(2,1)S(1)}, bf16[2,96,960]{2,1,0:T(8,128)(2,1)S(1)}, u32[]{:S(2)}, u32[]{:S(2)}) collective-permute-start(bf16[2,96,960]{2,1,0:T(8,128)(2,1)S(1)} %copy-done.5), channel_id=1, source_target_pairs={{0,3},{1,0},{2,1},{3,2},{4,7},{5,4},{6,5},{7,6},{8,11},{9,8},{10,9... | collective-permute-start | bytes 1105928 | tf_op jit(solution)/shard_map/ppermute | solution.py:109
  48.3 18.5 %collective-permute-start.8 = (bf16[2,96,960]{2,1,0:T(8,128)(2,1)S(1)}, bf16[2,96,960]{2,1,0:T(8,128)(2,1)S(1)}, u32[]{:S(2)}, u32[]{:S(2)}) collective-permute-start(bf16[2,96,960]{2,1,0:T(8,128)(2,1)S(1)} %collective-permute-done.4), channel_id=1, source_target_pairs={{0,1},{1,2},{2,3},{3,0},{4,5},{5,6},{6,7},{7,4},{8,9},{9,10},{10,1... | collective-permute-start | bytes 1105928 | tf_op jit(solution)/shard_map/ppermute | solution.py:109
  54.6 22.6 %collective-permute-start.10 = (bf16[240,1920]{1,0:T(8,128)(2,1)}, bf16[240,1920]{1,0:T(8,128)(2,1)S(1)}, u32[]{:S(2)}, u32[]{:S(2)}) collective-permute-start(bf16[240,1920]{1,0:T(8,128)(2,1)} %pad_maximum_fusion.5), channel_id=1, source_target_pairs={{0,16},{8,24},{16,0},{24,8},{1,17},{9,25},{17,1},{25,9},{2,18},{10... | collective-permute-start | bytes 2764808 | tf_op jit(solution)/shard_map/ppermute | solution.py:81
  79.2 13.9 %collective-permute-start.14 = (bf16[192,960]{1,0:T(8,128)(2,1)S(1)}, bf16[192,960]{1,0:T(8,128)(2,1)S(1)}, u32[]{:S(2)}, u32[]{:S(2)}) collective-permute-start(bf16[192,960]{1,0:T(8,128)(2,1)S(1)} %collective-permute-done.13), channel_id=1, source_target_pairs={{0,1},{1,2},{2,3},{3,0},{4,5},{5,6},{6,7},{7,4},{8,9},{9,10},{10,1... | collective-permute-start | bytes 1105928 | tf_op jit(solution)/shard_map/ppermute | solution.py:109
  82.7 18.8 %collective-permute-start.16 = (bf16[192,960]{1,0:T(8,128)(2,1)S(1)}, bf16[192,960]{1,0:T(8,128)(2,1)S(1)}, u32[]{:S(2)}, u32[]{:S(2)}) collective-permute-start(bf16[192,960]{1,0:T(8,128)(2,1)S(1)} %convolution_convert_fusion.8), channel_id=1, source_target_pairs={{0,1},{1,2},{2,3},{3,0},{4,5},{5,6},{6,7},{7,4},{8,9},{9,10},{10,1... | collective-permute-start | bytes 1105928 | tf_op jit(solution)/shard_map/ppermute | solution.py:109
  93.1 16.9 %collective-permute-start.15 = (bf16[192,960]{1,0:T(8,128)(2,1)S(1)}, bf16[192,960]{1,0:T(8,128)(2,1)S(1)}, u32[]{:S(2)}, u32[]{:S(2)}) collective-permute-start(bf16[192,960]{1,0:T(8,128)(2,1)S(1)} %collective-permute-done.14), channel_id=1, source_target_pairs={{0,1},{1,2},{2,3},{3,0},{4,5},{5,6},{6,7},{7,4},{8,9},{9,10},{10,1... | collective-permute-start | bytes 1105928 | tf_op jit(solution)/shard_map/ppermute | solution.py:109
  102.4 13.6 %collective-permute-start.17 = (bf16[192,960]{1,0:T(8,128)(2,1)S(1)}, bf16[192,960]{1,0:T(8,128)(2,1)S(1)}, u32[]{:S(2)}, u32[]{:S(2)}) collective-permute-start(bf16[192,960]{1,0:T(8,128)(2,1)S(1)} %fusion.38), channel_id=1, source_target_pairs={{0,1},{1,2},{2,3},{3,0},{4,5},{5,6},{6,7},{7,4},{8,9},{9,10},{10,1... | collective-permute-start | bytes 1105928 | tf_op jit(solution)/shard_map/ppermute | solution.py:109
  124.3 20.6 %collective-permute-start.21 = (bf16[480,1920]{1,0:T(8,128)(2,1)S(1)}, bf16[480,1920]{1,0:T(8,128)(2,1)S(1)}, u32[]{:S(2)}, u32[]{:S(2)}) collective-permute-start(bf16[480,1920]{1,0:T(8,128)(2,1)S(1)} %get-tuple-element.150), channel_id=1, source_target_pairs={{0,8},{8,0},{16,24},{24,16},{1,9},{9,1},{17,25},{25,17},{2,10},{10... | collective-permute-start | bytes 5529608 | tf_op jit(solution)/shard_map/ppermute | solution.py:81
  148.4 13.7 %collective-permute-start.24 = (bf16[384,640]{1,0:T(8,128)(2,1)S(1)}, bf16[384,640]{1,0:T(8,128)(2,1)S(1)}, u32[]{:S(2)}, u32[]{:S(2)}) collective-permute-start(bf16[384,640]{1,0:T(8,128)(2,1)S(1)} %get-tuple-element.151), channel_id=1, source_target_pairs={{0,4},{4,0},{1,5},{5,1},{2,6},{6,2},{3,7},{7,3},{8,12},{12,8},{9,1... | collective-permute-start | bytes 1474568 | tf_op jit(solution)/shard_map/ppermute | solution.py:81
  150.0 14.1 %collective-permute-start.26 = (bf16[240,960]{1,0:T(8,128)(2,1)S(1)}, bf16[240,960]{1,0:T(8,128)(2,1)S(1)}, u32[]{:S(2)}, u32[]{:S(2)}) collective-permute-start(bf16[240,960]{1,0:T(8,128)(2,1)S(1)} %get-tuple-element.172), channel_id=1, source_target_pairs={{0,16},{8,24},{16,0},{24,8},{1,17},{9,25},{17,1},{25,9},{2,18},{10... | collective-permute-start | bytes 1382408 | tf_op jit(solution)/shard_map/ppermute | solution.py:81
  155.0 29.8 %collective-permute-start.23 = (bf16[240,1664]{1,0:T(8,128)(2,1)}, bf16[240,1664]{1,0:T(8,128)(2,1)}, u32[]{:S(2)}, u32[]{:S(2)}) collective-permute-start(bf16[240,1664]{1,0:T(8,128)(2,1)} %slice_add_fusion.1), channel_id=1, source_target_pairs={{0,16},{8,24},{16,0},{24,8},{1,17},{9,25},{17,1},{25,9},{2,18},{10... | collective-permute-start | bytes 2396168 | tf_op jit(solution)/shard_map/ppermute | solution.py:81
  163.0 16.1 %collective-permute-start.25 = (bf16[192,640]{1,0:T(8,128)(2,1)}, bf16[192,640]{1,0:T(8,128)(2,1)}, u32[]{:S(2)}, u32[]{:S(2)}) collective-permute-start(bf16[192,640]{1,0:T(8,128)(2,1)} %slice.457), channel_id=1, source_target_pairs={{0,1},{1,0},{2,3},{3,2},{4,5},{5,4},{6,7},{7,6},{8,9},{9,8},{10,11... | collective-permute-start | bytes 737288 | tf_op jit(solution)/shard_map/ppermute | solution.py:81
  165.9 20.8 %collective-permute-start.29 = (bf16[192,960]{1,0:T(8,128)(2,1)}, bf16[192,960]{1,0:T(8,128)(2,1)}, u32[]{:S(2)}, u32[]{:S(2)}) collective-permute-start(bf16[192,960]{1,0:T(8,128)(2,1)} %add.320), channel_id=1, source_target_pairs={{0,1},{1,2},{2,3},{3,0},{4,5},{5,6},{6,7},{7,4},{8,9},{9,10},{10,1... | collective-permute-start | bytes 1105928 | tf_op jit(solution)/shard_map/ppermute | solution.py:109
  191.5 15.5 %collective-permute-start.33 = (bf16[240,960]{1,0:T(8,128)(2,1)}, bf16[240,960]{1,0:T(8,128)(2,1)}, u32[]{:S(2)}, u32[]{:S(2)}) collective-permute-start(bf16[240,960]{1,0:T(8,128)(2,1)} %slice_add_fusion.3), channel_id=1, source_target_pairs={{0,16},{8,24},{16,0},{24,8},{1,17},{9,25},{17,1},{25,9},{2,18},{10... | collective-permute-start | bytes 1382408 | tf_op jit(solution)/shard_map/ppermute | solution.py:81
  199.5 13.0 %collective-permute-start.34 = (bf16[240,960]{1,0:T(8,128)(2,1)}, bf16[240,960]{1,0:T(8,128)(2,1)}, u32[]{:S(2)}, u32[]{:S(2)}) collective-permute-start(bf16[240,960]{1,0:T(8,128)(2,1)} %get-tuple-element.112), channel_id=1, source_target_pairs={{0,4},{4,0},{1,5},{5,1},{2,6},{6,2},{3,7},{7,3},{8,12},{12,8},{9,1... | collective-permute-start | bytes 1382408 | tf_op jit(solution)/shard_map/ppermute | solution.py:81
  202.3 17.3 %all-to-all-start.1 = ((bf16[4,32,1664]{2,1,0:T(8,128)(2,1)}), bf16[4,32,1664]{2,1,0:T(8,128)(2,1)}, u32[]{:S(2)}, u32[]{:S(2)}) async-start(bf16[4,32,1664]{2,1,0:T(8,128)(2,1)} %bitcast.14), calls=%async_computation.1 | async-start | bytes 851968 | tf_op jit(solution)/shard_map/all_to_all | solution.py:132
  221.7 30.8 %all-to-all-start.2 = ((bf16[4,32,2688]{2,1,0:T(8,128)(2,1)}), bf16[4,32,2688]{2,1,0:T(8,128)(2,1)}, u32[]{:S(2)}, u32[]{:S(2)}) async-start(bf16[4,32,2688]{2,1,0:T(8,128)(2,1)} %broadcast_in_dim.16), calls=%async_computation.2 | async-start | bytes 1376256 | tf_op jit(solution)/shard_map/all_to_all | solution.py:141
  228.6 28.1 %collective-permute-start.30 = (bf16[96,960]{1,0:T(8,128)(2,1)}, bf16[96,960]{1,0:T(8,128)(2,1)}, u32[]{:S(2)}, u32[]{:S(2)}) collective-permute-start(bf16[96,960]{1,0:T(8,128)(2,1)} %get-tuple-element.184), channel_id=1, source_target_pairs={{0,2},{1,3},{2,0},{3,1},{4,6},{5,7},{6,4},{7,5},{8,10},{9,11},{10,... | collective-permute-start | bytes 552968 | tf_op jit(solution)/shard_map/ppermute | solution.py:81
  232.2 27.7 %collective-permute-start.36 = (bf16[96,960]{1,0:T(8,128)(2,1)}, bf16[96,960]{1,0:T(8,128)(2,1)}, u32[]{:S(2)}, u32[]{:S(2)}) collective-permute-start(bf16[96,960]{1,0:T(8,128)(2,1)} %get-tuple-element.180), channel_id=1, source_target_pairs={{0,2},{1,3},{2,0},{3,1},{4,6},{5,7},{6,4},{7,5},{8,10},{9,11},{10,... | collective-permute-start | bytes 552968 | tf_op jit(solution)/shard_map/ppermute | solution.py:81
  252.5 15.5 %collective-permute-start.37 = (bf16[128,2688]{1,0:T(8,128)(2,1)}, bf16[128,2688]{1,0:T(8,128)(2,1)S(1)}, u32[]{:S(2)}, u32[]{:S(2)}) collective-permute-start(bf16[128,2688]{1,0:T(8,128)(2,1)} %bitcast.19), channel_id=1, source_target_pairs={{0,4},{4,0},{1,5},{5,1},{2,6},{6,2},{3,7},{7,3},{8,12},{12,8},{9,1... | collective-permute-start | bytes 2064392 | tf_op jit(solution)/shard_map/ppermute | solution.py:81
  (61 other events, 637.1 us)
